TPU v7x, 128 devices: a whole 4x4x4 slice. The times are simulated.
128 devices in a mesh: gx: 8 (over y, core), gy: 16 (over x, z).
Axes of the slice: x: 4, y: 4, z: 4, core: 2. Of those that a mesh axis runs over, the one named last changes fastest.
Arguments:
- dist_old: bfloat16 [12288, 8, 4096], P(('gx', 'gy')), may hold values from 0.0625 to 16, as said below
- source_owner: int32 [12288], P(('gx', 'gy')), may hold values from 0 to 127, as said below
- levels: int32 [12288], P(('gx', 'gy')), may hold values from 0 to 2
- active: int32 [12288, 8], P(('gx', 'gy')), may hold values 0 or 1
Outputs:
- dist_new: bfloat16 [12288, 8, 4096], P(('gx', 'gy'))
Inputs may be any that keep to these rules, and one draw needn't show every extreme that they name: `dist_old`: Positive. New slot k of device d receives old slot k of device source_owner[d * 96 + k]; for each k these sources over d are a permutation of the devices. A device takes at most 1 block from any one device, and exactly 1 from some.
All inputs are finite; a program needn't handle non-finite values. No bound on the sum of `active` on one device may be relied on, other than what follows from the above.
Results may differ from a plain program's by a relative error of at most 0.0045.
Values may be sent and summed in bfloat16 or wider, within the bound.
No kernel may reach another device: no remote copies, remote signals or barrier semaphores. Data moves between devices by JAX's collectives and lax.ppermute only.
A program may use at most 128 MiB of HBM per device.

v0:
```python
import math

import jax
import jax.numpy as jnp
from jax import lax
from jax.sharding import PartitionSpec as P

VS = 16
BX = 4
BY = 4
BZ = 6


RELAX_INCREMENT = 0.3
COURANT = 0.028


def with_halo(shard, sides, width):
    for axis, dim in sides:
        devices, length = (lax.axis_size(axis), shard.shape[dim])
        up = [(i, (i + 1) % devices) for i in range(devices - 1)]
        down = [(j, i) for i, j in up]
        last = lax.slice_in_dim(shard, length - width, length, axis=dim)
        first = lax.slice_in_dim(shard, 0, width, axis=dim)
        before = lax.ppermute(last, axis, up)
        after = lax.ppermute(first, axis, down)
        shard = jnp.concatenate([before, shard, after], axis=dim)
    return shard


def velocity_table(points):
    total = points * points * points
    index = jnp.arange(total, dtype=jnp.int32)
    stacked = jnp.stack([index // (points * points), index // points % points, index % points])
    return 2 * stacked + 1 - points


def collide(cell_rows, points):
    total = points * points * points
    weights = velocity_table(points).astype(jnp.float32)
    along_x, along_y, along_z = (weights[0], weights[1], weights[2])
    filler = jnp.zeros_like(along_x)
    columns = [
        jnp.ones_like(along_x),
        along_x,
        along_y,
        along_z,
        along_x * along_x,
        along_y * along_y,
        along_z * along_z,
        along_x * along_y,
        along_x * along_z,
        along_y * along_z,
    ]
    moments_basis = jnp.stack(columns + [filler] * 6, axis=1)
    raw_sums = (
        jnp.dot(cell_rows, moments_basis.astype(jnp.bfloat16), preferred_element_type=jnp.float32)
        / total
    )
    spacing = 3.0 / points
    zeroth_moment_field = raw_sums[:, 0]
    drift_x = spacing * raw_sums[:, 1] / zeroth_moment_field
    drift_y = spacing * raw_sums[:, 2] / zeroth_moment_field
    drift_z = spacing * raw_sums[:, 3] / zeroth_moment_field
    square = spacing * spacing
    spread_second_moment_first = square * raw_sums[:, 4] / zeroth_moment_field - drift_x * drift_x
    spread_second_moment_second = square * raw_sums[:, 5] / zeroth_moment_field - drift_y * drift_y
    spread_second_moment_third = square * raw_sums[:, 6] / zeroth_moment_field - drift_z * drift_z
    spread_xy = square * raw_sums[:, 7] / zeroth_moment_field - drift_x * drift_y
    spread_xz = square * raw_sums[:, 8] / zeroth_moment_field - drift_x * drift_z
    spread_yz = square * raw_sums[:, 9] / zeroth_moment_field - drift_y * drift_z
    thermal_energy_per_particle = (
        spread_second_moment_first + spread_second_moment_second + spread_second_moment_third
    ) / 3.0
    anisotropic_factor_first_first = (
        1.5 * thermal_energy_per_particle - 0.5 * spread_second_moment_first
    )
    anisotropic_factor_second_second = (
        1.5 * thermal_energy_per_particle - 0.5 * spread_second_moment_second
    )
    anisotropic_factor_third_third = (
        1.5 * thermal_energy_per_particle - 0.5 * spread_second_moment_third
    )
    lam_xy = -0.5 * spread_xy
    lam_xz = -0.5 * spread_xz
    lam_yz = -0.5 * spread_yz
    adj_xx = anisotropic_factor_second_second * anisotropic_factor_third_third - lam_yz * lam_yz
    adj_yy = anisotropic_factor_first_first * anisotropic_factor_third_third - lam_xz * lam_xz
    adj_zz = anisotropic_factor_first_first * anisotropic_factor_second_second - lam_xy * lam_xy
    adj_xy = lam_xz * lam_yz - lam_xy * anisotropic_factor_third_third
    adj_xz = lam_xy * lam_yz - lam_xz * anisotropic_factor_second_second
    adj_yz = lam_xy * lam_xz - anisotropic_factor_first_first * lam_yz
    determinant = anisotropic_factor_first_first * adj_xx + lam_xy * adj_xy + lam_xz * adj_xz
    inv_xx = adj_xx / determinant
    inv_yy = adj_yy / determinant
    inv_zz = adj_zz / determinant
    inv_xy = adj_xy / determinant
    inv_xz = adj_xz / determinant
    inv_yz = adj_yz / determinant
    pull_x = inv_xx * drift_x + inv_xy * drift_y + inv_xz * drift_z
    pull_y = inv_xy * drift_x + inv_yy * drift_y + inv_yz * drift_z
    pull_z = inv_xz * drift_x + inv_yz * drift_y + inv_zz * drift_z
    quadratic = drift_x * pull_x + drift_y * pull_y + drift_z * pull_z
    log_prefactor = (
        jnp.log(zeroth_moment_field)
        + 3.0 * math.log(6.0)
        - 1.5 * math.log(2.0 * math.pi)
        - 0.5 * jnp.log(determinant)
    )
    zero_rows = jnp.zeros_like(zeroth_moment_field)
    coefficients = jnp.stack(
        [
            log_prefactor - 0.5 * quadratic,
            spacing * pull_x,
            spacing * pull_y,
            spacing * pull_z,
            -0.5 * square * inv_xx,
            -0.5 * square * inv_yy,
            -0.5 * square * inv_zz,
            -square * inv_xy,
            -square * inv_xz,
            -square * inv_yz,
        ]
        + [zero_rows] * 6,
        axis=1,
    )
    exponent = jnp.dot(coefficients, moments_basis.T, precision=lax.Precision.HIGHEST)
    gauss = jnp.exp(exponent)
    inverse_relax_period = 1.0 - jnp.exp(
        -RELAX_INCREMENT * zeroth_moment_field * jnp.sqrt(thermal_energy_per_particle)
    )
    moved = cell_rows.astype(jnp.float32)
    return (moved + inverse_relax_period[:, None] * (gauss - moved)).astype(jnp.bfloat16)


def to_grid(blocks, blocks_x, blocks_y, blocks_z):
    trailing = blocks.shape[2:]
    shaped = blocks.reshape((blocks_x, blocks_y, blocks_z, 2, 2, 2) + trailing)
    permute_order = (0, 3, 1, 4, 2, 5) + tuple(range(6, 6 + len(trailing)))
    return shaped.transpose(permute_order).reshape(
        (2 * blocks_x, 2 * blocks_y, 2 * blocks_z) + trailing
    )


def from_grid(grid, blocks_x, blocks_y, blocks_z):
    trailing = grid.shape[3:]
    shaped = grid.reshape((blocks_x, 2, blocks_y, 2, blocks_z, 2) + trailing)
    permute_order = (0, 2, 4, 1, 3, 5) + tuple(range(6, 6 + len(trailing)))
    return shaped.transpose(permute_order).reshape((blocks_x * blocks_y * blocks_z, 8) + trailing)


def advance(padded, courant, active_grid, points):
    speeds = velocity_table(points).astype(jnp.float32) * (3.0 / points)
    center = padded[1:-1, 1:-1, 1:-1].astype(jnp.float32)
    behind = [padded[:-2, 1:-1, 1:-1], padded[1:-1, :-2, 1:-1], padded[1:-1, 1:-1, :-2]]
    beyond = [padded[2:, 1:-1, 1:-1], padded[1:-1, 2:, 1:-1], padded[1:-1, 1:-1, 2:]]
    net_flux = jnp.zeros_like(center)
    for direction in range(3):
        forward = jnp.maximum(speeds[direction], 0.0)
        backward = jnp.minimum(speeds[direction], 0.0)
        net_flux = (
            net_flux
            + forward * (center - behind[direction].astype(jnp.float32))
            + backward * (beyond[direction].astype(jnp.float32) - center)
        )
    result = active_grid[..., None] * (center - courant[..., None] * net_flux)
    return result.astype(jnp.bfloat16)


def per_device(dist_old, source_owner, levels, active):
    blocks = dist_old.shape[0]
    total = dist_old.shape[2]
    devices = lax.axis_size("gx") * lax.axis_size("gy")
    capacity = (blocks + devices - 1) // devices
    slots = jnp.arange(blocks, dtype=jnp.int32)
    earlier_same = (source_owner[:, None] == source_owner[None, :]) & (
        slots[None, :] < slots[:, None]
    )
    rank = jnp.sum(earlier_same.astype(jnp.int32), axis=1)
    position = source_owner * capacity + rank
    request = jnp.full((devices * capacity,), blocks, jnp.int32).at[position].set(slots)
    asked = lax.all_to_all(
        request.reshape(devices, capacity), ("gx", "gy"), split_axis=0, concat_axis=0, tiled=True
    )
    picked = jnp.minimum(asked, blocks - 1)
    items = lax.all_to_all(dist_old[picked], ("gx", "gy"), split_axis=0, concat_axis=0, tiled=True)
    arrived = collide(items.reshape(-1, total), VS).reshape(items.shape)
    landed = arrived.reshape(devices * capacity, 8, total)[position]
    kept = jnp.where(active[:, :, None] > 0, landed, jnp.zeros_like(landed))
    grid = to_grid(kept, BX, BY, BZ)
    widened = with_halo(grid, (("gx", 0), ("gy", 1)), 1)
    padded = jnp.pad(widened, ((0, 0), (0, 0), (1, 1), (0, 0)))
    courant = COURANT * jnp.exp2(levels.astype(jnp.float32))
    courant_grid = to_grid(jnp.broadcast_to(courant[:, None], (blocks, 8)), BX, BY, BZ)
    active_grid = to_grid(active.astype(jnp.float32), BX, BY, BZ)
    return from_grid(advance(padded, courant_grid, active_grid, VS), BX, BY, BZ)


def solution(mesh):
    return jax.shard_map(
        per_device,
        mesh=mesh,
        in_specs=(
            P(("gx", "gy"), None, None),
            P(("gx", "gy")),
            P(("gx", "gy")),
            P(("gx", "gy"), None),
        ),
        out_specs=P(("gx", "gy"), None, None),
        check_vma=False,
    )
```

profile of v0, /device:TPU:7, one launch (start us, length us, event | category | flops | bytes accessed | tf_op | source)
XLA Modules:
  0.0 347.8 jit_solution(5574980807192200877)
XLA Ops:
  2.6 18.5 %all_to_all.14 = s32[128,1,1]{2,1,0:T(1,128)S(1)} all-to-all(s32[128,1,1]{2,1,0:T(1,128)S(1)} %copy.97), channel_id=1, replica_groups=mesh['gx'=8,'gy'=16] {'gx','gy'}, dimensions={0} | all-to-all | bytes 1024 | tf_op jit(solution)/shard_map/all_to_all | solution.py:182
  23.4 9.4 %gather_fusion = bf16[128,8,4096]{2,1,0:T(8,128)(2,1)} fusion(bf16[96,8,4096]{2,1,0:T(8,128)(2,1)} %param.4, s32[1024]{0:T(1024)S(1)} %pad_clamp_fusion.1), kind=kCustom, calls=%fused_computation | custom fusion | bytes 16777728 | tf_op jit(solution)/shard_map/gather | solution.py:186
  32.8 7.5 %all-to-all-start.1 = ((bf16[128,1,8,4096]{3,2,1,0:T(8,128)(2,1)}), bf16[128,1,8,4096]{3,2,1,0:T(8,128)(2,1)}, u32[]{:S(2)}, u32[]{:S(2)}) async-start(bf16[128,1,8,4096]{3,2,1,0:T(8,128)(2,1)} %bitcast.68), calls=%async_computation.1 | async-start | bytes 16777216 | tf_op jit(solution)/shard_map/all_to_all | solution.py:186
  42.0 103.4 %all-to-all-done.1 = bf16[128,1,8,4096]{3,2,1,0:T(8,128)(2,1)} async-done(((bf16[128,1,8,4096]{3,2,1,0:T(8,128)(2,1)}), bf16[128,1,8,4096]{3,2,1,0:T(8,128)(2,1)}, u32[]{:S(2)}, u32[]{:S(2)}) %all-to-all-start.1) | async-done | bytes 8388640 | tf_op jit(solution)/shard_map/all_to_all | solution.py:186
  145.4 5.6 %fusion.24 = f32[1024,16]{0,1:T(8,128)S(1)} fusion(bf16[128,1,8,4096]{3,2,1,0:T(8,128)(2,1)} %all-to-all-done.1, f32[4096,16]{0,1:T(8,128)S(1)} %stack.17), kind=kOutput, calls=%fused_computation.44 | convolution fusion | flops 134299648 | bytes 8716288 | tf_op jit(solution)/shard_map/dot_general | solution.py:57
  151.5 20.7 %fusion.22 = bf16[128,8,4096]{2,1,0:T(8,128)(2,1)} fusion(f32[1024,16]{0,1:T(8,128)S(1)} %stack.20, f32[4096,16]{0,1:T(8,128)S(1)} %stack.17, f32[1024]{0:T(1024)S(1)} %bitcast.77, bf16[128,1,8,4096]{3,2,1,0:T(8,128)(2,1)} %all-to-all-done.1), kind=kOutput, calls=%fused_computation.38 | convolution fusion | flops 826277888 | bytes 17108992 | tf_op jit(solution)/shard_map/dot_general | solution.py:127
  172.1 9.4 %gather_fusion.1 = bf16[96,8,4096]{2,1,0:T(8,128)(2,1)} fusion(bf16[128,8,4096]{2,1,0:T(8,128)(2,1)} %fusion.22, s32[1024]{0:T(1024)S(1)} %pad_clamp_fusion), kind=kCustom, calls=%fused_computation.1 | custom fusion | bytes 12583296 | tf_op jit(solution)/shard_map/gather | solution.py:188
  181.6 10.8 %gather.10 = bf16[4,4,6,2,2,2,4096]{6,5,4,3,2,1,0:T(2,128)(2,1)} reshape(bf16[96,8,4096]{2,1,0:T(8,128)(2,1)} %gather_fusion.1) | data formatting | bytes 12582912 | tf_op jit(solution)/shard_map/gather | solution.py:188
  192.4 7.8 %fusion.23 = bf16[4,2,4,2,6,2,4096]{6,5,3,1,4,2,0:T(2,128)(2,1)S(1)} fusion(bf16[4,4,6,2,2,2,4096]{6,5,4,3,2,1,0:T(2,128)(2,1)} %gather.10, pred[4,4,6,2,2,2]{5,4,3,2,1,0:T(4,128)(4,1)S(1)} %copy.96), kind=kLoop, calls=%fused_computation.39 | loop fusion | flops 3145728 | bytes 12583680 | tf_op jit(solution)/shard_map/transpose | solution.py:140
  200.2 6.3 %copy.98 = bf16[4,2,4,2,6,2,4096]{6,3,2,5,4,1,0:T(2,128)(2,1)} copy(bf16[4,2,4,2,6,2,4096]{6,5,3,1,4,2,0:T(2,128)(2,1)S(1)} %fusion.23) | data formatting | bytes 12582912 | tf_op jit(solution)/shard_map/transpose | solution.py:140
  206.5 10.2 %reshape.275 = bf16[8,8,12,4096]{3,1,2,0:T(8,128)(2,1)} reshape(bf16[4,2,4,2,6,2,4096]{6,3,2,5,4,1,0:T(2,128)(2,1)} %copy.98) | data formatting | bytes 12582912 | tf_op jit(solution)/shard_map/reshape | solution.py:140
  222.8 6.2 %collective-permute-done = bf16[1,8,12,4096]{3,1,2,0:T(8,128)(2,1)S(1)} collective-permute-done((bf16[1,8,12,4096]{3,1,2,0:T(8,128)(2,1)S(1)}, bf16[1,8,12,4096]{3,1,2,0:T(8,128)(2,1)S(1)}, u32[]{:S(2)}, u32[]{:S(2)}) %collective-permute-start) | collective-permute-done | bytes 786464 | tf_op jit(solution)/shard_map/ppermute | solution.py:25
  229.1 3.2 constant_dynamic-update-slice_fusion.1
  233.5 3.3 copy-done
  236.8 4.3 %fusion.74 = (bf16[10,1,12,4096]{3,1,2,0:T(2,128)(2,1)S(1)}, bf16[10,1,12,4096]{3,1,2,0:T(2,128)(2,1)S(1)}) fusion(bf16[10,8,12,4096]{3,1,2,0:T(8,128)(2,1)S(1)} %constant_dynamic-update-slice_fusion), kind=kLoop, calls=%fused_computation.148 | loop fusion | bytes 3932160 | tf_op jit(solution)/shard_map/slice | solution.py:23
  246.2 3.4 collective-permute-start.2
  251.1 18.7 %collective-permute-done.3 = bf16[10,1,12,4096]{3,2,1,0:T(8,128)(2,1)} collective-permute-done((bf16[10,1,12,4096]{3,2,1,0:T(8,128)(2,1)}, bf16[10,1,12,4096]{3,2,1,0:T(8,128)(2,1)}, u32[]{:S(2)}, u32[]{:S(2)}) %collective-permute-start.3) | collective-permute-done | bytes 983072 | tf_op jit(solution)/shard_map/ppermute | solution.py:26
  269.8 3.4 copy.104
  273.6 3.6 %copy.102 = bf16[10,1,12,4096]{3,1,2,0:T(2,128)(2,1)S(1)} copy(bf16[10,1,12,4096]{3,2,1,0:T(8,128)(2,1)} %collective-permute-done.2) | data formatting | bytes 1966080 | tf_op jit(solution)/shard_map/ppermute | solution.py:25
  277.2 11.8 %fusion.5 = bf16[10,10,14,4096]{3,1,2,0:T(8,128)(2,1)} fusion(bf16[10,1,12,4096]{3,1,2,0:T(2,128)(2,1)S(1)} %copy.104, bf16[10,8,12,4096]{3,1,2,0:T(8,128)(2,1)} %copy-done, bf16[10,1,12,4096]{3,1,2,0:T(2,128)(2,1)S(1)} %copy.102), kind=kLoop, calls=%fused_computation.19 | loop fusion | flops 68812800 | bytes 21299200 | tf_op jit(solution)/shard_map/concatenate | solution.py:27
  289.1 25.0 %multiply_convert_fusion = bf16[8,8,12,4096]{3,1,2,0:T(8,128)(2,1)} fusion(bf16[8,8,12,4096]{3,1,2,0:T(8,128)(2,1)S(1)} %bitcast.65, bf16[10,10,14,4096]{3,1,2,0:T(8,128)(2,1)} %fusion.5, bf16[10,1,12,4096]{3,1,2,0:T(2,128)(2,1)S(1)} %copy.104, bf16[10,8,12,4096]{3,1,2,0:T(8,128)(2,1)S(1)} %bitcast.67, bf16[10,1,12,4096]{3,1,2,0:T(2,128)(2,1)S(1)} %copy.102, ...), kind=kLoop, calls=%fused_computation.34 | loop fusion | flops 125829120 | bytes 36673536 | tf_op jit(solution)/shard_map/convert_element_type | solution.py:167
  314.1 10.8 %reshape.276 = bf16[4,2,4,2,6,2,4096]{6,3,2,5,4,1,0:T(2,128)(2,1)} reshape(bf16[8,8,12,4096]{3,1,2,0:T(8,128)(2,1)} %multiply_convert_fusion) | data formatting | bytes 12582912 | tf_op jit(solution)/shard_map/reshape | solution.py:147
  325.0 12.7 %copy.107 = bf16[4,4,6,2,2,2,4096]{6,5,4,3,2,1,0:T(2,128)(2,1)} copy(bf16[4,4,6,2,2,2,4096]{6,4,1,5,2,3,0:T(2,128)(2,1)} %bitcast.69) | data formatting | bytes 12582912 | tf_op jit(solution)/shard_map/transpose | solution.py:149
  337.7 10.1 %reshape.277 = bf16[96,8,4096]{2,1,0:T(8,128)(2,1)} reshape(bf16[4,4,6,2,2,2,4096]{6,5,4,3,2,1,0:T(2,128)(2,1)} %copy.107) | data formatting | bytes 12582912 | tf_op jit(solution)/shard_map/reshape | solution.py:149
  (68 shorter events, 21.3 us)
Async XLA Ops:
  32.8 7.5 %copy-start.2 = (s32[96,8]{0,1:T(8,128)S(1)}, s32[96,8]{0,1:T(8,128)}, u32[]{:S(2)}) copy-start(s32[96,8]{0,1:T(8,128)} %param.7) | copy-start | bytes 9220
  32.8 112.6 %all-to-all-start.1 = ((bf16[128,1,8,4096]{3,2,1,0:T(8,128)(2,1)}), bf16[128,1,8,4096]{3,2,1,0:T(8,128)(2,1)}, u32[]{:S(2)}, u32[]{:S(2)}) async-start(bf16[128,1,8,4096]{3,2,1,0:T(8,128)(2,1)} %bitcast.68), calls=%async_computation.1 | async-start | bytes 16777216 | tf_op jit(solution)/shard_map/all_to_all | solution.py:186
  218.2 10.8 %collective-permute-start = (bf16[1,8,12,4096]{3,1,2,0:T(8,128)(2,1)S(1)}, bf16[1,8,12,4096]{3,1,2,0:T(8,128)(2,1)S(1)}, u32[]{:S(2)}, u32[]{:S(2)}) collective-permute-start(bf16[1,8,12,4096]{3,1,2,0:T(8,128)(2,1)S(1)} %get-tuple-element.41), channel_id=1, source_target_pairs={{0,16},{16,32},{32,48},{48,64},{64,80},{80,96},{96,112},{1,17},{17... | collective-permute-start | bytes 2359304 | tf_op jit(solution)/shard_map/ppermute | solution.py:25
  220.1 13.3 %collective-permute-start.1 = (bf16[1,8,12,4096]{3,1,2,0:T(8,128)(2,1)S(1)}, bf16[1,8,12,4096]{3,1,2,0:T(8,128)(2,1)S(1)}, u32[]{:S(2)}, u32[]{:S(2)}) collective-permute-start(bf16[1,8,12,4096]{3,1,2,0:T(8,128)(2,1)S(1)} %get-tuple-element.40), channel_id=1, source_target_pairs={{16,0},{32,16},{48,32},{64,48},{80,64},{96,80},{112,96},{17,1},{33... | collective-permute-start | bytes 2359304 | tf_op jit(solution)/shard_map/ppermute | solution.py:26
  229.1 20.6 %copy-start.3 = (s32[96]{0:T(128)S(1)}, s32[96]{0:T(128)}, u32[]{:S(2)}) copy-start(s32[96]{0:T(128)} %param.6) | copy-start | bytes 1156
  233.5 10.9 %copy-start.1 = (bf16[1,8,12,4096]{3,1,2,0:T(8,128)(2,1)}, bf16[1,8,12,4096]{3,1,2,0:T(8,128)(2,1)S(1)}, u32[]{:S(2)}) copy-start(bf16[1,8,12,4096]{3,1,2,0:T(8,128)(2,1)S(1)} %collective-permute-done.1) | copy-start | bytes 2359300
  233.5 3.3 copy-start
  244.3 25.5 %collective-permute-start.3 = (bf16[10,1,12,4096]{3,2,1,0:T(8,128)(2,1)}, bf16[10,1,12,4096]{3,2,1,0:T(8,128)(2,1)}, u32[]{:S(2)}, u32[]{:S(2)}) collective-permute-start(bf16[10,1,12,4096]{3,2,1,0:T(8,128)(2,1)} %copy.103), channel_id=1, source_target_pairs={{1,0},{2,1},{3,2},{4,3},{5,4},{6,5},{7,6},{8,7},{9,8},{10,9},{11,1... | collective-permute-start | bytes 2949128 | tf_op jit(solution)/shard_map/ppermute | solution.py:26
  246.2 27.4 %collective-permute-start.2 = (bf16[10,1,12,4096]{3,2,1,0:T(8,128)(2,1)S(1)}, bf16[10,1,12,4096]{3,2,1,0:T(8,128)(2,1)}, u32[]{:S(2)}, u32[]{:S(2)}) collective-permute-start(bf16[10,1,12,4096]{3,2,1,0:T(8,128)(2,1)S(1)} %copy.101), channel_id=1, source_target_pairs={{0,1},{1,2},{2,3},{3,4},{4,5},{5,6},{6,7},{7,8},{8,9},{9,10},{10,1... | collective-permute-start | bytes 2949128 | tf_op jit(solution)/shard_map/ppermute | solution.py:25
  273.6 15.4 %slice-start = ((s8[6291456]{0:T(1024)(128)(4,1)}), s8[4194304]{0:T(1024)(128)(4,1)S(1)}, s32[]{:S(2)}) async-start(s8[6291456]{0:T(1024)(128)(4,1)} %bitcast.64), calls=%async_computation.2 | async-start | bytes 8388608
  273.6 15.4 %slice-start.2 = ((s8[7864320]{0:T(1024)(128)(4,1)}), s8[4194304]{0:T(1024)(128)(4,1)S(1)}, s32[]{:S(2)}) async-start(s8[7864320]{0:T(1024)(128)(4,1)} %bitcast.66), calls=%async_computation.4 | async-start | bytes 8388608
  277.2 11.9 %slice-start.1 = ((s8[6291456]{0:T(1024)(128)(4,1)}), s8[2097152]{0:T(1024)(128)(4,1)S(1)}, s32[]{:S(2)}) async-start(s8[6291456]{0:T(1024)(128)(4,1)} %bitcast.64), calls=%async_computation.3 | async-start | bytes 4194304
  277.2 11.9 %slice-start.3 = ((s8[7864320]{0:T(1024)(128)(4,1)}), s8[3670016]{0:T(1024)(128)(4,1)S(1)}, s32[]{:S(2)}) async-start(s8[7864320]{0:T(1024)(128)(4,1)} %bitcast.66), calls=%async_computation.5 | async-start | bytes 7340032
where the time goes:
time: 354 us; the launch traced here: 348 us
  waiting for transfers between devices  130 us (37%)
  local copies, waits for them, and re-layouts  106 us (30%)
  other arithmetic  49.2 us (14%)
  matrix products  26.3 us (7%)
  blocking collectives  18.5 us (5%)
  starting transfers between devices  17.3 us (5%)
    all_to_all x1, waiting for transfers between devices, per_device(): lax.all_to_all(dist_old[picked], ('gx', 'gy'), split_axis=0, concat_axis=...  103 us
    convert_element_type x1, other arithmetic, advance(): return result.astype(jnp.bfloat16)  25 us
    dot_general x1, matrix products, collide(): jnp.dot(coefficients, moments_basis.T, precision=lax.Precision.HIGHEST)  20.7 us
    gather x2, local copies, waits for them, and re-layouts, per_device(): landed = arrived.reshape(devices * capacity, 8, total)[position]  20.3 us
    ppermute x2, waiting for transfers between devices, with_halo(): after = lax.ppermute(first, axis, down)  19.9 us
    all_to_all x1, blocking collectives, per_device(): lax.all_to_all(request.reshape(devices, capacity), ('gx', 'gy'), split_ax...  18.5 us
    transpose x1, local copies, waits for them, and re-layouts, from_grid(): shaped.transpose(permute_order)  12.7 us
    concatenate x1, other arithmetic, with_halo(): shard = jnp.concatenate([before, shard, after], axis=dim)  11.8 us
  transfers between devices with their start and end apart: 5, of which 5 were waited for; matrix products, arithmetic and copies ran while one was open for 3% of the time, Pallas kernels for 0%

commit v1 on v0

v1 whole, which is shorter than its diff:
```python
import math

import jax
import jax.numpy as jnp
import ml_dtypes
import numpy as np
from jax import lax
from jax.experimental import pallas as pl
from jax.experimental.pallas import tpu as pltpu
from jax.sharding import PartitionSpec as P

VS = 16
BX, BY, BZ = 4, 4, 6
BLOCKS = BX * BY * BZ
TOTAL = VS * VS * VS
CELLS = 8
SLAB = BY * BZ
RELAX_INCREMENT = 0.3
COURANT = 0.028
SPACING = 3.0 / VS
LOG2E = 1.0 / math.log(2.0)

CHUNKS = 2
WIDTH = TOTAL // CHUNKS
TILES = WIDTH // 128
PIECE = 16
GROUP = 8
STEP = 512
ZERO_BLOCK = BLOCKS
X_HALO = BLOCKS + 1
Y_HALO = X_HALO + SLAB
HELD = Y_HALO + BX * BZ


def basis_rows():
    index = np.arange(TOTAL)
    x, y, z = (2 * i + 1 - VS for i in (index // (VS * VS), index // VS % VS, index % VS))
    rows = np.zeros((16, TOTAL), np.float32)
    rows[:10] = [np.ones_like(x), x, y, z, x * x, y * y, z * z, x * y, x * z, y * z]
    whole = np.zeros((128, TOTAL), np.float32)
    for copy in range(3):
        whole[16 * copy : 16 * copy + 16] = rows
    return whole.astype(ml_dtypes.bfloat16)


def coefficients_of(sums):
    raw = [sums[i : i + 1] * (1.0 / TOTAL) for i in range(10)]
    density = raw[0]
    drift = [SPACING * raw[1 + a] / density for a in range(3)]
    square = SPACING * SPACING
    spread = [square * raw[4 + a] / density - drift[a] * drift[a] for a in range(3)]
    spread_xy = square * raw[7] / density - drift[0] * drift[1]
    spread_xz = square * raw[8] / density - drift[0] * drift[2]
    spread_yz = square * raw[9] / density - drift[1] * drift[2]
    temperature = (spread[0] + spread[1] + spread[2]) / 3.0
    xx, yy, zz = (1.5 * temperature - 0.5 * s for s in spread)
    xy, xz, yz = (-0.5 * s for s in (spread_xy, spread_xz, spread_yz))
    adj_xx, adj_yy, adj_zz = yy * zz - yz * yz, xx * zz - xz * xz, xx * yy - xy * xy
    adj_xy, adj_xz, adj_yz = xz * yz - xy * zz, xy * yz - xz * yy, xy * xz - xx * yz
    determinant = xx * adj_xx + xy * adj_xy + xz * adj_xz
    inv = [a / determinant for a in (adj_xx, adj_yy, adj_zz, adj_xy, adj_xz, adj_yz)]
    pull = [
        inv[0] * drift[0] + inv[3] * drift[1] + inv[4] * drift[2],
        inv[3] * drift[0] + inv[1] * drift[1] + inv[5] * drift[2],
        inv[4] * drift[0] + inv[5] * drift[1] + inv[2] * drift[2],
    ]
    quadratic = drift[0] * pull[0] + drift[1] * pull[1] + drift[2] * pull[2]
    log_prefactor = (
        jnp.log(density)
        + (3.0 * math.log(6.0) - 1.5 * math.log(2.0 * math.pi))
        - 0.5 * jnp.log(determinant)
    )
    rows = [log_prefactor - 0.5 * quadratic]
    rows += [SPACING * p for p in pull]
    rows += [-0.5 * square * i for i in inv[:3]]
    rows += [-square * i for i in inv[3:]]
    fraction = 1.0 - jnp.exp(-RELAX_INCREMENT * density * jnp.sqrt(temperature))
    return [LOG2E * r for r in rows], fraction


def collide_kernel(asked, dist, basis, *rest):
    sends = rest[:CHUNKS]
    held, relaxed, sums, factors, target, in_sems, out_sems = rest[CHUNKS:]
    pieces = BLOCKS // PIECE

    def arrival(piece):
        rows = pl.ds(piece * PIECE, PIECE)
        return pltpu.make_async_copy(dist.at[rows], held.at[rows], in_sems.at[piece])

    for piece in range(pieces):
        arrival(piece).start()

    @pl.loop(0, asked.shape[0])
    def _(device):
        target[asked[device]] = device

    for piece in range(pieces):
        arrival(piece).wait()
        cells = held[pl.ds(piece * PIECE, PIECE)].astype(jnp.float32)
        cells = cells.reshape(PIECE * CELLS, TOTAL).astype(jnp.bfloat16)
        sums[:, pl.ds(piece * PIECE * CELLS, PIECE * CELLS)] = lax.dot_general(
            basis[0:16, :], cells, (((1,), (1,)), ((), ())), preferred_element_type=jnp.float32
        )

    rows, fraction = coefficients_of(sums[...])
    exact = [[], [], []]
    for row in rows:
        for part in range(3):
            near = row.astype(jnp.bfloat16).astype(jnp.float32)
            exact[part].append(near)
            row = row - near
    zero = jnp.zeros((6, BLOCKS * CELLS), jnp.float32)
    stacked = jnp.concatenate(
        exact[0]
        + [zero]
        + exact[1]
        + [zero]
        + exact[2]
        + [zero, fraction, jnp.zeros((79, BLOCKS * CELLS), jnp.float32)],
        axis=0,
    )
    factors[...] = stacked.T

    @pl.loop(0, BLOCKS // GROUP)
    def _(group):
        first = group * GROUP
        own = factors[pl.ds(pl.multiple_of(first * CELLS, GROUP * CELLS), GROUP * CELLS), :]
        left = own.astype(jnp.bfloat16)
        fraction = own[:, 48:49]
        for step in range(TOTAL // STEP):
            lanes = pl.ds(step * STEP, STEP)
            gauss = jnp.exp2(
                jnp.dot(left, basis[:, lanes], preferred_element_type=jnp.float32)
            )
            moved = held[pl.ds(first, GROUP), :, lanes].astype(jnp.float32)
            moved = moved.reshape(GROUP * CELLS, STEP)
            mixed = moved + fraction * (gauss - moved)
            relaxed[pl.ds(first, GROUP), :, lanes] = mixed.reshape(GROUP, CELLS, STEP).astype(
                jnp.bfloat16
            )
        for block in range(GROUP):
            for chunk in range(CHUNKS):
                pltpu.make_async_copy(
                    relaxed.at[first + block, :, pl.ds(chunk * WIDTH, WIDTH)],
                    sends[chunk].at[target[first + block]],
                    out_sems.at[chunk],
                ).start()

    for chunk in range(CHUNKS):
        pltpu.make_async_copy(
            relaxed.at[:, :, pl.ds(chunk * WIDTH, WIDTH)],
            sends[chunk].at[pl.ds(0, BLOCKS)],
            out_sems.at[chunk],
        ).wait()


def collide(asked, dist, devices):
    return pl.pallas_call(
        collide_kernel,
        out_shape=[jax.ShapeDtypeStruct((devices, CELLS, WIDTH), jnp.bfloat16)] * CHUNKS,
        in_specs=[
            pl.BlockSpec(memory_space=pltpu.SMEM),
            pl.BlockSpec(memory_space=pl.ANY),
            pl.BlockSpec(memory_space=pltpu.VMEM),
        ],
        out_specs=[pl.BlockSpec(memory_space=pl.ANY)] * CHUNKS,
        scratch_shapes=[
            pltpu.VMEM((BLOCKS, CELLS, TOTAL), jnp.bfloat16),
            pltpu.VMEM((BLOCKS, CELLS, TOTAL), jnp.bfloat16),
            pltpu.VMEM((16, BLOCKS * CELLS), jnp.float32),
            pltpu.VMEM((BLOCKS * CELLS, 128), jnp.float32),
            pltpu.SMEM((devices,), jnp.int32),
            pltpu.SemaphoreType.DMA((BLOCKS // PIECE,)),
            pltpu.SemaphoreType.DMA((CHUNKS,)),
        ],
        compiler_params=pltpu.CompilerParams(vmem_limit_bytes=40 << 20),
        cost_estimate=pl.CostEstimate(
            flops=2 * BLOCKS * CELLS * TOTAL * 144,
            bytes_accessed=4 * BLOCKS * CELLS * TOTAL,
            transcendentals=BLOCKS * CELLS * TOTAL,
        ),
        name="collide",
    )(asked, dist, basis_rows())


def row_masks():
    row = lax.broadcasted_iota(jnp.int32, (CELLS, 128), 0)
    return row < 4, (row & 2) == 0, (row & 1) == 0


def swap(x, distance, low):
    if distance == 4:
        return pltpu.roll(x, 4, 0)
    return jnp.where(low, pltpu.roll(x, CELLS - distance, 0), pltpu.roll(x, distance, 0))


def faces_kernel(chunk, owner, received, mask, face_x, face_down, face_up, held, sems):
    low_x, low_y, _ = row_masks()
    x_first = 0 if chunk == 0 else (BX - 1) * SLAB

    def fetch(block, place, sem):
        pltpu.make_async_copy(received.at[owner[block]], held.at[place], sems.at[sem]).start()

    def block_y(pair, edge):
        return pair // 3 * SLAB + edge * BZ + pair % 3 * 2

    @pl.loop(0, SLAB)
    def _(i):
        fetch(x_first + i, i, 0)

    @pl.loop(0, 12)
    def _(pair):
        for side in range(2):
            fetch(block_y(pair, 0) + side, SLAB + 2 * pair + side, 1)
            fetch(block_y(pair, BY - 1) + side, 2 * SLAB + 2 * pair + side, 2)

    for sem in range(3):
        rows = pl.ds(sem * SLAB, SLAB)
        pltpu.make_async_copy(received.at[pl.ds(0, SLAB)], held.at[rows], sems.at[sem]).wait()

    @pl.loop(0, 12)
    def _(pair):
        def load(place, block, lanes):
            return held[place, :, lanes].astype(jnp.float32) * mask[block]

        for tile in range(TILES):
            lanes = pl.ds(tile * 128, 128)
            a, b = (load(2 * pair + s, x_first + 2 * pair + s, lanes) for s in range(2))
            keep = low_x if chunk == 0 else ~low_x
            face_x[pair, :, lanes] = jnp.where(keep, a, swap(b, 4, low_x)).astype(jnp.bfloat16)
            up = tile % 2
            edge = up * (BY - 1)
            place = SLAB + up * SLAB + 2 * pair
            a, b = (load(place + s, block_y(pair, edge) + s, lanes) for s in range(2))
            keep = ~low_y if up else low_y
            face = face_up if up else face_down
            face[pair, :, pl.ds(tile // 2 * 128, 128)] = jnp.where(
                keep, a, swap(b, 2, low_y)
            ).astype(jnp.bfloat16)


def faces(chunk, owner, received, mask):
    shapes = [(12, CELLS, WIDTH), (12, CELLS, WIDTH // 2), (12, CELLS, WIDTH // 2)]
    return pl.pallas_call(
        lambda *refs: faces_kernel(chunk, *refs),
        out_shape=[jax.ShapeDtypeStruct(s, jnp.bfloat16) for s in shapes],
        in_specs=[
            pl.BlockSpec(memory_space=pltpu.SMEM),
            pl.BlockSpec(memory_space=pl.ANY),
            pl.BlockSpec(memory_space=pltpu.VMEM),
        ],
        out_specs=[pl.BlockSpec(memory_space=pltpu.VMEM)] * 3,
        scratch_shapes=[
            pltpu.VMEM((3 * SLAB, CELLS, WIDTH), jnp.bfloat16),
            pltpu.SemaphoreType.DMA((3,)),
        ],
        compiler_params=pltpu.CompilerParams(vmem_limit_bytes=24 << 20),
        cost_estimate=pl.CostEstimate(
            flops=8 * SLAB * CELLS * WIDTH,
            bytes_accessed=8 * SLAB * CELLS * WIDTH,
            transcendentals=0,
        ),
        name=f"faces{chunk}",
    )(owner, received, mask)


def advance_kernel(chunk, owner, received, mask, rate, halo_x, halo_down, halo_up, *rest):
    out, held, kept, made, in_sems, out_sems = rest[-6:]
    low_x, low_y, low_z = row_masks()
    lane = lax.broadcasted_iota(jnp.int32, (CELLS, 128), 1)
    speed_z = SPACING * jnp.abs(2 * (lane % VS) + 1 - VS).astype(jnp.float32)
    speed_y = [
        SPACING * jnp.abs(2 * (lane // VS + 8 * odd) + 1 - VS).astype(jnp.float32) for odd in range(2)
    ]
    rising_z = lane % VS >= VS // 2
    from_below = rising_z & ~low_z
    from_above = ~rising_z & low_z

    def slab_copy(slab):
        rows = pl.ds(slab * SLAB, SLAB)
        return pltpu.make_async_copy(received.at[pl.ds(0, SLAB)], held.at[rows], in_sems.at[slab])

    for slab in range(BX):

        @pl.loop(slab * SLAB, slab * SLAB + SLAB)
        def _(block):
            pltpu.make_async_copy(
                received.at[owner[block]], held.at[block], in_sems.at[slab]
            ).start()

    kept[ZERO_BLOCK] = jnp.zeros((CELLS, WIDTH), jnp.float32)

    @pl.loop(0, 12)
    def _(pair):
        for tile in range(TILES):
            lanes = pl.ds(tile * 128, 128)
            face = halo_x[pair, :, lanes].astype(jnp.float32)
            kept[X_HALO + 2 * pair, :, lanes] = face
            kept[X_HALO + 2 * pair + 1, :, lanes] = swap(face, 4, low_x)
            halo = halo_down if tile % 2 else halo_up
            face = halo[pair, :, pl.ds(tile // 2 * 128, 128)].astype(jnp.float32)
            kept[Y_HALO + 2 * pair, :, lanes] = face
            kept[Y_HALO + 2 * pair + 1, :, lanes] = swap(face, 2, low_y)

    for slab in range(BX):
        slab_copy(slab).wait()

        @pl.loop(slab * SLAB, slab * SLAB + SLAB)
        def _(block):
            own_mask = mask[block]
            for tile in range(TILES):
                lanes = pl.ds(tile * 128, 128)
                kept[block, :, lanes] = held[block, :, lanes].astype(jnp.float32) * own_mask

    def result_copy(bx):
        rows = pl.ds(bx * SLAB, SLAB)
        return pltpu.make_async_copy(
            made.at[rows], out.at[rows, :, pl.ds(chunk * WIDTH, WIDTH)], out_sems.at[bx]
        )

    for bx in range(BX):

        @pl.loop(0, SLAB)
        def _(within):
            by, bz = within // BZ, within % BZ
            block = bx * SLAB + within
            if chunk == 0:
                next_x = X_HALO + within if bx == BX - 1 else block + SLAB
            else:
                next_x = X_HALO + within if bx == 0 else block - SLAB
            side = Y_HALO + bx * BZ + bz
            above_y = jnp.where(by == BY - 1, side, block + BZ)
            below_y = jnp.where(by == 0, side, block - BZ)
            above_z = jnp.where(bz == BZ - 1, ZERO_BLOCK, block + 1)
            below_z = jnp.where(bz == 0, ZERO_BLOCK, block - 1)
            own_rate = rate[block]
            for tile in range(TILES):
                lanes = pl.ds(tile * 128, 128)
                odd = tile % 2
                own = kept[block, :, lanes]
                other = kept[next_x, :, lanes]
                from_x = swap(
                    jnp.where(low_x, other, own) if chunk == 0 else jnp.where(low_x, own, other),
                    4,
                    low_x,
                )
                other = kept[below_y if odd else above_y, :, lanes]
                from_y = swap(
                    jnp.where(low_y, own, other) if odd else jnp.where(low_y, other, own), 2, low_y
                )
                from_z = swap(
                    jnp.where(
                        from_below,
                        kept[below_z, :, lanes],
                        jnp.where(from_above, kept[above_z, :, lanes], own),
                    ),
                    1,
                    low_z,
                )
                speed_x = SPACING * abs(2 * (chunk * (VS // CHUNKS) + tile // 2) + 1 - VS)
                flux = (
                    speed_x * (own - from_x)
                    + speed_y[odd] * (own - from_y)
                    + speed_z * (own - from_z)
                )
                made[block, :, lanes] = (own - own_rate * flux).astype(jnp.bfloat16)

        result_copy(bx).start()
    for bx in range(BX):
        result_copy(bx).wait()


def advance(chunk, owner, received, mask, rate, halos, earlier):
    anywhere = pl.BlockSpec(memory_space=pl.ANY)
    vmem = pl.BlockSpec(memory_space=pltpu.VMEM)
    extra = [] if earlier is None else [earlier]
    return pl.pallas_call(
        lambda *refs: advance_kernel(chunk, *refs),
        out_shape=jax.ShapeDtypeStruct((BLOCKS, CELLS, TOTAL), jnp.bfloat16),
        in_specs=[pl.BlockSpec(memory_space=pltpu.SMEM), anywhere]
        + [vmem] * 5
        + [anywhere] * len(extra),
        out_specs=anywhere,
        scratch_shapes=[
            pltpu.VMEM((BLOCKS, CELLS, WIDTH), jnp.bfloat16),
            pltpu.VMEM((HELD, CELLS, WIDTH), jnp.float32),
            pltpu.VMEM((BLOCKS, CELLS, WIDTH), jnp.bfloat16),
            pltpu.SemaphoreType.DMA((BX,)),
            pltpu.SemaphoreType.DMA((BX,)),
        ],
        input_output_aliases={} if earlier is None else {7: 0},
        compiler_params=pltpu.CompilerParams(vmem_limit_bytes=40 << 20),
        cost_estimate=pl.CostEstimate(
            flops=24 * BLOCKS * CELLS * WIDTH,
            bytes_accessed=5 * BLOCKS * CELLS * WIDTH,
            transcendentals=0,
        ),
        name=f"advance{chunk}",
    )(owner, received, mask, rate, *halos, *extra)


def after(received, source_owner, levels, active):
    n_gx, n_gy = lax.axis_size("gx"), lax.axis_size("gy")
    mask = jnp.broadcast_to(
        active.astype(jnp.float32)[:, :, None], (BLOCKS, CELLS, 128)
    )
    courant = COURANT * jnp.exp2(levels.astype(jnp.float32))
    rate = mask * courant[:, None, None]

    def up(n):
        return [(i, i + 1) for i in range(n - 1)]

    def down(n):
        return [(i + 1, i) for i in range(n - 1)]

    out = None
    for chunk in range(CHUNKS):
        face_x, face_down, face_up = faces(chunk, source_owner, received[chunk], mask)
        halos = (
            lax.ppermute(face_x, "gx", down(n_gx) if chunk == 0 else up(n_gx)),
            lax.ppermute(face_up, "gy", up(n_gy)),
            lax.ppermute(face_down, "gy", down(n_gy)),
        )
        out = advance(chunk, source_owner, received[chunk], mask, rate, halos, out)
    return out


def per_device(dist_old, source_owner, levels, active):
    axes = ("gx", "gy")
    n_gx, n_gy = lax.axis_size("gx"), lax.axis_size("gy")
    devices = n_gx * n_gy
    slots = lax.broadcasted_iota(jnp.int32, (devices, BLOCKS), 1)
    owners = lax.broadcasted_iota(jnp.int32, (devices, BLOCKS), 0)
    request = BLOCKS + jnp.sum(
        jnp.where(source_owner[None, :] == owners, slots - BLOCKS, 0), axis=1
    )
    asked = lax.all_to_all(
        request.reshape(devices, 1), axes, split_axis=0, concat_axis=0, tiled=True
    ).reshape(devices)
    sends = collide(asked, dist_old, devices)

    received = [
        lax.all_to_all(s, axes, split_axis=0, concat_axis=0, tiled=True) for s in sends
    ]
    return after(received, source_owner, levels, active)


def solution(mesh):
    return jax.shard_map(
        per_device,
        mesh=mesh,
        in_specs=(
            P(("gx", "gy"), None, None),
            P(("gx", "gy")),
            P(("gx", "gy")),
            P(("gx", "gy"), None),
        ),
        out_specs=P(("gx", "gy"), None, None),
        check_vma=False,
    )
```

time: 354 us -> 198 us (0.56)
  local copies, waits for them, and re-layouts: 106 us -> 3.79 us
  waiting for transfers between devices: 130 us -> 38.3 us
  blocking collectives: 18.5 us -> 75.8 us
  Pallas kernels: 0 us -> 49.1 us
  other arithmetic: 49.2 us -> 3.39 us
  matrix products: 26.3 us -> 0 us
  starting transfers between devices: 17.3 us -> 24.3 us
    all_to_all x1, waiting for transfers between devices: 103 us -> 38.3 us  [per_device(): lax.all_to_all(s, axes, split_axis=0, concat_axis=0, tiled=True)]
    all_to_all x1 -> x2, blocking collectives: 18.5 us -> 75.8 us  [the longest x1 57.3 us: per_device(): lax.all_to_all(s, axes, split_axis=0, concat_axis=0, tiled=True)]
    pallas_call x0 -> x5, Pallas kernels: none -> 49.1 us  [the longest x2 22.6 us: advance(): pl.pallas_call(lambda *refs: advance_kernel(chunk, *refs), out_shape=jax....]
    reshape x5 -> x0, local copies, waits for them, and re-layouts: 31.9 us -> none  [the longest x1 10.8 us: from_grid(): shaped = grid.reshape((blocks_x, 2, blocks_y, 2, blocks_z, 2) + trailing)]
    gather x3 -> x0, local copies, waits for them, and re-layouts: 29.6 us -> none  [the longest x2 20.3 us: per_device(): landed = arrived.reshape(devices * capacity, 8, total)[position]]
    ppermute x4 -> x6, waiting for transfers between devices: 26.5 us -> 0.02 us  [the longest x2 0.01 us: after(): lax.ppermute(face_up, 'gy', up(n_gy))]
    dot_general x2 -> x0, matrix products: 26.3 us -> none  [the longest x1 20.7 us: collide(): jnp.dot(coefficients, moments_basis.T, precision=lax.Precision.HIGHEST)]
    convert_element_type x3 -> x1, other arithmetic: 25.1 us -> 0.01 us  [after(): active.astype(jnp.float32)[:, :, None]]
  transfers between devices with their start and end apart: 5 -> 7, of which waited for: 5 -> 1; matrix products, arithmetic and copies ran while one was open for 3% -> 0% of each run, Pallas kernels for 0% -> 11%
where the time goes in v1:
time: 198 us; the launch traced here: 195 us
  blocking collectives  75.8 us (38%)
  Pallas kernels  49.1 us (25%)
  waiting for transfers between devices  38.3 us (19%)
  starting transfers between devices  24.3 us (12%)
  local copies, waits for them, and re-layouts  3.79 us (2%)
  other arithmetic  3.39 us (2%)
    all_to_all x1, blocking collectives, per_device(): lax.all_to_all(s, axes, split_axis=0, concat_axis=0, tiled=True)  57.3 us
    all_to_all x1, waiting for transfers between devices, per_device(): lax.all_to_all(s, axes, split_axis=0, concat_axis=0, tiled=True)  38.3 us
    pallas_call x2, Pallas kernels, advance(): pl.pallas_call(lambda *refs: advance_kernel(chunk, *refs), out_shape=jax....  22.6 us
    pallas_call x1, Pallas kernels, collide(): pl.pallas_call(collide_kernel, out_shape=[jax.ShapeDtypeStruct((devices,...  19 us
    all_to_all x1, blocking collectives, per_device(): lax.all_to_all(request.reshape(devices, 1), axes, split_axis=0, concat_ax...  18.5 us
    pallas_call x2, Pallas kernels, faces(): pl.pallas_call(lambda *refs: faces_kernel(chunk, *refs), out_shape=[jax.S...  7.51 us
    all_to_all x1, starting transfers between devices, per_device(): lax.all_to_all(s, axes, split_axis=0, concat_axis=0, tiled=True)  7.16 us
    ppermute x2, starting transfers between devices, after(): lax.ppermute(face_up, 'gy', up(n_gy))  6.72 us
  transfers between devices with their start and end apart: 7, of which 1 were waited for; matrix products, arithmetic and copies ran while one was open for 0% of the time, Pallas kernels for 11%

profile of v1, /device:TPU:7, one launch (start us, length us, event | category | flops | bytes accessed | tf_op | source)
XLA Modules:
  0.0 195.0 jit_solution(1144180748146439888)
XLA Ops:
  0.0 0.8 select_reduce_fusion
  0.8 0.1 copy.12
  0.9 18.5 %all_to_all.16 = s32[128,1,1]{2,1,0:T(1,128)S(1)} all-to-all(s32[128,1,1]{2,1,0:T(1,128)S(1)} %copy.12), channel_id=1, replica_groups=mesh['gx'=8,'gy'=16] {'gx','gy'}, dimensions={0} | all-to-all | bytes 1024 | tf_op jit(solution)/shard_map/all_to_all | solution.py:437
  19.4 2.3 %reduce.asked = s32[128]{0:T(128)S(1)} reduce(s32[128,1,1]{2,1,0:T(1,128)S(1)} %all_to_all.16, s32[]{:T(128)} %constant.3.clone.1), dimensions={1,2}, to_apply=%all_to_all.10.reduce_sub_computation | reduce | bytes 1028 | tf_op jit(solution)/shard_map/all_to_all | solution.py:437
  21.7 1.2 copy-done.3
  23.0 19.0 %collide.1 = (bf16[128,8,2048]{2,1,0:T(8,128)(2,1)S(1)}, bf16[128,8,2048]{2,1,0:T(8,128)(2,1)S(1)}) custom-call(s32[128]{0:T(128)S(1)} %reduce.asked, bf16[96,8,4096]{2,1,0:T(8,128)(2,1)} %dist.1, bf16[128,4096]{1,0:T(8,128)(2,1)S(1)} %copy-done.3), custom_call_target="tpu_custom_call" | custom-call | flops 905969664 | bytes 12582912 | tf_op jit(solution)/shard_map/collide/pallas_call | solution.py:158
  42.0 0.0 copy-start.2
  42.0 57.3 %all_to_all.17.refs_1_ = bf16[128,8,2048]{2,1,0:T(8,128)(2,1)} all-to-all(bf16[128,8,2048]{2,1,0:T(8,128)(2,1)S(1)} %get-tuple-element.17), channel_id=1, replica_groups=mesh['gx'=8,'gy'=16] {'gx','gy'}, dimensions={0} | all-to-all | bytes 8388608 | tf_op jit(solution)/shard_map/all_to_all | solution.py:443
  99.3 7.2 %all-to-all-start.1 = ((bf16[128,8,2048]{2,1,0:T(8,128)(2,1)}), bf16[128,8,2048]{2,1,0:T(8,128)(2,1)}, u32[]{:S(2)}, u32[]{:S(2)}) async-start(bf16[128,8,2048]{2,1,0:T(8,128)(2,1)} %copy-done.2), calls=%async_computation.1 | async-start | bytes 8388608 | tf_op jit(solution)/shard_map/all_to_all | solution.py:443
  106.5 0.1 copy.13
  106.6 0.2 broadcast_in_dim.7.refs_2_
  106.8 2.2 %copy-done = bf16[128,8,2048]{2,1,0:T(8,128)(2,1)S(1)} copy-done((bf16[128,8,2048]{2,1,0:T(8,128)(2,1)S(1)}, bf16[128,8,2048]{2,1,0:T(8,128)(2,1)}, u32[]{:S(2)}) %copy-start) | copy-done | bytes 4194328
  109.0 4.7 %faces0.1 = (bf16[12,8,2048]{2,1,0:T(8,128)(2,1)S(1)}, bf16[12,8,1024]{2,1,0:T(8,128)(2,1)S(1)}, bf16[12,8,1024]{2,1,0:T(8,128)(2,1)S(1)}) custom-call(s32[96]{0:T(128)S(1)} %copy-done.4, bf16[128,8,2048]{2,1,0:T(8,128)(2,1)S(1)} %copy-done, f32[96,8,128]{2,1,0:T(8,128)S(1)} %broadcast_in_dim.7.refs_2_), custom_call_target="tpu_custom_call" | custom-call | flops 3145728 | bytes 3145728 | tf_op jit(solution)/shard_map/faces0/pallas_call | solution.py:244
  113.7 3.4 %collective-permute-start.4 = (bf16[12,8,1024]{2,1,0:T(8,128)(2,1)S(1)}, bf16[12,8,1024]{2,1,0:T(8,128)(2,1)S(1)}, u32[]{:S(2)}, u32[]{:S(2)}) collective-permute-start(bf16[12,8,1024]{2,1,0:T(8,128)(2,1)S(1)} %get-tuple-element.19), channel_id=1, source_target_pairs={{0,1},{1,2},{2,3},{3,4},{4,5},{5,6},{6,7},{7,8},{8,9},{9,10},{10,1... | collective-permute-start | bytes 589832 | tf_op jit(solution)/shard_map/ppermute | solution.py:421
  117.0 2.5 %collective-permute-start.3 = (bf16[12,8,2048]{2,1,0:T(8,128)(2,1)S(1)}, bf16[12,8,2048]{2,1,0:T(8,128)(2,1)S(1)}, u32[]{:S(2)}, u32[]{:S(2)}) collective-permute-start(bf16[12,8,2048]{2,1,0:T(8,128)(2,1)S(1)} %get-tuple-element.18), channel_id=1, source_target_pairs={{16,0},{32,16},{48,32},{64,48},{80,64},{96,80},{112,96},{17,1},{33... | collective-permute-start | bytes 1179656 | tf_op jit(solution)/shard_map/ppermute | solution.py:420
  119.6 38.3 %all-to-all-done.1.refs_1_ = bf16[128,8,2048]{2,1,0:T(8,128)(2,1)} async-done(((bf16[128,8,2048]{2,1,0:T(8,128)(2,1)}), bf16[128,8,2048]{2,1,0:T(8,128)(2,1)}, u32[]{:S(2)}, u32[]{:S(2)}) %all-to-all-start.1) | async-done | bytes 4194336 | tf_op jit(solution)/shard_map/all_to_all | solution.py:443
  157.8 2.8 %faces1.1 = (bf16[12,8,2048]{2,1,0:T(8,128)(2,1)S(1)}, bf16[12,8,1024]{2,1,0:T(8,128)(2,1)S(1)}, bf16[12,8,1024]{2,1,0:T(8,128)(2,1)S(1)}) custom-call(s32[96]{0:T(128)S(1)} %copy-done.4, bf16[128,8,2048]{2,1,0:T(8,128)(2,1)} %all-to-all-done.1.refs_1_, f32[96,8,128]{2,1,0:T(8,128)S(1)} %broadcast_in_dim.7.refs_2_), custom_call_target="tpu_custom_call" | custom-call | flops 3145728 | bytes 3145728 | tf_op jit(solution)/shard_map/faces1/pallas_call | solution.py:244
  160.7 1.9 collective-permute-start
  162.7 1.9 collective-permute-start.5
  164.6 3.4 %collective-permute-start.1 = (bf16[12,8,1024]{2,1,0:T(8,128)(2,1)S(1)}, bf16[12,8,1024]{2,1,0:T(8,128)(2,1)S(1)}, u32[]{:S(2)}, u32[]{:S(2)}) collective-permute-start(bf16[12,8,1024]{2,1,0:T(8,128)(2,1)S(1)} %get-tuple-element.15), channel_id=1, source_target_pairs={{0,1},{1,2},{2,3},{3,4},{4,5},{5,6},{6,7},{7,8},{8,9},{9,10},{10,1... | collective-permute-start | bytes 589832 | tf_op jit(solution)/shard_map/ppermute | solution.py:421
  168.0 4.0 %collective-permute-start.2 = (bf16[12,8,1024]{2,1,0:T(8,128)(2,1)S(1)}, bf16[12,8,1024]{2,1,0:T(8,128)(2,1)S(1)}, u32[]{:S(2)}, u32[]{:S(2)}) collective-permute-start(bf16[12,8,1024]{2,1,0:T(8,128)(2,1)S(1)} %get-tuple-element.16), channel_id=1, source_target_pairs={{1,0},{2,1},{3,2},{4,3},{5,4},{6,5},{7,6},{8,7},{9,8},{10,9},{11,1... | collective-permute-start | bytes 589832 | tf_op jit(solution)/shard_map/ppermute | solution.py:422
  172.0 0.3 broadcast_multiply_fusion.refs_3_
  172.3 13.3 %advance0.1.refs_7_ = bf16[96,8,4096]{2,1,0:T(8,128)(2,1)} custom-call(s32[96]{0:T(128)S(1)} %copy-done.4, bf16[128,8,2048]{2,1,0:T(8,128)(2,1)S(1)} %copy-done.1, f32[96,8,128]{2,1,0:T(8,128)S(1)} %broadcast_in_dim.7.refs_2_, f32[96,8,128]{2,1,0:T(8,128)S(1)} %broadcast_multiply_fusion.refs_3_, bf16[12,8,2048]{2,1,0:T(8,128)(2,1)S(1)} %collective-permute-done.3.refs_4_, ...), custom_call_target="tpu_custom_call" | custom-call | flops 37748736 | bytes 7864320 | tf_op jit(solution)/shard_map/advance0/pallas_call | solution.py:377
  185.6 9.4 %advance1.1 = bf16[96,8,4096]{2,1,0:T(8,128)(2,1)} custom-call(s32[96]{0:T(128)S(1)} %copy-done.4, bf16[128,8,2048]{2,1,0:T(8,128)(2,1)} %all-to-all-done.1.refs_1_, f32[96,8,128]{2,1,0:T(8,128)S(1)} %broadcast_in_dim.7.refs_2_, f32[96,8,128]{2,1,0:T(8,128)S(1)} %broadcast_multiply_fusion.refs_3_, ...), custom_call_target="tpu_custom_call", output_to_operand_aliasing={{}: (7, {})} | custom-call | flops 37748736 | bytes 7864320 | tf_op jit(solution)/shard_map/advance1/pallas_call | solution.py:377
  (21 shorter events, 0.1 us)
Async XLA Ops:
  21.7 1.2 copy-start.3
  42.0 57.3 %copy-start.2 = (bf16[128,8,2048]{2,1,0:T(8,128)(2,1)}, bf16[128,8,2048]{2,1,0:T(8,128)(2,1)S(1)}, u32[]{:S(2)}) copy-start(bf16[128,8,2048]{2,1,0:T(8,128)(2,1)S(1)} %get-tuple-element.13) | copy-start | bytes 12582916
  99.3 7.2 %copy-start.5 = (s32[96,8]{0,1:T(8,128)S(1)}, s32[96,8]{0,1:T(8,128)}, u32[]{:S(2)}) copy-start(s32[96,8]{0,1:T(8,128)} %param.8) | copy-start | bytes 9220
  99.3 7.4 %copy-start.4 = (s32[96]{0:T(128)S(1)}, s32[96]{0:T(128)}, u32[]{:S(2)}) copy-start(s32[96]{0:T(128)} %refs_0_.7) | copy-start | bytes 1156
  99.3 58.5 %all-to-all-start.1 = ((bf16[128,8,2048]{2,1,0:T(8,128)(2,1)}), bf16[128,8,2048]{2,1,0:T(8,128)(2,1)}, u32[]{:S(2)}, u32[]{:S(2)}) async-start(bf16[128,8,2048]{2,1,0:T(8,128)(2,1)} %copy-done.2), calls=%async_computation.1 | async-start | bytes 8388608 | tf_op jit(solution)/shard_map/all_to_all | solution.py:443
  106.8 2.2 %copy-start = (bf16[128,8,2048]{2,1,0:T(8,128)(2,1)S(1)}, bf16[128,8,2048]{2,1,0:T(8,128)(2,1)}, u32[]{:S(2)}) copy-start(bf16[128,8,2048]{2,1,0:T(8,128)(2,1)} %all_to_all.17.refs_1_) | copy-start | bytes 12582916
  109.0 53.7 %copy-start.6 = (s32[96]{0:T(128)S(1)}, s32[96]{0:T(128)}, u32[]{:S(2)}) copy-start(s32[96]{0:T(128)} %param.7) | copy-start | bytes 1156
  113.7 54.3 %collective-permute-start.4 = (bf16[12,8,1024]{2,1,0:T(8,128)(2,1)S(1)}, bf16[12,8,1024]{2,1,0:T(8,128)(2,1)S(1)}, u32[]{:S(2)}, u32[]{:S(2)}) collective-permute-start(bf16[12,8,1024]{2,1,0:T(8,128)(2,1)S(1)} %get-tuple-element.19), channel_id=1, source_target_pairs={{0,1},{1,2},{2,3},{3,4},{4,5},{5,6},{6,7},{7,8},{8,9},{9,10},{10,1... | collective-permute-start | bytes 589832 | tf_op jit(solution)/shard_map/ppermute | solution.py:421
  117.0 55.3 %collective-permute-start.3 = (bf16[12,8,2048]{2,1,0:T(8,128)(2,1)S(1)}, bf16[12,8,2048]{2,1,0:T(8,128)(2,1)S(1)}, u32[]{:S(2)}, u32[]{:S(2)}) collective-permute-start(bf16[12,8,2048]{2,1,0:T(8,128)(2,1)S(1)} %get-tuple-element.18), channel_id=1, source_target_pairs={{16,0},{32,16},{48,32},{64,48},{80,64},{96,80},{112,96},{17,1},{33... | collective-permute-start | bytes 1179656 | tf_op jit(solution)/shard_map/ppermute | solution.py:420
  157.8 14.4 %copy-start.1 = (bf16[128,8,2048]{2,1,0:T(8,128)(2,1)S(1)}, bf16[128,8,2048]{2,1,0:T(8,128)(2,1)}, u32[]{:S(2)}) copy-start(bf16[128,8,2048]{2,1,0:T(8,128)(2,1)} %all_to_all.17.refs_1_) | copy-start | bytes 12582916
  160.7 24.9 %collective-permute-start = (bf16[12,8,2048]{2,1,0:T(8,128)(2,1)S(1)}, bf16[12,8,2048]{2,1,0:T(8,128)(2,1)S(1)}, u32[]{:S(2)}, u32[]{:S(2)}) collective-permute-start(bf16[12,8,2048]{2,1,0:T(8,128)(2,1)S(1)} %get-tuple-element.14), channel_id=1, source_target_pairs={{0,16},{16,32},{32,48},{48,64},{64,80},{80,96},{96,112},{1,17},{17... | collective-permute-start | bytes 1179656 | tf_op jit(solution)/shard_map/ppermute | solution.py:420
  162.7 9.6 %collective-permute-start.5 = (bf16[12,8,1024]{2,1,0:T(8,128)(2,1)S(1)}, bf16[12,8,1024]{2,1,0:T(8,128)(2,1)S(1)}, u32[]{:S(2)}, u32[]{:S(2)}) collective-permute-start(bf16[12,8,1024]{2,1,0:T(8,128)(2,1)S(1)} %get-tuple-element.20), channel_id=1, source_target_pairs={{1,0},{2,1},{3,2},{4,3},{5,4},{6,5},{7,6},{8,7},{9,8},{10,9},{11,1... | collective-permute-start | bytes 589832 | tf_op jit(solution)/shard_map/ppermute | solution.py:422
  164.6 21.0 %collective-permute-start.1 = (bf16[12,8,1024]{2,1,0:T(8,128)(2,1)S(1)}, bf16[12,8,1024]{2,1,0:T(8,128)(2,1)S(1)}, u32[]{:S(2)}, u32[]{:S(2)}) collective-permute-start(bf16[12,8,1024]{2,1,0:T(8,128)(2,1)S(1)} %get-tuple-element.15), channel_id=1, source_target_pairs={{0,1},{1,2},{2,3},{3,4},{4,5},{5,6},{6,7},{7,8},{8,9},{9,10},{10,1... | collective-permute-start | bytes 589832 | tf_op jit(solution)/shard_map/ppermute | solution.py:421
  168.0 17.6 %collective-permute-start.2 = (bf16[12,8,1024]{2,1,0:T(8,128)(2,1)S(1)}, bf16[12,8,1024]{2,1,0:T(8,128)(2,1)S(1)}, u32[]{:S(2)}, u32[]{:S(2)}) collective-permute-start(bf16[12,8,1024]{2,1,0:T(8,128)(2,1)S(1)} %get-tuple-element.16), channel_id=1, source_target_pairs={{1,0},{2,1},{3,2},{4,3},{5,4},{6,5},{7,6},{8,7},{9,8},{10,9},{11,1... | collective-permute-start | bytes 589832 | tf_op jit(solution)/shard_map/ppermute | solution.py:422

commit v2 on v1

v2 whole, which is shorter than its diff:
```python
import math

import jax
import jax.numpy as jnp
import ml_dtypes
import numpy as np
from jax import lax
from jax.experimental import pallas as pl
from jax.experimental.pallas import tpu as pltpu
from jax.sharding import PartitionSpec as P

VS = 16
BX, BY, BZ = 4, 4, 6
BLOCKS = BX * BY * BZ
TOTAL = VS * VS * VS
CELLS = 8
SLAB = BY * BZ
RELAX_INCREMENT = 0.3
COURANT = 0.028
SPACING = 3.0 / VS
LOG2E = 1.0 / math.log(2.0)

SPLIT = (0, 24, 32)
CHUNKS = len(SPLIT) - 1
PIECE = 16
GROUP = 8
STEP = 512
X_HALO = BLOCKS
Y_HALO = X_HALO + SLAB
HELD = Y_HALO + BX * BZ


def lanes_of(chunk):
    return pl.ds(SPLIT[chunk] * 128, width_of(chunk))


def width_of(chunk):
    return 128 * (SPLIT[chunk + 1] - SPLIT[chunk])


def tiles_of(chunk):
    found, count_x, count_y = [], [0, 0], [0, 0]
    for tile in range(SPLIT[chunk], SPLIT[chunk + 1]):
        x, y = int(tile >= TOTAL // 256), tile % 2
        found.append((tile - SPLIT[chunk], x, y, count_x[x], count_y[y]))
        count_x[x] += 1
        count_y[y] += 1
    return found, count_x, count_y


def lanes(tile):
    return pl.ds(tile * 128, 128)


def basis_rows():
    index = np.arange(TOTAL)
    x, y, z = (2 * i + 1 - VS for i in (index // (VS * VS), index // VS % VS, index % VS))
    rows = np.zeros((16, TOTAL), np.float32)
    rows[:10] = [np.ones_like(x), x, y, z, x * x, y * y, z * z, x * y, x * z, y * z]
    whole = np.zeros((128, TOTAL), np.float32)
    for copy in range(3):
        whole[16 * copy : 16 * copy + 16] = rows
    return whole.astype(ml_dtypes.bfloat16)


def coefficients_of(sums):
    raw = [sums[i : i + 1] * (1.0 / TOTAL) for i in range(10)]
    density = raw[0]
    drift = [SPACING * raw[1 + a] / density for a in range(3)]
    square = SPACING * SPACING
    spread = [square * raw[4 + a] / density - drift[a] * drift[a] for a in range(3)]
    spread_xy = square * raw[7] / density - drift[0] * drift[1]
    spread_xz = square * raw[8] / density - drift[0] * drift[2]
    spread_yz = square * raw[9] / density - drift[1] * drift[2]
    temperature = (spread[0] + spread[1] + spread[2]) / 3.0
    xx, yy, zz = (1.5 * temperature - 0.5 * s for s in spread)
    xy, xz, yz = (-0.5 * s for s in (spread_xy, spread_xz, spread_yz))
    adj_xx, adj_yy, adj_zz = yy * zz - yz * yz, xx * zz - xz * xz, xx * yy - xy * xy
    adj_xy, adj_xz, adj_yz = xz * yz - xy * zz, xy * yz - xz * yy, xy * xz - xx * yz
    determinant = xx * adj_xx + xy * adj_xy + xz * adj_xz
    inv = [a / determinant for a in (adj_xx, adj_yy, adj_zz, adj_xy, adj_xz, adj_yz)]
    pull = [
        inv[0] * drift[0] + inv[3] * drift[1] + inv[4] * drift[2],
        inv[3] * drift[0] + inv[1] * drift[1] + inv[5] * drift[2],
        inv[4] * drift[0] + inv[5] * drift[1] + inv[2] * drift[2],
    ]
    quadratic = drift[0] * pull[0] + drift[1] * pull[1] + drift[2] * pull[2]
    log_prefactor = (
        jnp.log(density)
        + (3.0 * math.log(6.0) - 1.5 * math.log(2.0 * math.pi))
        - 0.5 * jnp.log(determinant)
    )
    rows = [log_prefactor - 0.5 * quadratic]
    rows += [SPACING * p for p in pull]
    rows += [-0.5 * square * i for i in inv[:3]]
    rows += [-square * i for i in inv[3:]]
    fraction = 1.0 - jnp.exp(-RELAX_INCREMENT * density * jnp.sqrt(temperature))
    return [LOG2E * r for r in rows], fraction


def relax_kernel(dist, basis, *rest):
    outs = rest[:CHUNKS]
    held, relaxed, sums, factors, in_sems, out_sems = rest[CHUNKS:]
    pieces = BLOCKS // PIECE

    def arrival(piece):
        rows = pl.ds(piece * PIECE, PIECE)
        return pltpu.make_async_copy(dist.at[rows], held.at[rows], in_sems.at[piece])

    def departure(first, count, chunk):
        rows, lanes = pl.ds(first, count), lanes_of(chunk)
        return pltpu.make_async_copy(
            relaxed.at[rows, :, lanes], outs[chunk].at[rows], out_sems.at[chunk]
        )

    for piece in range(pieces):
        arrival(piece).start()
    for piece in range(pieces):
        arrival(piece).wait()
        cells = held[pl.ds(piece * PIECE, PIECE)].astype(jnp.float32)
        cells = cells.reshape(PIECE * CELLS, TOTAL).astype(jnp.bfloat16)
        sums[:, pl.ds(piece * PIECE * CELLS, PIECE * CELLS)] = lax.dot_general(
            basis[0:16, :], cells, (((1,), (1,)), ((), ())), preferred_element_type=jnp.float32
        )

    rows, fraction = coefficients_of(sums[...])
    exact = [[], [], []]
    for row in rows:
        for part in range(3):
            near = row.astype(jnp.bfloat16).astype(jnp.float32)
            exact[part].append(near)
            row = row - near
    zero = jnp.zeros((6, BLOCKS * CELLS), jnp.float32)
    stacked = jnp.concatenate(
        exact[0]
        + [zero]
        + exact[1]
        + [zero]
        + exact[2]
        + [zero, fraction, jnp.zeros((79, BLOCKS * CELLS), jnp.float32)],
        axis=0,
    )
    factors[...] = stacked.T

    @pl.loop(0, BLOCKS // GROUP)
    def _(group):
        first = group * GROUP
        own = factors[pl.ds(pl.multiple_of(first * CELLS, GROUP * CELLS), GROUP * CELLS), :]
        left = own.astype(jnp.bfloat16)
        fraction = jnp.broadcast_to(own[:, 48:49], (GROUP * CELLS, 128))
        for step in range(TOTAL // STEP):
            power = jnp.dot(
                left, basis[:, pl.ds(step * STEP, STEP)], preferred_element_type=jnp.float32
            )
            for tile in range(STEP // 128):
                lanes = pl.ds(step * STEP + tile * 128, 128)
                gauss = jnp.exp2(power[:, tile * 128 : tile * 128 + 128])
                moved = held[pl.ds(first, GROUP), :, lanes].astype(jnp.float32)
                moved = moved.reshape(GROUP * CELLS, 128)
                mixed = moved + fraction * (gauss - moved)
                relaxed[pl.ds(first, GROUP), :, lanes] = mixed.reshape(
                    GROUP, CELLS, 128
                ).astype(jnp.bfloat16)
        for chunk in range(CHUNKS):
            departure(first, GROUP, chunk).start()

    for chunk in range(CHUNKS):
        departure(0, BLOCKS, chunk).wait()


def relax(dist):
    return pl.pallas_call(
        relax_kernel,
        out_shape=[
            jax.ShapeDtypeStruct((BLOCKS, CELLS, width_of(c)), jnp.bfloat16) for c in range(CHUNKS)
        ],
        in_specs=[
            pl.BlockSpec(memory_space=pl.ANY),
            pl.BlockSpec(memory_space=pltpu.VMEM),
        ],
        out_specs=[pl.BlockSpec(memory_space=pl.ANY)] * CHUNKS,
        scratch_shapes=[
            pltpu.VMEM((BLOCKS, CELLS, TOTAL), jnp.bfloat16),
            pltpu.VMEM((BLOCKS, CELLS, TOTAL), jnp.bfloat16),
            pltpu.VMEM((16, BLOCKS * CELLS), jnp.float32),
            pltpu.VMEM((BLOCKS * CELLS, 128), jnp.float32),
            pltpu.SemaphoreType.DMA((BLOCKS // PIECE,)),
            pltpu.SemaphoreType.DMA((CHUNKS,)),
        ],
        compiler_params=pltpu.CompilerParams(vmem_limit_bytes=60 << 20),
        cost_estimate=pl.CostEstimate(
            flops=2 * BLOCKS * CELLS * TOTAL * 1500,
            bytes_accessed=4 * BLOCKS * CELLS * TOTAL,
            transcendentals=BLOCKS * CELLS * TOTAL,
        ),
        name="relax",
    )(dist, basis_rows())


def pack_kernel(asked, relaxed, send, sem):
    @pl.loop(0, asked.shape[0])
    def _(device):
        slot = asked[device]

        @pl.when(slot < BLOCKS)
        def _():
            pltpu.make_async_copy(relaxed.at[slot], send.at[device], sem).start()

    pltpu.make_async_copy(relaxed, send.at[pl.ds(0, BLOCKS)], sem).wait()


def pack(chunk, asked, relaxed, devices):
    width = width_of(chunk)
    return pl.pallas_call(
        pack_kernel,
        out_shape=jax.ShapeDtypeStruct((devices, CELLS, width), jnp.bfloat16),
        in_specs=[
            pl.BlockSpec(memory_space=pltpu.SMEM),
            pl.BlockSpec(memory_space=pl.ANY),
        ],
        out_specs=pl.BlockSpec(memory_space=pl.ANY),
        scratch_shapes=[pltpu.SemaphoreType.DMA(())],
        cost_estimate=pl.CostEstimate(
            flops=0, bytes_accessed=4 * BLOCKS * CELLS * width, transcendentals=0
        ),
        name=f"pack{chunk}",
    )(asked, relaxed)


def row_masks():
    row = lax.broadcasted_iota(jnp.int32, (CELLS, 128), 0)
    return row < 4, (row & 2) == 0, (row & 1) == 0


def swap(x, distance):
    if distance == 4:
        return pltpu.roll(x, 4, 0)
    row = lax.broadcasted_iota(jnp.int32, (CELLS, 128), 0)
    return jnp.take_along_axis(x, row ^ distance, axis=0)


def face_kinds(chunk):
    _, count_x, count_y = tiles_of(chunk)
    counts = [("x", 0, count_x[0]), ("x", 1, count_x[1]), ("y", 0, count_y[0]), ("y", 1, count_y[1])]
    return [k for k in counts if k[2]]


def face_block(axis, up, pair):
    if axis == "x":
        return (BX - 1) * SLAB * up + 2 * pair
    return pair // 3 * SLAB + up * (BY - 1) * BZ + pair % 3 * 2


def faces_kernel(chunk, owner, received, mask, *rest):
    kinds = face_kinds(chunk)
    faces, (held, sems) = rest[: len(kinds)], rest[len(kinds) :]
    low_x, low_y, _ = row_masks()

    for n, (axis, up, _) in enumerate(kinds):

        @pl.loop(0, 12)
        def _(pair):
            for side in range(2):
                block = face_block(axis, up, pair) + side
                pltpu.make_async_copy(
                    received.at[owner[block]], held.at[n * SLAB + 2 * pair + side], sems.at[n]
                ).start()

    for n, (axis, up, _) in enumerate(kinds):
        rows = pl.ds(n * SLAB, SLAB)
        pltpu.make_async_copy(received.at[pl.ds(0, SLAB)], held.at[rows], sems.at[n]).wait()

        @pl.loop(0, 12)
        def _(pair):
            block = face_block(axis, up, pair)
            masks = [mask[block + side] for side in range(2)]
            for tile, x, y, place_x, place_y in tiles_of(chunk)[0]:
                if up != (x if axis == "x" else y):
                    continue
                a, b = (
                    held[n * SLAB + 2 * pair + side, :, lanes(tile)].astype(jnp.float32)
                    * masks[side]
                    for side in range(2)
                )
                low = low_x if axis == "x" else low_y
                b = swap(b, 4 if axis == "x" else 2)
                face = jnp.where(low, b, a) if up else jnp.where(low, a, b)
                place = place_x if axis == "x" else place_y
                faces[n][pair, :, lanes(place)] = face.astype(jnp.bfloat16)


def faces(chunk, owner, received, mask):
    kinds = face_kinds(chunk)
    moved = sum(128 * tiles for _, _, tiles in kinds)
    return pl.pallas_call(
        lambda *refs: faces_kernel(chunk, *refs),
        out_shape=[
            jax.ShapeDtypeStruct((12, CELLS, 128 * tiles), jnp.bfloat16) for _, _, tiles in kinds
        ],
        in_specs=[
            pl.BlockSpec(memory_space=pltpu.SMEM),
            pl.BlockSpec(memory_space=pl.ANY),
            pl.BlockSpec(memory_space=pltpu.VMEM),
        ],
        out_specs=[pl.BlockSpec(memory_space=pltpu.VMEM)] * len(kinds),
        scratch_shapes=[
            pltpu.VMEM((len(kinds) * SLAB, CELLS, width_of(chunk)), jnp.bfloat16),
            pltpu.SemaphoreType.DMA((len(kinds),)),
        ],
        compiler_params=pltpu.CompilerParams(vmem_limit_bytes=20 << 20),
        cost_estimate=pl.CostEstimate(
            flops=8 * SLAB * CELLS * moved,
            bytes_accessed=8 * SLAB * CELLS * moved,
            transcendentals=0,
        ),
        name=f"faces{chunk}",
    )(owner, received, mask)


def advance_kernel(chunk, owner, received, mask, rate, *rest):
    kinds = face_kinds(chunk)
    halos, (out, held, kept, made, in_sems, out_sems) = rest[: len(kinds)], rest[-6:]
    tiles = tiles_of(chunk)[0]
    low_x, low_y, low_z = row_masks()
    lane = lax.broadcasted_iota(jnp.int32, (CELLS, 128), 1)
    speed_z = SPACING * jnp.abs(2 * (lane % VS) + 1 - VS).astype(jnp.float32)
    speed_y = [
        SPACING * jnp.abs(2 * (lane // VS + 8 * odd) + 1 - VS).astype(jnp.float32)
        for odd in range(2)
    ]
    rising_z = lane % VS >= VS // 2
    from_below = rising_z & ~low_z
    from_above = ~rising_z & low_z
    nothing = jnp.zeros((CELLS, 128), jnp.float32)

    for slab in range(BX):

        @pl.loop(slab * SLAB, slab * SLAB + SLAB)
        def _(block):
            pltpu.make_async_copy(
                received.at[owner[block]], held.at[block], in_sems.at[slab]
            ).start()

    for (axis, up, _), halo in zip(kinds, halos):

        @pl.loop(0, 12)
        def _(pair):
            for tile, x, y, place_x, place_y in tiles:
                if up != (x if axis == "x" else y):
                    continue
                place = place_x if axis == "x" else place_y
                first = X_HALO if axis == "x" else Y_HALO
                face = halo[pair, :, lanes(place)].astype(jnp.float32)
                kept[first + 2 * pair, :, lanes(tile)] = face
                kept[first + 2 * pair + 1, :, lanes(tile)] = swap(face, 4 if axis == "x" else 2)

    for slab in range(BX):
        rows = pl.ds(slab * SLAB, SLAB)
        pltpu.make_async_copy(received.at[pl.ds(0, SLAB)], held.at[rows], in_sems.at[slab]).wait()

        @pl.loop(slab * SLAB, slab * SLAB + SLAB)
        def _(block):
            own_mask = mask[block]
            for tile in range(len(tiles)):
                kept[block, :, lanes(tile)] = (
                    held[block, :, lanes(tile)].astype(jnp.float32) * own_mask
                )

    def result_copy(bx):
        rows = pl.ds(bx * SLAB, SLAB)
        return pltpu.make_async_copy(
            made.at[rows], out.at[rows, :, lanes_of(chunk)], out_sems.at[bx]
        )

    for bx in range(BX):

        @pl.loop(0, BY)
        def _(by):
            line = bx * SLAB + by * BZ
            side = Y_HALO + bx * BZ
            near_y = [
                jnp.where(by == BY - 1, side, line + BZ),
                jnp.where(by == 0, side, line - BZ),
            ]
            near_x = [
                X_HALO + by * BZ if bx == BX - 1 else line + SLAB,
                X_HALO + by * BZ if bx == 0 else line - SLAB,
            ]
            for tile, x, y, _, _ in tiles:
                own_line = [kept[line + bz, :, lanes(tile)] for bz in range(BZ)]
                speed_x = SPACING * abs(2 * ((SPLIT[chunk] + tile) // 2) + 1 - VS)
                for bz in range(BZ):
                    own = own_line[bz]
                    below = own_line[bz - 1] if bz else nothing
                    above = own_line[bz + 1] if bz < BZ - 1 else nothing
                    other = kept[near_x[x] + bz, :, lanes(tile)]
                    from_x = swap(
                        jnp.where(low_x, own, other) if x else jnp.where(low_x, other, own), 4
                    )
                    other = kept[near_y[y] + bz, :, lanes(tile)]
                    from_y = swap(
                        jnp.where(low_y, own, other) if y else jnp.where(low_y, other, own), 2
                    )
                    from_z = swap(
                        jnp.where(from_below, below, jnp.where(from_above, above, own)), 1
                    )
                    flux = (
                        speed_x * (own - from_x)
                        + speed_y[y] * (own - from_y)
                        + speed_z * (own - from_z)
                    )
                    made[line + bz, :, lanes(tile)] = (own - rate[line + bz] * flux).astype(
                        jnp.bfloat16
                    )

        result_copy(bx).start()
    for bx in range(BX):
        result_copy(bx).wait()


def advance(chunk, owner, received, mask, rate, halos, earlier):
    anywhere = pl.BlockSpec(memory_space=pl.ANY)
    vmem = pl.BlockSpec(memory_space=pltpu.VMEM)
    extra = [] if earlier is None else [earlier]
    width = width_of(chunk)
    return pl.pallas_call(
        lambda *refs: advance_kernel(chunk, *refs),
        out_shape=jax.ShapeDtypeStruct((BLOCKS, CELLS, TOTAL), jnp.bfloat16),
        in_specs=[pl.BlockSpec(memory_space=pltpu.SMEM), anywhere]
        + [vmem] * (2 + len(halos))
        + [anywhere] * len(extra),
        out_specs=anywhere,
        scratch_shapes=[
            pltpu.VMEM((BLOCKS, CELLS, width), jnp.bfloat16),
            pltpu.VMEM((HELD, CELLS, width), jnp.float32),
            pltpu.VMEM((BLOCKS, CELLS, width), jnp.bfloat16),
            pltpu.SemaphoreType.DMA((BX,)),
            pltpu.SemaphoreType.DMA((BX,)),
        ],
        input_output_aliases={} if earlier is None else {4 + len(halos): 0},
        compiler_params=pltpu.CompilerParams(vmem_limit_bytes=40 << 20),
        cost_estimate=pl.CostEstimate(
            flops=100 * BLOCKS * CELLS * width,
            bytes_accessed=5 * BLOCKS * CELLS * width,
            transcendentals=0,
        ),
        name=f"advance{chunk}",
    )(owner, received, mask, rate, *halos, *extra)


def after(received, source_owner, levels, active):
    n_gx, n_gy = lax.axis_size("gx"), lax.axis_size("gy")
    mask = jnp.broadcast_to(
        active.astype(jnp.float32)[:, :, None], (BLOCKS, CELLS, 128)
    )
    courant = COURANT * jnp.exp2(levels.astype(jnp.float32))
    rate = mask * courant[:, None, None]

    def up(n):
        return [(i, i + 1) for i in range(n - 1)]

    def down(n):
        return [(i + 1, i) for i in range(n - 1)]

    out = None
    for chunk in range(CHUNKS):
        arrived = received[chunk]
        if out is not None:
            arrived, out = lax.optimization_barrier((arrived, out))
        sent = faces(chunk, source_owner, arrived, mask)
        halos = []
        for (axis, to_above, _), face in zip(face_kinds(chunk), sent):
            name, n = ("gx", n_gx) if axis == "x" else ("gy", n_gy)
            halos.append(lax.ppermute(face, name, up(n) if to_above else down(n)))
        out = advance(chunk, source_owner, arrived, mask, rate, halos, out)
    return out


def per_device(dist_old, source_owner, levels, active):
    axes = ("gx", "gy")
    n_gx, n_gy = lax.axis_size("gx"), lax.axis_size("gy")
    devices = n_gx * n_gy
    slots = lax.broadcasted_iota(jnp.int32, (devices, BLOCKS), 1)
    owners = lax.broadcasted_iota(jnp.int32, (devices, BLOCKS), 0)
    request = BLOCKS + jnp.sum(
        jnp.where(source_owner[None, :] == owners, slots - BLOCKS, 0), axis=1
    )
    asked = lax.all_to_all(request, axes, split_axis=0, concat_axis=0, tiled=True)
    received = [
        lax.all_to_all(
            pack(chunk, asked, relaxed, devices), axes, split_axis=0, concat_axis=0, tiled=True
        )
        for chunk, relaxed in enumerate(relax(dist_old))
    ]
    return after(received, source_owner, levels, active)


def solution(mesh):
    return jax.shard_map(
        per_device,
        mesh=mesh,
        in_specs=(
            P(("gx", "gy"), None, None),
            P(("gx", "gy")),
            P(("gx", "gy")),
            P(("gx", "gy"), None),
        ),
        out_specs=P(("gx", "gy"), None, None),
        check_vma=False,
    )
```

time: 198 us -> 334 us (1.69)
  Pallas kernels: 49.1 us -> 230 us
  blocking collectives: 75.8 us -> 0 us
  starting transfers between devices: 24.3 us -> 49.9 us
  waiting for transfers between devices: 38.3 us -> 47.3 us
    pallas_call x1 -> x3, Pallas kernels: 19 us -> 206 us  [the longest x2 194 us: pack(): pl.pallas_call(pack_kernel, out_shape=jax.ShapeDtypeStruct((devices, CELL...]
    all_to_all x2 -> x0, blocking collectives: 75.8 us -> none  [the longest x1 57.3 us: per_device(): lax.all_to_all(s, axes, split_axis=0, concat_axis=0, tiled=True)]
    ppermute x6 -> x7, waiting for transfers between devices: 0.02 us -> 22.3 us  [after(): halos.append(lax.ppermute(face, name, up(n) if to_above else down(n)))]
    all_to_all x1 -> x3, starting transfers between devices: 7.16 us -> 28.7 us  [the longest x2 17.9 us: per_device(): lax.all_to_all(pack(chunk, asked, relaxed, devices), axes, split_axis=0,...]
    all_to_all x1 -> x3, waiting for transfers between devices: 38.3 us -> 24.9 us  [the longest x2 24.9 us: per_device(): lax.all_to_all(pack(chunk, asked, relaxed, devices), axes, split_axis=0,...]
    pallas_call x2, Pallas kernels: 22.6 us -> 17.1 us  [advance(): pl.pallas_call(lambda *refs: advance_kernel(chunk, *refs), out_shape=jax....]
    ppermute x6 -> x7, starting transfers between devices: 17.1 us -> 21.2 us  [after(): halos.append(lax.ppermute(face, name, up(n) if to_above else down(n)))]
    unnamed x14 -> x6, local copies, waits for them, and re-layouts: 3.43 us -> 0.02 us
  transfers between devices with their start and end apart: 7 -> 10, of which waited for: 1 -> 6; matrix products, arithmetic and copies ran while one was open for 0% -> 0% of each run, Pallas kernels for 11% -> 23%
where the time goes in v2:
time: 334 us; the launch traced here: 333 us
  Pallas kernels  230 us (69%)
  starting transfers between devices  49.9 us (15%)
  waiting for transfers between devices  47.3 us (14%)
  other arithmetic  3.98 us (1%)
    pallas_call x2, Pallas kernels, pack(): pl.pallas_call(pack_kernel, out_shape=jax.ShapeDtypeStruct((devices, CELL...  194 us
    all_to_all x2, waiting for transfers between devices, per_device(): lax.all_to_all(pack(chunk, asked, relaxed, devices), axes, split_axis=0,...  24.9 us
    ppermute x7, waiting for transfers between devices, after(): halos.append(lax.ppermute(face, name, up(n) if to_above else down(n)))  22.3 us
    ppermute x7, starting transfers between devices, after(): halos.append(lax.ppermute(face, name, up(n) if to_above else down(n)))  21.2 us
    all_to_all x2, starting transfers between devices, per_device(): lax.all_to_all(pack(chunk, asked, relaxed, devices), axes, split_axis=0,...  17.9 us
    pallas_call x2, Pallas kernels, advance(): pl.pallas_call(lambda *refs: advance_kernel(chunk, *refs), out_shape=jax....  17.1 us
    pallas_call x1, Pallas kernels, relax(): pl.pallas_call(relax_kernel, out_shape=[jax.ShapeDtypeStruct((BLOCKS, CEL...  12.1 us
    all_to_all x1, starting transfers between devices, per_device(): lax.all_to_all(request, axes, split_axis=0, concat_axis=0, tiled=True)  10.8 us
  transfers between devices with their start and end apart: 10, of which 6 were waited for; matrix products, arithmetic and copies ran while one was open for 0% of the time, Pallas kernels for 23%

profile of v2, /device:TPU:7, one launch (start us, length us, event | category | flops | bytes accessed | tf_op | source)
XLA Modules:
  0.0 332.7 jit_solution(10138354984979717512)
XLA Ops:
  1.5 10.8 %all-to-all-start = ((s32[128,1,1]{2,1,0:T(1,128)}), s32[128,1,1]{2,1,0:T(1,128)S(1)}, u32[]{:S(2)}, u32[]{:S(2)}) async-start(s32[128,1,1]{2,1,0:T(1,128)} %copy.12), calls=%async_computation | async-start | bytes 131072 | tf_op jit(solution)/shard_map/all_to_all | solution.py:488
  12.3 12.1 %relax.1 = (bf16[96,8,3072]{2,1,0:T(8,128)(2,1)}, bf16[96,8,1024]{2,1,0:T(8,128)(2,1)}) custom-call(bf16[96,8,4096]{2,1,0:T(8,128)(2,1)} %dist.1, bf16[128,4096]{1,0:T(8,128)(2,1)} %constant.13.clone.basis), custom_call_target="tpu_custom_call" | custom-call | flops 9437184000 | bytes 12582912 | tf_op jit(solution)/shard_map/relax/pallas_call | solution.py:172
  24.5 2.9 reduce.asked
  27.4 144.7 %pack0.1 = bf16[128,8,3072]{2,1,0:T(8,128)(2,1)} custom-call(s32[128]{0:T(128)} %reduce.asked, bf16[96,8,3072]{2,1,0:T(8,128)(2,1)} %get-tuple-element.17.relaxed), custom_call_target="tpu_custom_call" | custom-call | bytes 9437184 | tf_op jit(solution)/shard_map/pack0/pallas_call | solution.py:214
  172.1 10.2 %all-to-all-start.2 = ((bf16[128,8,3072]{2,1,0:T(8,128)(2,1)}), bf16[128,8,3072]{2,1,0:T(8,128)(2,1)}, u32[]{:S(2)}, u32[]{:S(2)}) async-start(bf16[128,8,3072]{2,1,0:T(8,128)(2,1)} %pack0.1), calls=%async_computation.2 | async-start | bytes 12582912 | tf_op jit(solution)/shard_map/all_to_all | solution.py:490
  182.3 49.6 %pack1.1 = bf16[128,8,1024]{2,1,0:T(8,128)(2,1)} custom-call(s32[128]{0:T(128)} %reduce.asked, bf16[96,8,1024]{2,1,0:T(8,128)(2,1)} %get-tuple-element.16.relaxed), custom_call_target="tpu_custom_call" | custom-call | bytes 3145728 | tf_op jit(solution)/shard_map/pack1/pallas_call | solution.py:214
  231.9 24.9 %all-to-all-done.2.refs_1_ = bf16[128,8,3072]{2,1,0:T(8,128)(2,1)} async-done(((bf16[128,8,3072]{2,1,0:T(8,128)(2,1)}), bf16[128,8,3072]{2,1,0:T(8,128)(2,1)}, u32[]{:S(2)}, u32[]{:S(2)}) %all-to-all-start.2) | async-done | bytes 6291488 | tf_op jit(solution)/shard_map/all_to_all | solution.py:490
  256.9 7.8 %all-to-all-start.1 = ((bf16[128,8,1024]{2,1,0:T(8,128)(2,1)}), bf16[128,8,1024]{2,1,0:T(8,128)(2,1)S(1)}, u32[]{:S(2)}, u32[]{:S(2)}) async-start(bf16[128,8,1024]{2,1,0:T(8,128)(2,1)} %pack1.1), calls=%async_computation.1 | async-start | bytes 4194304 | tf_op jit(solution)/shard_map/all_to_all | solution.py:490
  264.9 3.3 %faces0.1 = (bf16[12,8,2048]{2,1,0:T(8,128)(2,1)S(1)}, bf16[12,8,1024]{2,1,0:T(8,128)(2,1)S(1)}, bf16[12,8,1536]{2,1,0:T(8,128)(2,1)S(1)}, bf16[12,8,1536]{2,1,0:T(8,128)(2,1)S(1)}) custom-call(s32[96]{0:T(128)S(1)} %copy-done, bf16[128,8,3072]{2,1,0:T(8,128)(2,1)} %all-to-all-done.2.refs_1_, f32[96,8,128]{2,1,0:T(8,128)S(1)} %broadcast_in_dim.7.refs_2_), custom_call_target="tpu_custom_call" | custom-call | flops 9437184 | bytes 9437184 | tf_op jit(solution)/shard_map/faces0/pallas_call | solution.py:295
  268.2 2.3 collective-permute-start
  270.5 5.3 %collective-permute-start.2 = (bf16[12,8,1536]{2,1,0:T(8,128)(2,1)S(1)}, bf16[12,8,1536]{2,1,0:T(8,128)(2,1)S(1)}, u32[]{:S(2)}, u32[]{:S(2)}) collective-permute-start(bf16[12,8,1536]{2,1,0:T(8,128)(2,1)S(1)} %get-tuple-element.20), channel_id=1, source_target_pairs={{1,0},{2,1},{3,2},{4,3},{5,4},{6,5},{7,6},{8,7},{9,8},{10,9},{11,1... | collective-permute-start | bytes 884744 | tf_op jit(solution)/shard_map/ppermute | solution.py:474
  275.8 1.9 collective-permute-start.3
  277.8 3.6 %collective-permute-start.1 = (bf16[12,8,1024]{2,1,0:T(8,128)(2,1)S(1)}, bf16[12,8,1024]{2,1,0:T(8,128)(2,1)S(1)}, u32[]{:S(2)}, u32[]{:S(2)}) collective-permute-start(bf16[12,8,1024]{2,1,0:T(8,128)(2,1)S(1)} %get-tuple-element.19), channel_id=1, source_target_pairs={{0,16},{16,32},{32,48},{48,64},{64,80},{80,96},{96,112},{1,17},{17... | collective-permute-start | bytes 589832 | tf_op jit(solution)/shard_map/ppermute | solution.py:474
  281.6 7.4 %collective-permute-done.1.refs_5_ = bf16[12,8,1024]{2,1,0:T(8,128)(2,1)S(1)} collective-permute-done((bf16[12,8,1024]{2,1,0:T(8,128)(2,1)S(1)}, bf16[12,8,1024]{2,1,0:T(8,128)(2,1)S(1)}, u32[]{:S(2)}, u32[]{:S(2)}) %collective-permute-start.1) | collective-permute-done | bytes 196640 | tf_op jit(solution)/shard_map/ppermute | solution.py:474
  289.0 6.9 %collective-permute-done.2.refs_6_ = bf16[12,8,1536]{2,1,0:T(8,128)(2,1)S(1)} collective-permute-done((bf16[12,8,1536]{2,1,0:T(8,128)(2,1)S(1)}, bf16[12,8,1536]{2,1,0:T(8,128)(2,1)S(1)}, u32[]{:S(2)}, u32[]{:S(2)}) %collective-permute-start.2) | collective-permute-done | bytes 294944 | tf_op jit(solution)/shard_map/ppermute | solution.py:474
  295.9 2.7 collective-permute-done.3.refs_7_
  298.6 10.0 %advance0.1.refs_7_ = bf16[96,8,4096]{2,1,0:T(8,128)(2,1)} custom-call(s32[96]{0:T(128)S(1)} %copy-done, bf16[128,8,3072]{2,1,0:T(8,128)(2,1)} %all-to-all-done.2.refs_1_, f32[96,8,128]{2,1,0:T(8,128)S(1)} %broadcast_in_dim.7.refs_2_, f32[96,8,128]{2,1,0:T(8,128)S(1)} %broadcast_multiply_fusion.refs_3_, ...), custom_call_target="tpu_custom_call" | custom-call | flops 235929600 | bytes 11796480 | tf_op jit(solution)/shard_map/advance0/pallas_call | solution.py:426
  308.6 3.5 %faces1.1 = (bf16[12,8,1024]{2,1,0:T(8,128)(2,1)S(1)}, bf16[12,8,512]{2,1,0:T(8,128)(2,1)S(1)}, bf16[12,8,512]{2,1,0:T(8,128)(2,1)S(1)}) custom-call(s32[96]{0:T(128)S(1)} %copy-done, bf16[128,8,1024]{2,1,0:T(8,128)(2,1)S(1)} %all-to-all-done.1.refs_1_, f32[96,8,128]{2,1,0:T(8,128)S(1)} %broadcast_in_dim.7.refs_2_), custom_call_target="tpu_custom_call" | custom-call | flops 3145728 | bytes 3145728 | tf_op jit(solution)/shard_map/faces1/pallas_call | solution.py:295
  312.1 2.9 collective-permute-start.4
  315.0 2.3 collective-permute-start.5
  317.2 3.0 collective-permute-start.6
  320.3 1.4 collective-permute-done.5.refs_5_
  321.7 3.9 %collective-permute-done.6.refs_6_ = bf16[12,8,512]{2,1,0:T(8,128)(2,1)S(1)} collective-permute-done((bf16[12,8,512]{2,1,0:T(8,128)(2,1)S(1)}, bf16[12,8,512]{2,1,0:T(8,128)(2,1)S(1)}, u32[]{:S(2)}, u32[]{:S(2)}) %collective-permute-start.6) | collective-permute-done | bytes 98336 | tf_op jit(solution)/shard_map/ppermute | solution.py:474
  325.6 7.2 %advance1.1 = bf16[96,8,4096]{2,1,0:T(8,128)(2,1)} custom-call(s32[96]{0:T(128)S(1)} %copy-done, bf16[128,8,1024]{2,1,0:T(8,128)(2,1)S(1)} %all-to-all-done.1.refs_1_, f32[96,8,128]{2,1,0:T(8,128)S(1)} %broadcast_in_dim.7.refs_2_, f32[96,8,128]{2,1,0:T(8,128)S(1)} %broadcast_multiply_fusion.refs_3_, ...), custom_call_target="tpu_custom_call", output_to_operand_aliasing={{}: (7, {})} | custom-call | flops 78643200 | bytes 3932160 | tf_op jit(solution)/shard_map/advance1/pallas_call | solution.py:426
  (19 shorter events, 2.1 us)
Async XLA Ops:
  1.5 22.9 %all-to-all-start = ((s32[128,1,1]{2,1,0:T(1,128)}), s32[128,1,1]{2,1,0:T(1,128)S(1)}, u32[]{:S(2)}, u32[]{:S(2)}) async-start(s32[128,1,1]{2,1,0:T(1,128)} %copy.12), calls=%async_computation | async-start | bytes 131072 | tf_op jit(solution)/shard_map/all_to_all | solution.py:488
  172.1 84.7 %all-to-all-start.2 = ((bf16[128,8,3072]{2,1,0:T(8,128)(2,1)}), bf16[128,8,3072]{2,1,0:T(8,128)(2,1)}, u32[]{:S(2)}, u32[]{:S(2)}) async-start(bf16[128,8,3072]{2,1,0:T(8,128)(2,1)} %pack0.1), calls=%async_computation.2 | async-start | bytes 12582912 | tf_op jit(solution)/shard_map/all_to_all | solution.py:490
  182.3 82.3 %copy-start.1 = (s32[96,8]{0,1:T(8,128)S(1)}, s32[96,8]{0,1:T(8,128)}, u32[]{:S(2)}) copy-start(s32[96,8]{0,1:T(8,128)} %param.8) | copy-start | bytes 9220
  182.3 82.6 %copy-start = (s32[96]{0:T(128)S(1)}, s32[96]{0:T(128)}, u32[]{:S(2)}) copy-start(s32[96]{0:T(128)} %refs_0_.7) | copy-start | bytes 1156
  231.9 45.8 %copy-start.2 = (s32[96]{0:T(128)S(1)}, s32[96]{0:T(128)}, u32[]{:S(2)}) copy-start(s32[96]{0:T(128)} %param.7) | copy-start | bytes 1156
  256.9 51.8 %all-to-all-start.1 = ((bf16[128,8,1024]{2,1,0:T(8,128)(2,1)}), bf16[128,8,1024]{2,1,0:T(8,128)(2,1)S(1)}, u32[]{:S(2)}, u32[]{:S(2)}) async-start(bf16[128,8,1024]{2,1,0:T(8,128)(2,1)} %pack1.1), calls=%async_computation.1 | async-start | bytes 4194304 | tf_op jit(solution)/shard_map/all_to_all | solution.py:490
  268.2 30.4 %collective-permute-start = (bf16[12,8,2048]{2,1,0:T(8,128)(2,1)S(1)}, bf16[12,8,2048]{2,1,0:T(8,128)(2,1)S(1)}, u32[]{:S(2)}, u32[]{:S(2)}) collective-permute-start(bf16[12,8,2048]{2,1,0:T(8,128)(2,1)S(1)} %get-tuple-element.18), channel_id=1, source_target_pairs={{16,0},{32,16},{48,32},{64,48},{80,64},{96,80},{112,96},{17,1},{33... | collective-permute-start | bytes 1179656 | tf_op jit(solution)/shard_map/ppermute | solution.py:474
  270.5 25.4 %collective-permute-start.2 = (bf16[12,8,1536]{2,1,0:T(8,128)(2,1)S(1)}, bf16[12,8,1536]{2,1,0:T(8,128)(2,1)S(1)}, u32[]{:S(2)}, u32[]{:S(2)}) collective-permute-start(bf16[12,8,1536]{2,1,0:T(8,128)(2,1)S(1)} %get-tuple-element.20), channel_id=1, source_target_pairs={{1,0},{2,1},{3,2},{4,3},{5,4},{6,5},{7,6},{8,7},{9,8},{10,9},{11,1... | collective-permute-start | bytes 884744 | tf_op jit(solution)/shard_map/ppermute | solution.py:474
  275.8 22.8 %collective-permute-start.3 = (bf16[12,8,1536]{2,1,0:T(8,128)(2,1)S(1)}, bf16[12,8,1536]{2,1,0:T(8,128)(2,1)S(1)}, u32[]{:S(2)}, u32[]{:S(2)}) collective-permute-start(bf16[12,8,1536]{2,1,0:T(8,128)(2,1)S(1)} %get-tuple-element.21), channel_id=1, source_target_pairs={{0,1},{1,2},{2,3},{3,4},{4,5},{5,6},{6,7},{7,8},{8,9},{9,10},{10,1... | collective-permute-start | bytes 884744 | tf_op jit(solution)/shard_map/ppermute | solution.py:474
  277.8 11.2 %collective-permute-start.1 = (bf16[12,8,1024]{2,1,0:T(8,128)(2,1)S(1)}, bf16[12,8,1024]{2,1,0:T(8,128)(2,1)S(1)}, u32[]{:S(2)}, u32[]{:S(2)}) collective-permute-start(bf16[12,8,1024]{2,1,0:T(8,128)(2,1)S(1)} %get-tuple-element.19), channel_id=1, source_target_pairs={{0,16},{16,32},{32,48},{48,64},{64,80},{80,96},{96,112},{1,17},{17... | collective-permute-start | bytes 589832 | tf_op jit(solution)/shard_map/ppermute | solution.py:474
  312.1 13.5 %collective-permute-start.4 = (bf16[12,8,1024]{2,1,0:T(8,128)(2,1)S(1)}, bf16[12,8,1024]{2,1,0:T(8,128)(2,1)S(1)}, u32[]{:S(2)}, u32[]{:S(2)}) collective-permute-start(bf16[12,8,1024]{2,1,0:T(8,128)(2,1)S(1)} %get-tuple-element.23), channel_id=1, source_target_pairs={{0,16},{16,32},{32,48},{48,64},{64,80},{80,96},{96,112},{1,17},{17... | collective-permute-start | bytes 589832 | tf_op jit(solution)/shard_map/ppermute | solution.py:474
  315.0 6.7 %collective-permute-start.5 = (bf16[12,8,512]{2,1,0:T(8,128)(2,1)S(1)}, bf16[12,8,512]{2,1,0:T(8,128)(2,1)S(1)}, u32[]{:S(2)}, u32[]{:S(2)}) collective-permute-start(bf16[12,8,512]{2,1,0:T(8,128)(2,1)S(1)} %get-tuple-element.24), channel_id=1, source_target_pairs={{1,0},{2,1},{3,2},{4,3},{5,4},{6,5},{7,6},{8,7},{9,8},{10,9},{11,1... | collective-permute-start | bytes 294920 | tf_op jit(solution)/shard_map/ppermute | solution.py:474
  317.2 8.3 %collective-permute-start.6 = (bf16[12,8,512]{2,1,0:T(8,128)(2,1)S(1)}, bf16[12,8,512]{2,1,0:T(8,128)(2,1)S(1)}, u32[]{:S(2)}, u32[]{:S(2)}) collective-permute-start(bf16[12,8,512]{2,1,0:T(8,128)(2,1)S(1)} %get-tuple-element.25), channel_id=1, source_target_pairs={{0,1},{1,2},{2,3},{3,4},{4,5},{5,6},{6,7},{7,8},{8,9},{9,10},{10,1... | collective-permute-start | bytes 294920 | tf_op jit(solution)/shard_map/ppermute | solution.py:474

commit v3 on v2

v3 whole, which is shorter than its diff:
```python
import math

import jax
import jax.numpy as jnp
import ml_dtypes
import numpy as np
from jax import lax
from jax.experimental import pallas as pl
from jax.experimental.pallas import tpu as pltpu
from jax.sharding import PartitionSpec as P

VS = 16
BX, BY, BZ = 4, 4, 6
BLOCKS = BX * BY * BZ
TOTAL = VS * VS * VS
CELLS = 8
SLAB = BY * BZ
RELAX_INCREMENT = 0.3
COURANT = 0.028
SPACING = 3.0 / VS
LOG2E = 1.0 / math.log(2.0)

TILES = TOTAL // 128
PIECE = 16
RELAX_VMEM = 60 << 20
PACK_VMEM = 54 << 20
FACES_VMEM = 16 << 20
ADVANCE_VMEM = 28 << 20
EDGE_VMEM = 20 << 20
GROUP = 8
STEP = 512


def lanes(tile):
    return pl.ds(tile * 128, 128)


def basis_rows():
    index = np.arange(TOTAL)
    x, y, z = (2 * i + 1 - VS for i in (index // (VS * VS), index // VS % VS, index % VS))
    rows = np.zeros((16, TOTAL), np.float32)
    rows[:10] = [np.ones_like(x), x, y, z, x * x, y * y, z * z, x * y, x * z, y * z]
    whole = np.zeros((48, TOTAL), np.float32)
    for copy in range(3):
        whole[16 * copy : 16 * copy + 16] = rows
    return whole.astype(ml_dtypes.bfloat16)


def coefficients_of(sums):
    raw = [sums[i : i + 1] * (1.0 / TOTAL) for i in range(10)]
    density = raw[0]
    drift = [SPACING * raw[1 + a] / density for a in range(3)]
    square = SPACING * SPACING
    spread = [square * raw[4 + a] / density - drift[a] * drift[a] for a in range(3)]
    spread_xy = square * raw[7] / density - drift[0] * drift[1]
    spread_xz = square * raw[8] / density - drift[0] * drift[2]
    spread_yz = square * raw[9] / density - drift[1] * drift[2]
    temperature = (spread[0] + spread[1] + spread[2]) / 3.0
    xx, yy, zz = (1.5 * temperature - 0.5 * s for s in spread)
    xy, xz, yz = (-0.5 * s for s in (spread_xy, spread_xz, spread_yz))
    adj_xx, adj_yy, adj_zz = yy * zz - yz * yz, xx * zz - xz * xz, xx * yy - xy * xy
    adj_xy, adj_xz, adj_yz = xz * yz - xy * zz, xy * yz - xz * yy, xy * xz - xx * yz
    determinant = xx * adj_xx + xy * adj_xy + xz * adj_xz
    inv = [a / determinant for a in (adj_xx, adj_yy, adj_zz, adj_xy, adj_xz, adj_yz)]
    pull = [
        inv[0] * drift[0] + inv[3] * drift[1] + inv[4] * drift[2],
        inv[3] * drift[0] + inv[1] * drift[1] + inv[5] * drift[2],
        inv[4] * drift[0] + inv[5] * drift[1] + inv[2] * drift[2],
    ]
    quadratic = drift[0] * pull[0] + drift[1] * pull[1] + drift[2] * pull[2]
    log_prefactor = (
        jnp.log(density)
        + (3.0 * math.log(6.0) - 1.5 * math.log(2.0 * math.pi))
        - 0.5 * jnp.log(determinant)
    )
    rows = [log_prefactor - 0.5 * quadratic]
    rows += [SPACING * p for p in pull]
    rows += [-0.5 * square * i for i in inv[:3]]
    rows += [-square * i for i in inv[3:]]
    fraction = 1.0 - jnp.exp(-RELAX_INCREMENT * density * jnp.sqrt(temperature))
    return [LOG2E * r for r in rows], fraction


def relax_kernel(dist, basis, out, held, relaxed, sums, factors, in_sems, out_sem):
    pieces = BLOCKS // PIECE

    def arrival(piece):
        rows = pl.ds(piece * PIECE, PIECE)
        return pltpu.make_async_copy(dist.at[rows], held.at[rows], in_sems.at[piece])

    for piece in range(pieces):
        arrival(piece).start()
    for piece in range(pieces):
        arrival(piece).wait()
        cells = held[pl.ds(piece * PIECE, PIECE)].astype(jnp.float32)
        cells = cells.reshape(PIECE * CELLS, TOTAL).astype(jnp.bfloat16)
        sums[:, pl.ds(piece * PIECE * CELLS, PIECE * CELLS)] = lax.dot_general(
            basis[0:16, :], cells, (((1,), (1,)), ((), ())), preferred_element_type=jnp.float32
        )

    rows, fraction = coefficients_of(sums[...])
    exact = [[], [], []]
    for row in rows:
        for part in range(3):
            near = row.astype(jnp.bfloat16).astype(jnp.float32)
            exact[part].append(near)
            row = row - near
    zero = jnp.zeros((6, BLOCKS * CELLS), jnp.float32)
    stacked = jnp.concatenate(
        exact[0]
        + [zero]
        + exact[1]
        + [zero]
        + exact[2]
        + [zero, fraction, jnp.zeros((79, BLOCKS * CELLS), jnp.float32)],
        axis=0,
    )
    factors[...] = stacked.T

    @pl.loop(0, BLOCKS // GROUP)
    def _(group):
        first = group * GROUP
        own = factors[pl.ds(pl.multiple_of(first * CELLS, GROUP * CELLS), GROUP * CELLS), :]
        left = own[:, :48].astype(jnp.bfloat16)
        fraction = jnp.broadcast_to(own[:, 48:49], (GROUP * CELLS, 128))
        for step in range(TOTAL // STEP):
            power = jnp.dot(
                left, basis[:, pl.ds(step * STEP, STEP)], preferred_element_type=jnp.float32
            )
            for tile in range(STEP // 128):
                place = lanes(step * (STEP // 128) + tile)
                gauss = jnp.exp2(power[:, tile * 128 : tile * 128 + 128])
                moved = held[pl.ds(first, GROUP), :, place].astype(jnp.float32)
                moved = moved.reshape(GROUP * CELLS, 128)
                mixed = moved + fraction * (gauss - moved)
                relaxed[pl.ds(first, GROUP), :, place] = mixed.reshape(
                    GROUP, CELLS, 128
                ).astype(jnp.bfloat16)
        rows = pl.ds(first, GROUP)
        pltpu.make_async_copy(relaxed.at[rows], out.at[rows], out_sem).start()

    pltpu.make_async_copy(relaxed, out, out_sem).wait()


VMEM = pl.BlockSpec(memory_space=pltpu.VMEM)
ANY = pl.BlockSpec(memory_space=pl.ANY)
WHOLE = (BLOCKS, CELLS, TOTAL)


def relax(dist):
    return pl.pallas_call(
        relax_kernel,
        out_shape=jax.ShapeDtypeStruct(WHOLE, jnp.bfloat16),
        in_specs=[ANY, VMEM],
        out_specs=ANY,
        scratch_shapes=[
            pltpu.VMEM(WHOLE, jnp.bfloat16),
            pltpu.VMEM(WHOLE, jnp.bfloat16),
            pltpu.VMEM((16, BLOCKS * CELLS), jnp.float32),
            pltpu.VMEM((BLOCKS * CELLS, 128), jnp.float32),
            pltpu.SemaphoreType.DMA((BLOCKS // PIECE,)),
            pltpu.SemaphoreType.DMA(()),
        ],
        compiler_params=pltpu.CompilerParams(vmem_limit_bytes=RELAX_VMEM),
        cost_estimate=pl.CostEstimate(
            flops=2 * BLOCKS * CELLS * TOTAL * 1500,
            bytes_accessed=4 * BLOCKS * CELLS * TOTAL,
            transcendentals=BLOCKS * CELLS * TOTAL,
        ),
        name="relax",
    )(dist, basis_rows())


def pack_kernel(asked, relaxed, send, held, row, target, row_sem, in_sems, out_sem):
    def arrival(piece):
        rows = pl.ds(piece * PIECE, PIECE)
        return pltpu.make_async_copy(relaxed.at[rows], held.at[rows], in_sems.at[piece])

    for piece in range(BLOCKS // PIECE):
        arrival(piece).start()
    device = lax.broadcasted_iota(jnp.int32, asked.shape, 0)
    slot = lax.broadcasted_iota(jnp.int32, asked.shape, 1)
    row[...] = jnp.broadcast_to(
        jnp.sum(jnp.where(asked[...] == slot, device, 0), axis=0, keepdims=True), row.shape
    )
    to_scalars = pltpu.make_async_copy(row, target, row_sem)
    to_scalars.start()
    to_scalars.wait()
    for piece in range(BLOCKS // PIECE):
        arrival(piece).wait()
        for block in range(piece * PIECE, piece * PIECE + PIECE):
            pltpu.make_async_copy(held.at[block], send.at[target[0, block]], out_sem).start()
    pltpu.make_async_copy(held, send.at[pl.ds(0, BLOCKS)], out_sem).wait()


def pack(asked, relaxed):
    devices = asked.shape[0]
    return pl.pallas_call(
        pack_kernel,
        out_shape=jax.ShapeDtypeStruct((devices, CELLS, TOTAL), jnp.bfloat16),
        in_specs=[VMEM, ANY],
        out_specs=ANY,
        scratch_shapes=[
            pltpu.VMEM(WHOLE, jnp.bfloat16),
            pltpu.VMEM((8, 128), jnp.int32),
            pltpu.SMEM((8, 128), jnp.int32),
            pltpu.SemaphoreType.DMA(()),
            pltpu.SemaphoreType.DMA((BLOCKS // PIECE,)),
            pltpu.SemaphoreType.DMA(()),
        ],
        compiler_params=pltpu.CompilerParams(vmem_limit_bytes=PACK_VMEM),
        cost_estimate=pl.CostEstimate(
            flops=0, bytes_accessed=4 * BLOCKS * CELLS * TOTAL, transcendentals=0
        ),
        name="pack",
    )(asked, relaxed)


def row_masks():
    row = lax.broadcasted_iota(jnp.int32, (CELLS, 128), 0)
    return row < 4, (row & 2) == 0, (row & 1) == 0


def swap(x, distance):
    if distance == 4:
        return pltpu.roll(x, 4, 0)
    row = lax.broadcasted_iota(jnp.int32, (CELLS, 128), 0)
    return jnp.take_along_axis(x, row ^ distance, axis=0)


PARTS = 4
FACES = (("y", 0), ("y", 1), ("x", 0), ("x", 1))
FACE = (12, CELLS, TOTAL // 2)


def face_block(axis, up, pair):
    if axis == "x":
        return (BX - 1) * SLAB * up + 2 * pair
    return pair // 3 * SLAB + up * (BY - 1) * BZ + pair % 3 * 2


def face_tiles(axis, up):
    return [t for t in range(TILES) if up == (t % 2 if axis == "y" else t // (TILES // 2))]


def faces_kernel(owner, arrived, mask, *rest):
    sent, (received, sems) = rest[: len(FACES)], rest[len(FACES) :]
    part = arrived.shape[0] // PARTS
    copies = [
        pltpu.make_async_copy(
            arrived.at[pl.ds(i * part, part)], received.at[pl.ds(i * part, part)], sems.at[i]
        )
        for i in range(PARTS)
    ]
    for copy in copies:
        copy.start()
    for copy in copies:
        copy.wait()
    low_x, low_y, _ = row_masks()
    for (axis, up), face in zip(FACES, sent):
        low, distance = (low_x, 4) if axis == "x" else (low_y, 2)

        @pl.loop(0, 12)
        def _(pair):
            block = face_block(axis, up, pair)
            sources = [owner[block + side] for side in range(2)]
            masks = [mask[block + side] for side in range(2)]
            for place, tile in enumerate(face_tiles(axis, up)):
                a, b = (
                    received[sources[side], :, lanes(tile)].astype(jnp.float32) * masks[side]
                    for side in range(2)
                )
                b = swap(b, distance)
                joined = jnp.where(low, b, a) if up else jnp.where(low, a, b)
                face[pair, :, lanes(place)] = joined.astype(jnp.bfloat16)


def faces(owner, received, mask):
    moved = 4 * math.prod(FACE)
    return pl.pallas_call(
        faces_kernel,
        out_shape=[jax.ShapeDtypeStruct(FACE, jnp.bfloat16) for _ in FACES]
        + [jax.ShapeDtypeStruct(received.shape, received.dtype)],
        in_specs=[pl.BlockSpec(memory_space=pltpu.SMEM), ANY, VMEM],
        out_specs=[VMEM] * (len(FACES) + 1),
        scratch_shapes=[pltpu.SemaphoreType.DMA((PARTS,))],
        compiler_params=pltpu.CompilerParams(vmem_limit_bytes=FACES_VMEM),
        cost_estimate=pl.CostEstimate(
            flops=8 * moved, bytes_accessed=4 * moved, transcendentals=0
        ),
        name="faces",
    )(owner, received, mask)


def speeds():
    lane = lax.broadcasted_iota(jnp.int32, (CELLS, 128), 1)
    speed_y = [
        SPACING * jnp.abs(2 * (lane // VS + 8 * odd) + 1 - VS).astype(jnp.float32)
        for odd in range(2)
    ]
    speed_z = SPACING * jnp.abs(2 * (lane % VS) + 1 - VS).astype(jnp.float32)
    return speed_y, speed_z, lane % VS >= VS // 2


def speed_x(tile):
    return SPACING * abs(2 * (tile // 2) + 1 - VS)


def advance_kernel(owner, received, mask, rate, partial, kept):
    low_x, low_y, low_z = row_masks()
    speed_y, speed_z, rising_z = speeds()
    from_below = rising_z & ~low_z
    from_above = ~rising_z & low_z
    nothing = jnp.zeros((CELLS, 128), jnp.float32)

    @pl.loop(0, BLOCKS)
    def _(block):
        source, own_mask = owner[block], mask[block]
        for tile in range(TILES):
            kept[block, :, lanes(tile)] = (
                received[source, :, lanes(tile)].astype(jnp.float32) * own_mask
            )

    kept[BLOCKS] = jnp.zeros((CELLS, TOTAL), jnp.float32)

    @pl.loop(0, BX * BY)
    def _(column):
        bx, by = column // BY, column % BY
        line = column * BZ
        outside = BLOCKS
        near_x = (
            [jnp.where(bx == BX - 1, outside, line + SLAB), jnp.where(bx == BX - 1, 0, 1)],
            [jnp.where(bx == 0, outside, line - SLAB), jnp.where(bx == 0, 0, 1)],
        )
        near_y = (
            [jnp.where(by == BY - 1, outside, line + BZ), jnp.where(by == BY - 1, 0, 1)],
            [jnp.where(by == 0, outside, line - BZ), jnp.where(by == 0, 0, 1)],
        )
        for tile in range(TILES):
            x, y = tile // (TILES // 2), tile % 2
            own_line = [kept[line + bz, :, lanes(tile)] for bz in range(BZ)]
            for bz in range(BZ):
                own = own_line[bz]
                below = own_line[bz - 1] if bz else nothing
                above = own_line[bz + 1] if bz < BZ - 1 else nothing
                start, stride = near_x[x]
                other = kept[start + stride * bz, :, lanes(tile)]
                from_x = swap(
                    jnp.where(low_x, own, other) if x else jnp.where(low_x, other, own), 4
                )
                start, stride = near_y[y]
                other = kept[start + stride * bz, :, lanes(tile)]
                from_y = swap(
                    jnp.where(low_y, own, other) if y else jnp.where(low_y, other, own), 2
                )
                from_z = swap(
                    jnp.where(from_below, below, jnp.where(from_above, above, own)), 1
                )
                flux = (
                    speed_x(tile) * (own - from_x)
                    + speed_y[y] * (own - from_y)
                    + speed_z * (own - from_z)
                )
                partial[line + bz, :, lanes(tile)] = own - rate[line + bz] * flux


def advance(owner, received, mask, rate):
    return pl.pallas_call(
        advance_kernel,
        out_shape=jax.ShapeDtypeStruct(WHOLE, jnp.float32),
        in_specs=[pl.BlockSpec(memory_space=pltpu.SMEM)] + [VMEM] * 3,
        out_specs=VMEM,
        scratch_shapes=[pltpu.VMEM((BLOCKS + 1, CELLS, TOTAL), jnp.float32)],
        compiler_params=pltpu.CompilerParams(vmem_limit_bytes=ADVANCE_VMEM),
        cost_estimate=pl.CostEstimate(
            flops=100 * math.prod(WHOLE), bytes_accessed=6 * math.prod(WHOLE), transcendentals=0
        ),
        name="advance",
    )(owner, received, mask, rate)


def edge_kernel(partial, rate, down_y, up_y, down_x, up_x, out, made, sems):
    low_x, low_y, _ = row_masks()
    speed_y, _, _ = speeds()

    def add(halo, axis, up, slots):
        low, distance = (low_x, 4) if axis == "x" else (low_y, 2)
        edge = ~low if up else low

        @pl.loop(*slots)
        def _(pair):
            block = face_block(axis, 1 - up, pair)
            for place, tile in enumerate(face_tiles(axis, up)):
                face = halo[pair, :, lanes(place)].astype(jnp.float32)
                speed = speed_x(tile) if axis == "x" else speed_y[up]
                other = swap(face, distance)
                near = (jnp.where(edge, face, 0.0), jnp.where(edge, other, 0.0))
                for side in range(2):
                    gain = rate[block + side] * (speed * swap(near[side], distance))
                    partial_at = (block + side, slice(None), lanes(tile))
                    partial[partial_at] = partial[partial_at] + gain

    def result_copy(bx):
        rows = pl.ds(bx * SLAB, SLAB)
        return pltpu.make_async_copy(made.at[rows], out.at[rows], sems.at[bx])

    for bx in range(BX):
        if bx == 0:
            add(up_x, "x", 1, (0, 12))
        if bx == BX - 1:
            add(down_x, "x", 0, (0, 12))
        add(down_y, "y", 0, (3 * bx, 3 * bx + 3))
        add(up_y, "y", 1, (3 * bx, 3 * bx + 3))

        @pl.loop(bx * SLAB, bx * SLAB + SLAB)
        def _(block):
            made[block] = partial[block].astype(jnp.bfloat16)

        result_copy(bx).start()
    for bx in range(BX):
        result_copy(bx).wait()


def edge(partial, rate, halos):
    return pl.pallas_call(
        edge_kernel,
        out_shape=jax.ShapeDtypeStruct(WHOLE, jnp.bfloat16),
        in_specs=[VMEM] * 6,
        out_specs=ANY,
        scratch_shapes=[pltpu.VMEM(WHOLE, jnp.bfloat16), pltpu.SemaphoreType.DMA((BX,))],
        compiler_params=pltpu.CompilerParams(vmem_limit_bytes=EDGE_VMEM),
        cost_estimate=pl.CostEstimate(
            flops=4 * math.prod(WHOLE), bytes_accessed=6 * math.prod(WHOLE), transcendentals=0
        ),
        name="edge",
    )(partial, rate, *halos)


def after(received, source_owner, levels, active):
    n_gx, n_gy = lax.axis_size("gx"), lax.axis_size("gy")
    mask = jnp.broadcast_to(
        active.astype(jnp.float32)[:, :, None], (BLOCKS, CELLS, 128)
    )
    courant = COURANT * jnp.exp2(levels.astype(jnp.float32))
    rate = mask * courant[:, None, None]

    def up(n):
        return [(i, i + 1) for i in range(n - 1)]

    def down(n):
        return [(i + 1, i) for i in range(n - 1)]

    *sent, received = faces(source_owner, received, mask)
    halos = []
    for (axis, to_above), face in zip(FACES, sent):
        name, n = ("gx", n_gx) if axis == "x" else ("gy", n_gy)
        halos.append(lax.ppermute(face, name, up(n) if to_above else down(n)))
    return edge(advance(source_owner, received, mask, rate), rate, halos)


def per_device(dist_old, source_owner, levels, active):
    axes = ("gx", "gy")
    devices = lax.axis_size("gx") * lax.axis_size("gy")
    owners = lax.broadcasted_iota(jnp.int32, (devices, BLOCKS), 0)
    slots = lax.broadcasted_iota(jnp.int32, (devices, BLOCKS), 1)
    request = BLOCKS + jnp.sum(
        jnp.where(source_owner[None, :] == owners, slots - BLOCKS, 0), axis=1, keepdims=True
    )
    asked = lax.all_to_all(
        jnp.broadcast_to(request, (devices, 128)), axes, split_axis=0, concat_axis=0, tiled=True
    )
    send = pack(asked, relax(dist_old))
    received = lax.all_to_all(send, axes, split_axis=0, concat_axis=0, tiled=True)
    return after(received, source_owner, levels, active)


def solution(mesh):
    return jax.shard_map(
        per_device,
        mesh=mesh,
        in_specs=(
            P(("gx", "gy"), None, None),
            P(("gx", "gy")),
            P(("gx", "gy")),
            P(("gx", "gy"), None),
        ),
        out_specs=P(("gx", "gy"), None, None),
        check_vma=False,
    )
```

time: 334 us -> 173 us (0.52)
  Pallas kernels: 230 us -> 36.1 us
  waiting for transfers between devices: 47.3 us -> 102 us
  starting transfers between devices: 49.9 us -> 32.4 us
    pallas_call x2 -> x1, Pallas kernels: 194 us -> 6.25 us  [pack(): pl.pallas_call(pack_kernel, out_shape=jax.ShapeDtypeStruct((devices, CELL...]
    all_to_all x3 -> x2, waiting for transfers between devices: 24.9 us -> 102 us  [the longest x1 102 us: per_device(): lax.all_to_all(send, axes, split_axis=0, concat_axis=0, tiled=True)]
    ppermute x7 -> x4, waiting for transfers between devices: 22.3 us -> 0.01 us  [after(): halos.append(lax.ppermute(face, name, up(n) if to_above else down(n)))]
    ppermute x7 -> x4, starting transfers between devices: 21.2 us -> 11.5 us  [after(): halos.append(lax.ppermute(face, name, up(n) if to_above else down(n)))]
    all_to_all x3 -> x2, starting transfers between devices: 28.7 us -> 21 us  [the longest x1 10.8 us: per_device(): lax.all_to_all(jnp.broadcast_to(request, (devices, 128)), axes, split_axi...]
    pallas_call x5 -> x4, Pallas kernels: 36.1 us -> 29.8 us  [the longest x1 11.5 us: relax(): pl.pallas_call(relax_kernel, out_shape=jax.ShapeDtypeStruct(WHOLE, jnp.bf...]
  transfers between devices with their start and end apart: 10 -> 6, of which waited for: 6 -> 1; matrix products, arithmetic and copies ran while one was open for 0% -> 0% of each run, Pallas kernels for 23% -> 12%
where the time goes in v3:
time: 173 us
  waiting for transfers between devices  102 us (59%)
  Pallas kernels  36.1 us (21%)
  starting transfers between devices  32.4 us (19%)
    all_to_all x1, waiting for transfers between devices, per_device(): lax.all_to_all(send, axes, split_axis=0, concat_axis=0, tiled=True)  102 us
    ppermute x4, starting transfers between devices, after(): halos.append(lax.ppermute(face, name, up(n) if to_above else down(n)))  11.5 us
    pallas_call x1, Pallas kernels, relax(): pl.pallas_call(relax_kernel, out_shape=jax.ShapeDtypeStruct(WHOLE, jnp.bf...  11.5 us
    all_to_all x1, starting transfers between devices, per_device(): lax.all_to_all(jnp.broadcast_to(request, (devices, 128)), axes, split_axi...  10.8 us
    all_to_all x1, starting transfers between devices, per_device(): lax.all_to_all(send, axes, split_axis=0, concat_axis=0, tiled=True)  10.2 us
    pallas_call x1, Pallas kernels, advance(): pl.pallas_call(advance_kernel, out_shape=jax.ShapeDtypeStruct(WHOLE, jnp....  9.16 us
    pallas_call x1, Pallas kernels, pack(): pl.pallas_call(pack_kernel, out_shape=jax.ShapeDtypeStruct((devices, CELL...  6.25 us
    pallas_call x1, Pallas kernels, faces(): pl.pallas_call(faces_kernel, out_shape=[jax.ShapeDtypeStruct(FACE, jnp.bf...  5.4 us
  transfers between devices with their start and end apart: 6, of which 1 were waited for; matrix products, arithmetic and copies ran while one was open for 0% of the time, Pallas kernels for 12%

profile of v3, /device:TPU:7, one launch (start us, length us, event | category | flops | bytes accessed | tf_op | source)
XLA Modules:
  0.0 173.1 jit_solution(17199275154225526907)
XLA Ops:
  0.0 0.8 select_reduce_fusion
  0.8 0.8 broadcast_in_dim.9
  1.6 10.8 %all-to-all-start = ((s32[128,1,128]{2,1,0:T(1,128)}), s32[128,1,128]{2,1,0:T(1,128)S(1)}, u32[]{:S(2)}, u32[]{:S(2)}) async-start(s32[128,1,128]{2,1,0:T(1,128)} %broadcast_in_dim.9), calls=%async_computation | async-start | bytes 131072 | tf_op jit(solution)/shard_map/all_to_all | solution.py:469
  12.4 11.5 %relax.1.relaxed = bf16[96,8,4096]{2,1,0:T(8,128)(2,1)} custom-call(bf16[96,8,4096]{2,1,0:T(8,128)(2,1)} %dist.1, bf16[48,4096]{1,0:T(8,128)(2,1)} %constant.13.clone.basis), custom_call_target="tpu_custom_call" | custom-call | flops 9437184000 | bytes 12582912 | tf_op jit(solution)/shard_map/relax/pallas_call | solution.py:151
  23.9 0.6 copy-done.1
  24.5 6.3 %pack.1 = bf16[128,8,4096]{2,1,0:T(8,128)(2,1)} custom-call(s32[128,128]{1,0:T(8,128)} %bitcast.1, bf16[96,8,4096]{2,1,0:T(8,128)(2,1)} %relax.1.relaxed), custom_call_target="tpu_custom_call" | custom-call | bytes 12582912 | tf_op jit(solution)/shard_map/pack/pallas_call | solution.py:198
  30.8 0.0 copy-start.2
  30.8 0.0 copy-start
  30.8 10.2 %all-to-all-start.1 = ((bf16[128,8,4096]{2,1,0:T(8,128)(2,1)}), bf16[128,8,4096]{2,1,0:T(8,128)(2,1)}, u32[]{:S(2)}, u32[]{:S(2)}) async-start(bf16[128,8,4096]{2,1,0:T(8,128)(2,1)} %pack.1), calls=%async_computation.1 | async-start | bytes 16777216 | tf_op jit(solution)/shard_map/all_to_all | solution.py:473
  41.0 0.0 copy-start.3
  41.0 0.1 copy.8
  41.1 101.6 %all-to-all-done.1.arrived = bf16[128,8,4096]{2,1,0:T(8,128)(2,1)} async-done(((bf16[128,8,4096]{2,1,0:T(8,128)(2,1)}), bf16[128,8,4096]{2,1,0:T(8,128)(2,1)}, u32[]{:S(2)}, u32[]{:S(2)}) %all-to-all-start.1) | async-done | bytes 8388640 | tf_op jit(solution)/shard_map/all_to_all | solution.py:473
  142.7 0.2 broadcast_in_dim.10.mask
  142.8 5.4 %faces.1 = (bf16[12,8,2048]{2,1,0:T(8,128)(2,1)S(1)}, bf16[12,8,2048]{2,1,0:T(8,128)(2,1)S(1)}, bf16[12,8,2048]{2,1,0:T(8,128)(2,1)S(1)}, bf16[12,8,2048]{2,1,0:T(8,128)(2,1)S(1)}, bf16[128,8,4096]{2,1,0:T(8,128)(2,1)S(1)}) custom-call(s32[96]{0:T(128)S(1)} %copy-done, bf16[128,8,4096]{2,1,0:T(8,128)(2,1)} %all-to-all-done.1.arrived, ...), custom_call_target="tpu_custom_call" | custom-call | flops 6291456 | bytes 3145728 | tf_op jit(solution)/shard_map/faces/pallas_call | solution.py:280
  148.3 1.9 %collective-permute-start = (bf16[12,8,2048]{2,1,0:T(8,128)(2,1)S(1)}, bf16[12,8,2048]{2,1,0:T(8,128)(2,1)S(1)}, u32[]{:S(2)}, u32[]{:S(2)}) collective-permute-start(bf16[12,8,2048]{2,1,0:T(8,128)(2,1)S(1)} %get-tuple-element.11), channel_id=1, source_target_pairs={{1,0},{2,1},{3,2},{4,3},{5,4},{6,5},{7,6},{8,7},{9,8},{10,9},{11,1... | collective-permute-start | bytes 1179656 | tf_op jit(solution)/shard_map/ppermute | solution.py:457
  150.2 3.5 %collective-permute-start.1 = (bf16[12,8,2048]{2,1,0:T(8,128)(2,1)S(1)}, bf16[12,8,2048]{2,1,0:T(8,128)(2,1)S(1)}, u32[]{:S(2)}, u32[]{:S(2)}) collective-permute-start(bf16[12,8,2048]{2,1,0:T(8,128)(2,1)S(1)} %get-tuple-element.12), channel_id=1, source_target_pairs={{0,1},{1,2},{2,3},{3,4},{4,5},{5,6},{6,7},{7,8},{8,9},{9,10},{10,1... | collective-permute-start | bytes 1179656 | tf_op jit(solution)/shard_map/ppermute | solution.py:457
  153.7 3.3 %collective-permute-start.2 = (bf16[12,8,2048]{2,1,0:T(8,128)(2,1)S(1)}, bf16[12,8,2048]{2,1,0:T(8,128)(2,1)S(1)}, u32[]{:S(2)}, u32[]{:S(2)}) collective-permute-start(bf16[12,8,2048]{2,1,0:T(8,128)(2,1)S(1)} %get-tuple-element.13), channel_id=1, source_target_pairs={{16,0},{32,16},{48,32},{64,48},{80,64},{96,80},{112,96},{17,1},{33... | collective-permute-start | bytes 1179656 | tf_op jit(solution)/shard_map/ppermute | solution.py:457
  157.0 2.7 %collective-permute-start.3 = (bf16[12,8,2048]{2,1,0:T(8,128)(2,1)S(1)}, bf16[12,8,2048]{2,1,0:T(8,128)(2,1)S(1)}, u32[]{:S(2)}, u32[]{:S(2)}) collective-permute-start(bf16[12,8,2048]{2,1,0:T(8,128)(2,1)S(1)} %get-tuple-element.14), channel_id=1, source_target_pairs={{0,16},{16,32},{32,48},{48,64},{64,80},{80,96},{96,112},{1,17},{17... | collective-permute-start | bytes 1179656 | tf_op jit(solution)/shard_map/ppermute | solution.py:457
  159.8 0.3 broadcast_multiply_fusion.rate
  160.1 9.2 %advance.1.partial = f32[96,8,4096]{2,1,0:T(8,128)S(1)} custom-call(s32[96]{0:T(128)S(1)} %copy-done, bf16[128,8,4096]{2,1,0:T(8,128)(2,1)S(1)} %get-tuple-element.10.received, f32[96,8,128]{2,1,0:T(8,128)S(1)} %broadcast_in_dim.10.mask, f32[96,8,128]{2,1,0:T(8,128)S(1)} %broadcast_multiply_fusion.rate), custom_call_target="tpu_custom_call" | custom-call | flops 314572800 | bytes 18874368 | tf_op jit(solution)/shard_map/advance/pallas_call | solution.py:368
  169.2 0.0 collective-permute-done.down_y
  169.2 0.0 collective-permute-done.2.down_x
  169.2 0.0 collective-permute-done.3.up_x
  169.3 3.8 %edge.1 = bf16[96,8,4096]{2,1,0:T(8,128)(2,1)} custom-call(f32[96,8,4096]{2,1,0:T(8,128)S(1)} %advance.1.partial, f32[96,8,128]{2,1,0:T(8,128)S(1)} %broadcast_multiply_fusion.rate, bf16[12,8,2048]{2,1,0:T(8,128)(2,1)S(1)} %collective-permute-done.down_y, bf16[12,8,2048]{2,1,0:T(8,128)(2,1)S(1)} %collective-permute-done.1.up_y, ...), custom_call_target="tpu_custom_call" | custom-call | flops 12582912 | bytes 18874368 | tf_op jit(solution)/shard_map/edge/pallas_call | solution.py:425
  (10 shorter events, 0.0 us)
Async XLA Ops:
  1.6 22.3 %all-to-all-start = ((s32[128,1,128]{2,1,0:T(1,128)}), s32[128,1,128]{2,1,0:T(1,128)S(1)}, u32[]{:S(2)}, u32[]{:S(2)}) async-start(s32[128,1,128]{2,1,0:T(1,128)} %broadcast_in_dim.9), calls=%async_computation | async-start | bytes 131072 | tf_op jit(solution)/shard_map/all_to_all | solution.py:469
  23.9 0.6 copy-start.1
  30.8 10.2 %copy-start.2 = (s32[96,8]{0,1:T(8,128)S(1)}, s32[96,8]{0,1:T(8,128)}, u32[]{:S(2)}) copy-start(s32[96,8]{0,1:T(8,128)} %param.8) | copy-start | bytes 9220
  30.8 112.1 %copy-start = (s32[96]{0:T(128)S(1)}, s32[96]{0:T(128)}, u32[]{:S(2)}) copy-start(s32[96]{0:T(128)} %owner.3) | copy-start | bytes 1156
  30.8 111.9 %all-to-all-start.1 = ((bf16[128,8,4096]{2,1,0:T(8,128)(2,1)}), bf16[128,8,4096]{2,1,0:T(8,128)(2,1)}, u32[]{:S(2)}, u32[]{:S(2)}) async-start(bf16[128,8,4096]{2,1,0:T(8,128)(2,1)} %pack.1), calls=%async_computation.1 | async-start | bytes 16777216 | tf_op jit(solution)/shard_map/all_to_all | solution.py:473
  41.0 118.8 %copy-start.3 = (s32[96]{0:T(128)S(1)}, s32[96]{0:T(128)}, u32[]{:S(2)}) copy-start(s32[96]{0:T(128)} %param.7) | copy-start | bytes 1156
  148.3 21.0 %collective-permute-start = (bf16[12,8,2048]{2,1,0:T(8,128)(2,1)S(1)}, bf16[12,8,2048]{2,1,0:T(8,128)(2,1)S(1)}, u32[]{:S(2)}, u32[]{:S(2)}) collective-permute-start(bf16[12,8,2048]{2,1,0:T(8,128)(2,1)S(1)} %get-tuple-element.11), channel_id=1, source_target_pairs={{1,0},{2,1},{3,2},{4,3},{5,4},{6,5},{7,6},{8,7},{9,8},{10,9},{11,1... | collective-permute-start | bytes 1179656 | tf_op jit(solution)/shard_map/ppermute | solution.py:457
  150.2 19.0 %collective-permute-start.1 = (bf16[12,8,2048]{2,1,0:T(8,128)(2,1)S(1)}, bf16[12,8,2048]{2,1,0:T(8,128)(2,1)S(1)}, u32[]{:S(2)}, u32[]{:S(2)}) collective-permute-start(bf16[12,8,2048]{2,1,0:T(8,128)(2,1)S(1)} %get-tuple-element.12), channel_id=1, source_target_pairs={{0,1},{1,2},{2,3},{3,4},{4,5},{5,6},{6,7},{7,8},{8,9},{9,10},{10,1... | collective-permute-start | bytes 1179656 | tf_op jit(solution)/shard_map/ppermute | solution.py:457
  153.7 15.5 %collective-permute-start.2 = (bf16[12,8,2048]{2,1,0:T(8,128)(2,1)S(1)}, bf16[12,8,2048]{2,1,0:T(8,128)(2,1)S(1)}, u32[]{:S(2)}, u32[]{:S(2)}) collective-permute-start(bf16[12,8,2048]{2,1,0:T(8,128)(2,1)S(1)} %get-tuple-element.13), channel_id=1, source_target_pairs={{16,0},{32,16},{48,32},{64,48},{80,64},{96,80},{112,96},{17,1},{33... | collective-permute-start | bytes 1179656 | tf_op jit(solution)/shard_map/ppermute | solution.py:457
  157.0 12.2 %collective-permute-start.3 = (bf16[12,8,2048]{2,1,0:T(8,128)(2,1)S(1)}, bf16[12,8,2048]{2,1,0:T(8,128)(2,1)S(1)}, u32[]{:S(2)}, u32[]{:S(2)}) collective-permute-start(bf16[12,8,2048]{2,1,0:T(8,128)(2,1)S(1)} %get-tuple-element.14), channel_id=1, source_target_pairs={{0,16},{16,32},{32,48},{48,64},{64,80},{80,96},{96,112},{1,17},{17... | collective-permute-start | bytes 1179656 | tf_op jit(solution)/shard_map/ppermute | solution.py:457

commit v4 on v3

--- a/solution.py
+++ b/solution.py
@@ -21,6 +21,8 @@
 LOG2E = 1.0 / math.log(2.0)
 
 TILES = TOTAL // 128
+LATE = tuple(range(TILES // 2 + 1, TILES, 2))
+CHUNKS = (tuple(t for t in range(TILES) if t not in LATE), LATE)
 PIECE = 16
 RELAX_VMEM = 60 << 20
 PACK_VMEM = 54 << 20
@@ -29,6 +31,20 @@
 EDGE_VMEM = 20 << 20
 GROUP = 8
 STEP = 512
+
+
+def runs_of(chunk):
+    runs = []
+    for place, tile in enumerate(CHUNKS[chunk]):
+        if runs and runs[-1][1] + runs[-1][2] == tile:
+            runs[-1][2] += 1
+        else:
+            runs.append([place, tile, 1])
+    return runs
+
+
+def shape_of(chunk, rows=BLOCKS):
+    return (rows, CELLS, 128 * len(CHUNKS[chunk]))
 
 
 def lanes(tile):
@@ -81,7 +97,9 @@
     return [LOG2E * r for r in rows], fraction
 
 
-def relax_kernel(dist, basis, out, held, relaxed, sums, factors, in_sems, out_sem):
+def relax_kernel(dist, basis, *rest):
+    outs, relaxed = rest[: len(CHUNKS)], rest[len(CHUNKS) : 2 * len(CHUNKS)]
+    held, sums, factors, in_sems, out_sems = rest[2 * len(CHUNKS) :]
     pieces = BLOCKS // PIECE
 
     def arrival(piece):
@@ -128,18 +146,21 @@
                 left, basis[:, pl.ds(step * STEP, STEP)], preferred_element_type=jnp.float32
             )
             for tile in range(STEP // 128):
-                place = lanes(step * (STEP // 128) + tile)
+                whole = step * (STEP // 128) + tile
+                late = int(whole in LATE)
                 gauss = jnp.exp2(power[:, tile * 128 : tile * 128 + 128])
-                moved = held[pl.ds(first, GROUP), :, place].astype(jnp.float32)
+                moved = held[pl.ds(first, GROUP), :, lanes(whole)].astype(jnp.float32)
                 moved = moved.reshape(GROUP * CELLS, 128)
                 mixed = moved + fraction * (gauss - moved)
-                relaxed[pl.ds(first, GROUP), :, place] = mixed.reshape(
-                    GROUP, CELLS, 128
-                ).astype(jnp.bfloat16)
+                relaxed[late][pl.ds(first, GROUP), :, lanes(CHUNKS[late].index(whole))] = (
+                    mixed.reshape(GROUP, CELLS, 128).astype(jnp.bfloat16)
+                )
         rows = pl.ds(first, GROUP)
-        pltpu.make_async_copy(relaxed.at[rows], out.at[rows], out_sem).start()
-
-    pltpu.make_async_copy(relaxed, out, out_sem).wait()
+        for made, out, sem in zip(relaxed, outs, range(len(CHUNKS))):
+            pltpu.make_async_copy(made.at[rows], out.at[rows], out_sems.at[sem]).start()
+
+    for made, out, sem in zip(relaxed, outs, range(len(CHUNKS))):
+        pltpu.make_async_copy(made, out, out_sems.at[sem]).wait()
 
 
 VMEM = pl.BlockSpec(memory_space=pltpu.VMEM)
@@ -150,16 +171,16 @@
 def relax(dist):
     return pl.pallas_call(
         relax_kernel,
-        out_shape=jax.ShapeDtypeStruct(WHOLE, jnp.bfloat16),
+        out_shape=[jax.ShapeDtypeStruct(shape_of(c), jnp.bfloat16) for c in range(len(CHUNKS))],
         in_specs=[ANY, VMEM],
-        out_specs=ANY,
-        scratch_shapes=[
-            pltpu.VMEM(WHOLE, jnp.bfloat16),
+        out_specs=[ANY] * len(CHUNKS),
+        scratch_shapes=[pltpu.VMEM(shape_of(c), jnp.bfloat16) for c in range(len(CHUNKS))]
+        + [
             pltpu.VMEM(WHOLE, jnp.bfloat16),
             pltpu.VMEM((16, BLOCKS * CELLS), jnp.float32),
             pltpu.VMEM((BLOCKS * CELLS, 128), jnp.float32),
             pltpu.SemaphoreType.DMA((BLOCKS // PIECE,)),
-            pltpu.SemaphoreType.DMA(()),
+            pltpu.SemaphoreType.DMA((len(CHUNKS),)),
         ],
         compiler_params=pltpu.CompilerParams(vmem_limit_bytes=RELAX_VMEM),
         cost_estimate=pl.CostEstimate(
@@ -193,15 +214,15 @@
     pltpu.make_async_copy(held, send.at[pl.ds(0, BLOCKS)], out_sem).wait()
 
 
-def pack(asked, relaxed):
+def pack(chunk, asked, relaxed):
     devices = asked.shape[0]
     return pl.pallas_call(
         pack_kernel,
-        out_shape=jax.ShapeDtypeStruct((devices, CELLS, TOTAL), jnp.bfloat16),
+        out_shape=jax.ShapeDtypeStruct(shape_of(chunk, devices), jnp.bfloat16),
         in_specs=[VMEM, ANY],
         out_specs=ANY,
         scratch_shapes=[
-            pltpu.VMEM(WHOLE, jnp.bfloat16),
+            pltpu.VMEM(shape_of(chunk), jnp.bfloat16),
             pltpu.VMEM((8, 128), jnp.int32),
             pltpu.SMEM((8, 128), jnp.int32),
             pltpu.SemaphoreType.DMA(()),
@@ -210,9 +231,9 @@
         ],
         compiler_params=pltpu.CompilerParams(vmem_limit_bytes=PACK_VMEM),
         cost_estimate=pl.CostEstimate(
-            flops=0, bytes_accessed=4 * BLOCKS * CELLS * TOTAL, transcendentals=0
+            flops=0, bytes_accessed=4 * math.prod(shape_of(chunk)), transcendentals=0
         ),
-        name="pack",
+        name=f"pack{chunk}",
     )(asked, relaxed)
 
 
@@ -229,8 +250,15 @@
 
 
 PARTS = 4
-FACES = (("y", 0), ("y", 1), ("x", 0), ("x", 1))
-FACE = (12, CELLS, TOTAL // 2)
+
+
+def face_kinds(chunk):
+    kinds = (("y", 1), ("x", 1), ("y", 0), ("x", 0))
+    return [kind for kind in kinds if face_tiles(chunk, *kind)]
+
+
+def face_shape(chunk, kind):
+    return (12, CELLS, 128 * len(face_tiles(chunk, *kind)))
 
 
 def face_block(axis, up, pair):
@@ -239,12 +267,39 @@
     return pair // 3 * SLAB + up * (BY - 1) * BZ + pair % 3 * 2
 
 
-def face_tiles(axis, up):
-    return [t for t in range(TILES) if up == (t % 2 if axis == "y" else t // (TILES // 2))]
-
-
-def faces_kernel(owner, arrived, mask, *rest):
-    sent, (received, sems) = rest[: len(FACES)], rest[len(FACES) :]
+def face_tiles(chunk, axis, up):
+    return [
+        (place, tile)
+        for place, tile in enumerate(CHUNKS[chunk])
+        if up == (tile % 2 if axis == "y" else tile // (TILES // 2))
+    ]
+
+
+def write_faces(chunk, owner, received, mask, sent):
+    low_x, low_y, _ = row_masks()
+    for (axis, up), face in zip(face_kinds(chunk), sent):
+        low, distance = (low_x, 4) if axis == "x" else (low_y, 2)
+
+        @pl.loop(0, 12)
+        def _(pair):
+            block = face_block(axis, up, pair)
+            sources = [owner[block + side] for side in range(2)]
+            masks = [mask[block + side] for side in range(2)]
+            for n, (place, _) in enumerate(face_tiles(chunk, axis, up)):
+                a, b = (
+                    received[sources[side], :, lanes(place)].astype(jnp.float32) * masks[side]
+                    for side in range(2)
+                )
+                b = swap(b, distance)
+                joined = jnp.where(low, b, a) if up else jnp.where(low, a, b)
+                face[pair, :, lanes(n)] = joined.astype(jnp.bfloat16)
+
+
+def faces_kernel(chunk, owner, arrived, mask, *rest):
+    if chunk:
+        write_faces(chunk, owner, arrived, mask, rest)
+        return
+    *sent, received, sems = rest
     part = arrived.shape[0] // PARTS
     copies = [
         pltpu.make_async_copy(
@@ -256,40 +311,28 @@
         copy.start()
     for copy in copies:
         copy.wait()
-    low_x, low_y, _ = row_masks()
-    for (axis, up), face in zip(FACES, sent):
-        low, distance = (low_x, 4) if axis == "x" else (low_y, 2)
-
-        @pl.loop(0, 12)
-        def _(pair):
-            block = face_block(axis, up, pair)
-            sources = [owner[block + side] for side in range(2)]
-            masks = [mask[block + side] for side in range(2)]
-            for place, tile in enumerate(face_tiles(axis, up)):
-                a, b = (
-                    received[sources[side], :, lanes(tile)].astype(jnp.float32) * masks[side]
-                    for side in range(2)
-                )
-                b = swap(b, distance)
-                joined = jnp.where(low, b, a) if up else jnp.where(low, a, b)
-                face[pair, :, lanes(place)] = joined.astype(jnp.bfloat16)
-
-
-def faces(owner, received, mask):
-    moved = 4 * math.prod(FACE)
-    return pl.pallas_call(
-        faces_kernel,
-        out_shape=[jax.ShapeDtypeStruct(FACE, jnp.bfloat16) for _ in FACES]
-        + [jax.ShapeDtypeStruct(received.shape, received.dtype)],
-        in_specs=[pl.BlockSpec(memory_space=pltpu.SMEM), ANY, VMEM],
-        out_specs=[VMEM] * (len(FACES) + 1),
-        scratch_shapes=[pltpu.SemaphoreType.DMA((PARTS,))],
+    write_faces(chunk, owner, received, mask, sent)
+
+
+def faces(chunk, owner, arrived, mask):
+    kinds = face_kinds(chunk)
+    shapes = [jax.ShapeDtypeStruct(face_shape(chunk, kind), jnp.bfloat16) for kind in kinds]
+    moved = sum(math.prod(s.shape) for s in shapes)
+    if chunk == 0:
+        shapes.append(jax.ShapeDtypeStruct(arrived.shape, arrived.dtype))
+    made = pl.pallas_call(
+        lambda *refs: faces_kernel(chunk, *refs),
+        out_shape=shapes,
+        in_specs=[pl.BlockSpec(memory_space=pltpu.SMEM), VMEM if chunk else ANY, VMEM],
+        out_specs=[VMEM] * len(shapes),
+        scratch_shapes=[] if chunk else [pltpu.SemaphoreType.DMA((PARTS,))],
         compiler_params=pltpu.CompilerParams(vmem_limit_bytes=FACES_VMEM),
         cost_estimate=pl.CostEstimate(
             flops=8 * moved, bytes_accessed=4 * moved, transcendentals=0
         ),
-        name="faces",
-    )(owner, received, mask)
+        name=f"faces{chunk}",
+    )(owner, arrived, mask)
+    return made[: len(kinds)], arrived if chunk else made[-1]
 
 
 def speeds():
@@ -306,7 +349,7 @@
     return SPACING * abs(2 * (tile // 2) + 1 - VS)
 
 
-def advance_kernel(owner, received, mask, rate, partial, kept):
+def advance_kernel(chunk, owner, received, mask, rate, partial, kept):
     low_x, low_y, low_z = row_masks()
     speed_y, speed_z, rising_z = speeds()
     from_below = rising_z & ~low_z
@@ -316,12 +359,12 @@
     @pl.loop(0, BLOCKS)
     def _(block):
         source, own_mask = owner[block], mask[block]
-        for tile in range(TILES):
-            kept[block, :, lanes(tile)] = (
-                received[source, :, lanes(tile)].astype(jnp.float32) * own_mask
+        for place in range(len(CHUNKS[chunk])):
+            kept[block, :, lanes(place)] = (
+                received[source, :, lanes(place)].astype(jnp.float32) * own_mask
             )
 
-    kept[BLOCKS] = jnp.zeros((CELLS, TOTAL), jnp.float32)
+    kept[BLOCKS] = jnp.zeros(shape_of(chunk)[1:], jnp.float32)
 
     @pl.loop(0, BX * BY)
     def _(column):
@@ -336,20 +379,20 @@
             [jnp.where(by == BY - 1, outside, line + BZ), jnp.where(by == BY - 1, 0, 1)],
             [jnp.where(by == 0, outside, line - BZ), jnp.where(by == 0, 0, 1)],
         )
-        for tile in range(TILES):
+        for place, tile in enumerate(CHUNKS[chunk]):
             x, y = tile // (TILES // 2), tile % 2
-            own_line = [kept[line + bz, :, lanes(tile)] for bz in range(BZ)]
+            own_line = [kept[line + bz, :, lanes(place)] for bz in range(BZ)]
             for bz in range(BZ):
                 own = own_line[bz]
                 below = own_line[bz - 1] if bz else nothing
                 above = own_line[bz + 1] if bz < BZ - 1 else nothing
                 start, stride = near_x[x]
-                other = kept[start + stride * bz, :, lanes(tile)]
+                other = kept[start + stride * bz, :, lanes(place)]
                 from_x = swap(
                     jnp.where(low_x, own, other) if x else jnp.where(low_x, other, own), 4
                 )
                 start, stride = near_y[y]
-                other = kept[start + stride * bz, :, lanes(tile)]
+                other = kept[start + stride * bz, :, lanes(place)]
                 from_y = swap(
                     jnp.where(low_y, own, other) if y else jnp.where(low_y, other, own), 2
                 )
@@ -361,79 +404,101 @@
                     + speed_y[y] * (own - from_y)
                     + speed_z * (own - from_z)
                 )
-                partial[line + bz, :, lanes(tile)] = own - rate[line + bz] * flux
-
-
-def advance(owner, received, mask, rate):
+                partial[line + bz, :, lanes(place)] = own - rate[line + bz] * flux
+
+
+def advance(chunk, owner, received, mask, rate):
+    shape = shape_of(chunk)
     return pl.pallas_call(
-        advance_kernel,
-        out_shape=jax.ShapeDtypeStruct(WHOLE, jnp.float32),
+        lambda *refs: advance_kernel(chunk, *refs),
+        out_shape=jax.ShapeDtypeStruct(shape, jnp.float32),
         in_specs=[pl.BlockSpec(memory_space=pltpu.SMEM)] + [VMEM] * 3,
         out_specs=VMEM,
-        scratch_shapes=[pltpu.VMEM((BLOCKS + 1, CELLS, TOTAL), jnp.float32)],
+        scratch_shapes=[pltpu.VMEM((BLOCKS + 1, *shape[1:]), jnp.float32)],
         compiler_params=pltpu.CompilerParams(vmem_limit_bytes=ADVANCE_VMEM),
         cost_estimate=pl.CostEstimate(
-            flops=100 * math.prod(WHOLE), bytes_accessed=6 * math.prod(WHOLE), transcendentals=0
+            flops=100 * math.prod(shape), bytes_accessed=6 * math.prod(shape), transcendentals=0
         ),
-        name="advance",
+        name=f"advance{chunk}",
     )(owner, received, mask, rate)
 
 
-def edge_kernel(partial, rate, down_y, up_y, down_x, up_x, out, made, sems):
+def edge_kernel(chunk, _, rate, *rest):
+    kinds = face_kinds(chunk)
+    halos, (out, partial, made, sems) = rest[: len(kinds)], rest[-4:]
     low_x, low_y, _ = row_masks()
     speed_y, _, _ = speeds()
 
-    def add(halo, axis, up, slots):
+    def add(kind, halo, slots):
+        axis, up = kind
         low, distance = (low_x, 4) if axis == "x" else (low_y, 2)
         edge = ~low if up else low
 
         @pl.loop(*slots)
         def _(pair):
             block = face_block(axis, 1 - up, pair)
-            for place, tile in enumerate(face_tiles(axis, up)):
-                face = halo[pair, :, lanes(place)].astype(jnp.float32)
+            for n, (place, tile) in enumerate(face_tiles(chunk, *kind)):
+                face = halo[pair, :, lanes(n)].astype(jnp.float32)
                 speed = speed_x(tile) if axis == "x" else speed_y[up]
                 other = swap(face, distance)
                 near = (jnp.where(edge, face, 0.0), jnp.where(edge, other, 0.0))
                 for side in range(2):
                     gain = rate[block + side] * (speed * swap(near[side], distance))
-                    partial_at = (block + side, slice(None), lanes(tile))
+                    partial_at = (block + side, slice(None), lanes(place))
                     partial[partial_at] = partial[partial_at] + gain
 
-    def result_copy(bx):
+    def result_copies(bx):
         rows = pl.ds(bx * SLAB, SLAB)
-        return pltpu.make_async_copy(made.at[rows], out.at[rows], sems.at[bx])
+        return [
+            pltpu.make_async_copy(
+                made.at[rows, :, pl.ds(place * 128, length * 128)],
+                out.at[rows, :, pl.ds(tile * 128, length * 128)],
+                sems.at[bx, n],
+            )
+            for n, (place, tile, length) in enumerate(runs_of(chunk))
+        ]
 
     for bx in range(BX):
-        if bx == 0:
-            add(up_x, "x", 1, (0, 12))
-        if bx == BX - 1:
-            add(down_x, "x", 0, (0, 12))
-        add(down_y, "y", 0, (3 * bx, 3 * bx + 3))
-        add(up_y, "y", 1, (3 * bx, 3 * bx + 3))
+        for kind, halo in zip(kinds, halos):
+            if kind[0] == "y":
+                add(kind, halo, (3 * bx, 3 * bx + 3))
+            elif bx == (0 if kind[1] else BX - 1):
+                add(kind, halo, (0, 12))
 
         @pl.loop(bx * SLAB, bx * SLAB + SLAB)
         def _(block):
             made[block] = partial[block].astype(jnp.bfloat16)
 
-        result_copy(bx).start()
+        for copy in result_copies(bx):
+            copy.start()
     for bx in range(BX):
-        result_copy(bx).wait()
-
-
-def edge(partial, rate, halos):
-    return pl.pallas_call(
-        edge_kernel,
-        out_shape=jax.ShapeDtypeStruct(WHOLE, jnp.bfloat16),
-        in_specs=[VMEM] * 6,
-        out_specs=ANY,
-        scratch_shapes=[pltpu.VMEM(WHOLE, jnp.bfloat16), pltpu.SemaphoreType.DMA((BX,))],
+        for copy in result_copies(bx):
+            copy.wait()
+
+
+def edge(chunk, partial, rate, halos, earlier):
+    shape = shape_of(chunk)
+    extra = [] if earlier is None else [earlier]
+    out, _ = pl.pallas_call(
+        lambda *refs: edge_kernel(chunk, *refs),
+        out_shape=[
+            jax.ShapeDtypeStruct(WHOLE, jnp.bfloat16),
+            jax.ShapeDtypeStruct(shape, jnp.float32),
+        ],
+        in_specs=[VMEM] * (2 + len(halos)) + [ANY] * len(extra),
+        out_specs=[ANY, VMEM],
+        scratch_shapes=[
+            pltpu.VMEM(shape, jnp.bfloat16),
+            pltpu.SemaphoreType.DMA((BX, len(runs_of(chunk)))),
+        ],
+        input_output_aliases={0: 1} | ({} if earlier is None else {2 + len(halos): 0}),
         compiler_params=pltpu.CompilerParams(vmem_limit_bytes=EDGE_VMEM),
         cost_estimate=pl.CostEstimate(
-            flops=4 * math.prod(WHOLE), bytes_accessed=6 * math.prod(WHOLE), transcendentals=0
+            flops=4 * math.prod(shape), bytes_accessed=6 * math.prod(shape), transcendentals=0
         ),
-        name="edge",
-    )(partial, rate, *halos)
+        name=f"edge{chunk}",
+    )(partial, rate, *halos, *extra)
+    return out
 
 
 def after(received, source_owner, levels, active):
@@ -450,27 +515,39 @@
     def down(n):
         return [(i + 1, i) for i in range(n - 1)]
 
-    *sent, received = faces(source_owner, received, mask)
-    halos = []
-    for (axis, to_above), face in zip(FACES, sent):
-        name, n = ("gx", n_gx) if axis == "x" else ("gy", n_gy)
-        halos.append(lax.ppermute(face, name, up(n) if to_above else down(n)))
-    return edge(advance(source_owner, received, mask, rate), rate, halos)
+    out = None
+    for chunk, arrived in enumerate(received):
+        if out is not None:
+            arrived, out = lax.optimization_barrier((arrived, out))
+        sent, arrived = faces(chunk, source_owner, arrived, mask)
+        halos = []
+        for (axis, to_above), face in zip(face_kinds(chunk), sent):
+            name, n = ("gx", n_gx) if axis == "x" else ("gy", n_gy)
+            halos.append(lax.ppermute(face, name, up(n) if to_above else down(n)))
+        partial = advance(chunk, source_owner, arrived, mask, rate)
+        out = edge(chunk, partial, rate, halos, out)
+    return out
 
 
 def per_device(dist_old, source_owner, levels, active):
     axes = ("gx", "gy")
-    devices = lax.axis_size("gx") * lax.axis_size("gy")
+    n_gx, n_gy = lax.axis_size("gx"), lax.axis_size("gy")
+    devices = n_gx * n_gy
     owners = lax.broadcasted_iota(jnp.int32, (devices, BLOCKS), 0)
     slots = lax.broadcasted_iota(jnp.int32, (devices, BLOCKS), 1)
     request = BLOCKS + jnp.sum(
         jnp.where(source_owner[None, :] == owners, slots - BLOCKS, 0), axis=1, keepdims=True
     )
-    asked = lax.all_to_all(
-        jnp.broadcast_to(request, (devices, 128)), axes, split_axis=0, concat_axis=0, tiled=True
-    )
-    send = pack(asked, relax(dist_old))
-    received = lax.all_to_all(send, axes, split_axis=0, concat_axis=0, tiled=True)
+    asked = jnp.broadcast_to(request, (devices, 128)).reshape(n_gx, n_gy, 128)
+    asked = lax.all_to_all(asked, "gx", split_axis=0, concat_axis=0, tiled=True)
+    asked = lax.all_to_all(asked, "gy", split_axis=1, concat_axis=1, tiled=True)
+    asked = asked.reshape(devices, 128)
+    received = [
+        lax.all_to_all(
+            pack(chunk, asked, relaxed), axes, split_axis=0, concat_axis=0, tiled=True
+        )
+        for chunk, relaxed in enumerate(relax(dist_old))
+    ]
     return after(received, source_owner, levels, active)
 
 

time: 173 us -> 179 us (1.035)
  waiting for transfers between devices: 102 us -> 79.2 us
  starting transfers between devices: 32.4 us -> 44.2 us
  blocking collectives: 0 us -> 9.79 us
  Pallas kernels: 36.1 us -> 41.5 us
    all_to_all x2 -> x3, waiting for transfers between devices: 102 us -> 71.4 us  [the longest x2 71.4 us: per_device(): lax.all_to_all(pack(chunk, asked, relaxed), axes, split_axis=0, concat_ax...]
    all_to_all x0 -> x1, blocking collectives: none -> 9.79 us  [per_device(): asked = lax.all_to_all(asked, 'gx', split_axis=0, concat_axis=0, tiled=True)]
    ppermute x4 -> x6, starting transfers between devices: 11.5 us -> 19.9 us  [after(): halos.append(lax.ppermute(face, name, up(n) if to_above else down(n)))]
    ppermute x4 -> x6, waiting for transfers between devices: 0.01 us -> 7.79 us  [after(): halos.append(lax.ppermute(face, name, up(n) if to_above else down(n)))]
    pallas_call x5 -> x9, Pallas kernels: 36.1 us -> 41.5 us  [the longest x1 11.6 us: relax(): pl.pallas_call(relax_kernel, out_shape=[jax.ShapeDtypeStruct(shape_of(c),...]
    all_to_all x2 -> x3, starting transfers between devices: 21 us -> 24.3 us  [the longest x2 16.6 us: per_device(): lax.all_to_all(pack(chunk, asked, relaxed), axes, split_axis=0, concat_ax...]
  transfers between devices with their start and end apart: 6 -> 9, of which waited for: 1 -> 3; matrix products, arithmetic and copies ran while one was open for 0% -> 0% of each run, Pallas kernels for 12% -> 19%
where the time goes in v4:
time: 179 us; the launch traced here: 178 us
  waiting for transfers between devices  79.2 us (44%)
  starting transfers between devices  44.2 us (25%)
  Pallas kernels  41.5 us (23%)
  blocking collectives  9.79 us (5%)
    all_to_all x2, waiting for transfers between devices, per_device(): lax.all_to_all(pack(chunk, asked, relaxed), axes, split_axis=0, concat_ax...  71.4 us
    ppermute x6, starting transfers between devices, after(): halos.append(lax.ppermute(face, name, up(n) if to_above else down(n)))  19.9 us
    all_to_all x2, starting transfers between devices, per_device(): lax.all_to_all(pack(chunk, asked, relaxed), axes, split_axis=0, concat_ax...  16.6 us
    pallas_call x1, Pallas kernels, relax(): pl.pallas_call(relax_kernel, out_shape=[jax.ShapeDtypeStruct(shape_of(c),...  11.6 us
    pallas_call x2, Pallas kernels, advance(): pl.pallas_call(lambda *refs: advance_kernel(chunk, *refs), out_shape=jax....  10.6 us
    all_to_all x1, blocking collectives, per_device(): asked = lax.all_to_all(asked, 'gx', split_axis=0, concat_axis=0, tiled=True)  9.79 us
    pallas_call x2, Pallas kernels, pack(): pl.pallas_call(pack_kernel, out_shape=jax.ShapeDtypeStruct(shape_of(chunk...  7.81 us
    ppermute x6, waiting for transfers between devices, after(): halos.append(lax.ppermute(face, name, up(n) if to_above else down(n)))  7.79 us
  transfers between devices with their start and end apart: 9, of which 3 were waited for; matrix products, arithmetic and copies ran while one was open for 0% of the time, Pallas kernels for 19%

profile of v4, /device:TPU:7, one launch (start us, length us, event | category | flops | bytes accessed | tf_op | source)
XLA Modules:
  0.0 177.7 jit_solution(11548013169965638598)
XLA Ops:
  0.0 0.8 select_reduce_fusion
  0.9 9.8 %all_to_all.20 = s32[8,16,128]{2,1,0:T(8,128)S(1)} all-to-all(s32[8,16,128]{2,1,0:T(8,128)S(1)} %broadcast_in_dim.9), channel_id=1, replica_groups=mesh['gx'=8,'gy'=16] {'gx'}, dimensions={0} | all-to-all | bytes 131072 | tf_op jit(solution)/shard_map/all_to_all | solution.py:542
  10.7 0.7 copy.16
  11.4 7.7 %all-to-all-start.1 = ((s32[8,16,128]{2,0,1:T(8,128)}), s32[8,16,128]{2,0,1:T(8,128)S(1)}, u32[]{:S(2)}, u32[]{:S(2)}) async-start(s32[8,16,128]{2,0,1:T(8,128)} %copy.16), calls=%async_computation.1 | async-start | bytes 131072 | tf_op jit(solution)/shard_map/all_to_all | solution.py:543
  19.1 11.6 %relax.1 = (bf16[96,8,3072]{2,1,0:T(8,128)(2,1)}, bf16[96,8,1024]{2,1,0:T(8,128)(2,1)}) custom-call(bf16[96,8,4096]{2,1,0:T(8,128)(2,1)} %dist.1, bf16[48,4096]{1,0:T(8,128)(2,1)} %constant.13.clone.basis), custom_call_target="tpu_custom_call" | custom-call | flops 9437184000 | bytes 12582912 | tf_op jit(solution)/shard_map/relax/pallas_call | solution.py:172
  31.4 4.7 %pack0.1 = bf16[128,8,3072]{2,1,0:T(8,128)(2,1)} custom-call(s32[128,128]{1,0:T(8,128)} %bitcast.1, bf16[96,8,3072]{2,1,0:T(8,128)(2,1)} %get-tuple-element.19.relaxed), custom_call_target="tpu_custom_call" | custom-call | bytes 9437184 | tf_op jit(solution)/shard_map/pack0/pallas_call | solution.py:219
  36.1 8.8 %all-to-all-start.3 = ((bf16[128,8,3072]{2,1,0:T(8,128)(2,1)}), bf16[128,8,3072]{2,1,0:T(8,128)(2,1)}, u32[]{:S(2)}, u32[]{:S(2)}) async-start(bf16[128,8,3072]{2,1,0:T(8,128)(2,1)} %pack0.1), calls=%async_computation.3 | async-start | bytes 12582912 | tf_op jit(solution)/shard_map/all_to_all | solution.py:546
  45.0 3.1 %pack1.1 = bf16[128,8,1024]{2,1,0:T(8,128)(2,1)} custom-call(s32[128,128]{1,0:T(8,128)} %bitcast.2, bf16[96,8,1024]{2,1,0:T(8,128)(2,1)} %get-tuple-element.18.relaxed), custom_call_target="tpu_custom_call" | custom-call | bytes 3145728 | tf_op jit(solution)/shard_map/pack1/pallas_call | solution.py:219
  48.1 71.4 %all-to-all-done.3.refs_1_ = bf16[128,8,3072]{2,1,0:T(8,128)(2,1)} async-done(((bf16[128,8,3072]{2,1,0:T(8,128)(2,1)}), bf16[128,8,3072]{2,1,0:T(8,128)(2,1)}, u32[]{:S(2)}, u32[]{:S(2)}) %all-to-all-start.3) | async-done | bytes 6291488 | tf_op jit(solution)/shard_map/all_to_all | solution.py:546
  119.5 7.8 %all-to-all-start.2 = ((bf16[128,8,1024]{2,1,0:T(8,128)(2,1)}), bf16[128,8,1024]{2,1,0:T(8,128)(2,1)S(1)}, u32[]{:S(2)}, u32[]{:S(2)}) async-start(bf16[128,8,1024]{2,1,0:T(8,128)(2,1)} %pack1.1), calls=%async_computation.2 | async-start | bytes 4194304 | tf_op jit(solution)/shard_map/all_to_all | solution.py:546
  127.5 4.6 %faces0.1 = (bf16[12,8,1024]{2,1,0:T(8,128)(2,1)S(1)}, bf16[12,8,1024]{2,1,0:T(8,128)(2,1)S(1)}, bf16[12,8,2048]{2,1,0:T(8,128)(2,1)S(1)}, bf16[12,8,2048]{2,1,0:T(8,128)(2,1)S(1)}, bf16[128,8,3072]{2,1,0:T(8,128)(2,1)S(1)}) custom-call(s32[96]{0:T(128)S(1)} %copy-done, bf16[128,8,3072]{2,1,0:T(8,128)(2,1)} %all-to-all-done.3.refs_1_, ...), custom_call_target="tpu_custom_call" | custom-call | flops 4718592 | bytes 2359296 | tf_op jit(solution)/shard_map/faces0/pallas_call | solution.py:323
  132.2 5.3 %collective-permute-start.2 = (bf16[12,8,2048]{2,1,0:T(8,128)(2,1)S(1)}, bf16[12,8,2048]{2,1,0:T(8,128)(2,1)S(1)}, u32[]{:S(2)}, u32[]{:S(2)}) collective-permute-start(bf16[12,8,2048]{2,1,0:T(8,128)(2,1)S(1)} %get-tuple-element.23), channel_id=1, source_target_pairs={{1,0},{2,1},{3,2},{4,3},{5,4},{6,5},{7,6},{8,7},{9,8},{10,9},{11,1... | collective-permute-start | bytes 1179656 | tf_op jit(solution)/shard_map/ppermute | solution.py:526
  137.5 2.5 %collective-permute-start.3 = (bf16[12,8,2048]{2,1,0:T(8,128)(2,1)S(1)}, bf16[12,8,2048]{2,1,0:T(8,128)(2,1)S(1)}, u32[]{:S(2)}, u32[]{:S(2)}) collective-permute-start(bf16[12,8,2048]{2,1,0:T(8,128)(2,1)S(1)} %get-tuple-element.24), channel_id=1, source_target_pairs={{16,0},{32,16},{48,32},{64,48},{80,64},{96,80},{112,96},{17,1},{33... | collective-permute-start | bytes 1179656 | tf_op jit(solution)/shard_map/ppermute | solution.py:526
  140.0 1.9 %collective-permute-start = (bf16[12,8,1024]{2,1,0:T(8,128)(2,1)S(1)}, bf16[12,8,1024]{2,1,0:T(8,128)(2,1)S(1)}, u32[]{:S(2)}, u32[]{:S(2)}) collective-permute-start(bf16[12,8,1024]{2,1,0:T(8,128)(2,1)S(1)} %get-tuple-element.21), channel_id=1, source_target_pairs={{0,1},{1,2},{2,3},{3,4},{4,5},{5,6},{6,7},{7,8},{8,9},{9,10},{10,1... | collective-permute-start | bytes 589832 | tf_op jit(solution)/shard_map/ppermute | solution.py:526
  142.0 3.1 %collective-permute-start.1 = (bf16[12,8,1024]{2,1,0:T(8,128)(2,1)S(1)}, bf16[12,8,1024]{2,1,0:T(8,128)(2,1)S(1)}, u32[]{:S(2)}, u32[]{:S(2)}) collective-permute-start(bf16[12,8,1024]{2,1,0:T(8,128)(2,1)S(1)} %get-tuple-element.22), channel_id=1, source_target_pairs={{0,16},{16,32},{32,48},{48,64},{64,80},{80,96},{96,112},{1,17},{17... | collective-permute-start | bytes 589832 | tf_op jit(solution)/shard_map/ppermute | solution.py:526
  145.3 7.3 %advance0.1.refs_0_ = f32[96,8,3072]{2,1,0:T(8,128)S(1)} custom-call(s32[96]{0:T(128)S(1)} %copy-done, bf16[128,8,3072]{2,1,0:T(8,128)(2,1)S(1)} %get-tuple-element.20.refs_1_, f32[96,8,128]{2,1,0:T(8,128)S(1)} %broadcast_in_dim.10.refs_2_, f32[96,8,128]{2,1,0:T(8,128)S(1)} %broadcast_multiply_fusion.refs_3_.refs_1_), custom_call_target="tpu_custom_call" | custom-call | flops 235929600 | bytes 14155776 | tf_op jit(solution)/shard_map/advance0/pallas_call | solution.py:412
  152.6 6.6 %collective-permute-done.refs_2_ = bf16[12,8,1024]{2,1,0:T(8,128)(2,1)S(1)} collective-permute-done((bf16[12,8,1024]{2,1,0:T(8,128)(2,1)S(1)}, bf16[12,8,1024]{2,1,0:T(8,128)(2,1)S(1)}, u32[]{:S(2)}, u32[]{:S(2)}) %collective-permute-start) | collective-permute-done | bytes 196640 | tf_op jit(solution)/shard_map/ppermute | solution.py:526
  159.2 1.2 collective-permute-done.2.refs_4_
  160.4 3.5 %edge0.1 = (bf16[96,8,4096]{2,1,0:T(8,128)(2,1)}, f32[96,8,3072]{2,1,0:T(8,128)S(1)}) custom-call(f32[96,8,3072]{2,1,0:T(8,128)S(1)} %advance0.1.refs_0_, f32[96,8,128]{2,1,0:T(8,128)S(1)} %broadcast_multiply_fusion.refs_3_.refs_1_, bf16[12,8,1024]{2,1,0:T(8,128)(2,1)S(1)} %collective-permute-done.refs_2_, ...), custom_call_target="tpu_custom_call", output_to_operand_aliasing={{1}: (0, {})} | custom-call | flops 9437184 | bytes 14155776 | tf_op jit(solution)/shard_map/edge0/pallas_call | solution.py:482
  163.9 1.1 faces1.1
  165.0 3.7 %collective-permute-start.4 = (bf16[12,8,1024]{2,1,0:T(8,128)(2,1)S(1)}, bf16[12,8,1024]{2,1,0:T(8,128)(2,1)S(1)}, u32[]{:S(2)}, u32[]{:S(2)}) collective-permute-start(bf16[12,8,1024]{2,1,0:T(8,128)(2,1)S(1)} %get-tuple-element.27), channel_id=1, source_target_pairs={{0,1},{1,2},{2,3},{3,4},{4,5},{5,6},{6,7},{7,8},{8,9},{9,10},{10,1... | collective-permute-start | bytes 589832 | tf_op jit(solution)/shard_map/ppermute | solution.py:526
  168.7 3.4 %collective-permute-start.5 = (bf16[12,8,1024]{2,1,0:T(8,128)(2,1)S(1)}, bf16[12,8,1024]{2,1,0:T(8,128)(2,1)S(1)}, u32[]{:S(2)}, u32[]{:S(2)}) collective-permute-start(bf16[12,8,1024]{2,1,0:T(8,128)(2,1)S(1)} %get-tuple-element.28), channel_id=1, source_target_pairs={{0,16},{16,32},{32,48},{48,64},{64,80},{80,96},{96,112},{1,17},{17... | collective-permute-start | bytes 589832 | tf_op jit(solution)/shard_map/ppermute | solution.py:526
  172.1 3.4 %advance1.1.refs_0_ = f32[96,8,1024]{2,1,0:T(8,128)S(1)} custom-call(s32[96]{0:T(128)S(1)} %copy-done, bf16[128,8,1024]{2,1,0:T(8,128)(2,1)S(1)} %all-to-all-done.2.refs_1_, f32[96,8,128]{2,1,0:T(8,128)S(1)} %broadcast_in_dim.10.refs_2_, f32[96,8,128]{2,1,0:T(8,128)S(1)} %broadcast_multiply_fusion.refs_3_.refs_1_), custom_call_target="tpu_custom_call" | custom-call | flops 78643200 | bytes 4718592 | tf_op jit(solution)/shard_map/advance1/pallas_call | solution.py:412
  175.5 2.2 %edge1.1 = (bf16[96,8,4096]{2,1,0:T(8,128)(2,1)}, f32[96,8,1024]{2,1,0:T(8,128)S(1)}) custom-call(f32[96,8,1024]{2,1,0:T(8,128)S(1)} %advance1.1.refs_0_, f32[96,8,128]{2,1,0:T(8,128)S(1)} %broadcast_multiply_fusion.refs_3_.refs_1_, bf16[12,8,1024]{2,1,0:T(8,128)(2,1)S(1)} %collective-permute-done.4.refs_2_, ...), custom_call_target="tpu_custom_call", output_to_operand_aliasing={{1}: (0, {}), {0}: (4, {})} | custom-call | flops 3145728 | bytes 4718592 | tf_op jit(solution)/shard_map/edge1/pallas_call | solution.py:482
  (22 shorter events, 1.4 us)
Async XLA Ops:
  11.4 19.4 %all-to-all-start.1 = ((s32[8,16,128]{2,0,1:T(8,128)}), s32[8,16,128]{2,0,1:T(8,128)S(1)}, u32[]{:S(2)}, u32[]{:S(2)}) async-start(s32[8,16,128]{2,0,1:T(8,128)} %copy.16), calls=%async_computation.1 | async-start | bytes 131072 | tf_op jit(solution)/shard_map/all_to_all | solution.py:543
  36.1 83.4 %all-to-all-start.3 = ((bf16[128,8,3072]{2,1,0:T(8,128)(2,1)}), bf16[128,8,3072]{2,1,0:T(8,128)(2,1)}, u32[]{:S(2)}, u32[]{:S(2)}) async-start(bf16[128,8,3072]{2,1,0:T(8,128)(2,1)} %pack0.1), calls=%async_computation.3 | async-start | bytes 12582912 | tf_op jit(solution)/shard_map/all_to_all | solution.py:546
  44.9 82.3 %copy-start.1 = (s32[96,8]{0,1:T(8,128)S(1)}, s32[96,8]{0,1:T(8,128)}, u32[]{:S(2)}) copy-start(s32[96,8]{0,1:T(8,128)} %param.8) | copy-start | bytes 9220
  44.9 82.6 %copy-start = (s32[96]{0:T(128)S(1)}, s32[96]{0:T(128)}, u32[]{:S(2)}) copy-start(s32[96]{0:T(128)} %refs_0_.7) | copy-start | bytes 1156
  48.0 92.0 %copy-start.2 = (s32[96]{0:T(128)S(1)}, s32[96]{0:T(128)}, u32[]{:S(2)}) copy-start(s32[96]{0:T(128)} %param.7) | copy-start | bytes 1156
  119.5 44.4 %all-to-all-start.2 = ((bf16[128,8,1024]{2,1,0:T(8,128)(2,1)}), bf16[128,8,1024]{2,1,0:T(8,128)(2,1)S(1)}, u32[]{:S(2)}, u32[]{:S(2)}) async-start(bf16[128,8,1024]{2,1,0:T(8,128)(2,1)} %pack1.1), calls=%async_computation.2 | async-start | bytes 4194304 | tf_op jit(solution)/shard_map/all_to_all | solution.py:546
  132.2 28.2 %collective-permute-start.2 = (bf16[12,8,2048]{2,1,0:T(8,128)(2,1)S(1)}, bf16[12,8,2048]{2,1,0:T(8,128)(2,1)S(1)}, u32[]{:S(2)}, u32[]{:S(2)}) collective-permute-start(bf16[12,8,2048]{2,1,0:T(8,128)(2,1)S(1)} %get-tuple-element.23), channel_id=1, source_target_pairs={{1,0},{2,1},{3,2},{4,3},{5,4},{6,5},{7,6},{8,7},{9,8},{10,9},{11,1... | collective-permute-start | bytes 1179656 | tf_op jit(solution)/shard_map/ppermute | solution.py:526
  137.5 22.9 %collective-permute-start.3 = (bf16[12,8,2048]{2,1,0:T(8,128)(2,1)S(1)}, bf16[12,8,2048]{2,1,0:T(8,128)(2,1)S(1)}, u32[]{:S(2)}, u32[]{:S(2)}) collective-permute-start(bf16[12,8,2048]{2,1,0:T(8,128)(2,1)S(1)} %get-tuple-element.24), channel_id=1, source_target_pairs={{16,0},{32,16},{48,32},{64,48},{80,64},{96,80},{112,96},{17,1},{33... | collective-permute-start | bytes 1179656 | tf_op jit(solution)/shard_map/ppermute | solution.py:526
  140.0 19.1 %collective-permute-start = (bf16[12,8,1024]{2,1,0:T(8,128)(2,1)S(1)}, bf16[12,8,1024]{2,1,0:T(8,128)(2,1)S(1)}, u32[]{:S(2)}, u32[]{:S(2)}) collective-permute-start(bf16[12,8,1024]{2,1,0:T(8,128)(2,1)S(1)} %get-tuple-element.21), channel_id=1, source_target_pairs={{0,1},{1,2},{2,3},{3,4},{4,5},{5,6},{6,7},{7,8},{8,9},{9,10},{10,1... | collective-permute-start | bytes 589832 | tf_op jit(solution)/shard_map/ppermute | solution.py:526
  142.0 17.2 %collective-permute-start.1 = (bf16[12,8,1024]{2,1,0:T(8,128)(2,1)S(1)}, bf16[12,8,1024]{2,1,0:T(8,128)(2,1)S(1)}, u32[]{:S(2)}, u32[]{:S(2)}) collective-permute-start(bf16[12,8,1024]{2,1,0:T(8,128)(2,1)S(1)} %get-tuple-element.22), channel_id=1, source_target_pairs={{0,16},{16,32},{32,48},{48,64},{64,80},{80,96},{96,112},{1,17},{17... | collective-permute-start | bytes 589832 | tf_op jit(solution)/shard_map/ppermute | solution.py:526
  165.0 10.5 %collective-permute-start.4 = (bf16[12,8,1024]{2,1,0:T(8,128)(2,1)S(1)}, bf16[12,8,1024]{2,1,0:T(8,128)(2,1)S(1)}, u32[]{:S(2)}, u32[]{:S(2)}) collective-permute-start(bf16[12,8,1024]{2,1,0:T(8,128)(2,1)S(1)} %get-tuple-element.27), channel_id=1, source_target_pairs={{0,1},{1,2},{2,3},{3,4},{4,5},{5,6},{6,7},{7,8},{8,9},{9,10},{10,1... | collective-permute-start | bytes 589832 | tf_op jit(solution)/shard_map/ppermute | solution.py:526
  168.7 6.8 %collective-permute-start.5 = (bf16[12,8,1024]{2,1,0:T(8,128)(2,1)S(1)}, bf16[12,8,1024]{2,1,0:T(8,128)(2,1)S(1)}, u32[]{:S(2)}, u32[]{:S(2)}) collective-permute-start(bf16[12,8,1024]{2,1,0:T(8,128)(2,1)S(1)} %get-tuple-element.28), channel_id=1, source_target_pairs={{0,16},{16,32},{32,48},{48,64},{64,80},{80,96},{96,112},{1,17},{17... | collective-permute-start | bytes 589832 | tf_op jit(solution)/shard_map/ppermute | solution.py:526

commit v5 on v4

--- a/solution.py
+++ b/solution.py
@@ -21,7 +21,7 @@
 LOG2E = 1.0 / math.log(2.0)
 
 TILES = TOTAL // 128
-LATE = tuple(range(TILES // 2 + 1, TILES, 2))
+LATE = (17, 19, 21, 23, 25, 26, 27, 28, 29, 30, 31)
 CHUNKS = (tuple(t for t in range(TILES) if t not in LATE), LATE)
 PIECE = 16
 RELAX_VMEM = 60 << 20
@@ -531,17 +531,15 @@
 
 def per_device(dist_old, source_owner, levels, active):
     axes = ("gx", "gy")
-    n_gx, n_gy = lax.axis_size("gx"), lax.axis_size("gy")
-    devices = n_gx * n_gy
+    devices = lax.axis_size("gx") * lax.axis_size("gy")
     owners = lax.broadcasted_iota(jnp.int32, (devices, BLOCKS), 0)
     slots = lax.broadcasted_iota(jnp.int32, (devices, BLOCKS), 1)
     request = BLOCKS + jnp.sum(
         jnp.where(source_owner[None, :] == owners, slots - BLOCKS, 0), axis=1, keepdims=True
     )
-    asked = jnp.broadcast_to(request, (devices, 128)).reshape(n_gx, n_gy, 128)
-    asked = lax.all_to_all(asked, "gx", split_axis=0, concat_axis=0, tiled=True)
-    asked = lax.all_to_all(asked, "gy", split_axis=1, concat_axis=1, tiled=True)
-    asked = asked.reshape(devices, 128)
+    asked = lax.all_to_all(
+        jnp.broadcast_to(request, (devices, 128)), axes, split_axis=0, concat_axis=0, tiled=True
+    )
     received = [
         lax.all_to_all(
             pack(chunk, asked, relaxed), axes, split_axis=0, concat_axis=0, tiled=True

time: 179 us -> 176 us (0.983)
  blocking collectives: 9.79 us -> 0 us
  starting transfers between devices: 44.2 us -> 50.9 us
  local copies, waits for them, and re-layouts: 1.71 us -> 3.7 us
  waiting for transfers between devices: 79.2 us -> 77.3 us
    all_to_all x2, waiting for transfers between devices: 71.4 us -> 61.5 us  [per_device(): lax.all_to_all(pack(chunk, asked, relaxed), axes, split_axis=0, concat_ax...]
    all_to_all x1 -> x0, blocking collectives: 9.79 us -> none  [per_device(): asked = lax.all_to_all(asked, 'gx', split_axis=0, concat_axis=0, tiled=True)]
    ppermute x6 -> x7, waiting for transfers between devices: 7.79 us -> 15.8 us  [after(): halos.append(lax.ppermute(face, name, up(n) if to_above else down(n)))]
    ppermute x6 -> x7, starting transfers between devices: 19.9 us -> 23.3 us  [after(): halos.append(lax.ppermute(face, name, up(n) if to_above else down(n)))]
    all_to_all x1, starting transfers between devices: 7.71 us -> 10.8 us  [per_device(): lax.all_to_all(jnp.broadcast_to(request, (devices, 128)), axes, split_axi...]
    unnamed x6 -> x14, local copies, waits for them, and re-layouts: 0.02 us -> 2.62 us
  transfers between devices with their start and end apart: 9 -> 10, of which waited for: 3 -> 3; matrix products, arithmetic and copies ran while one was open for 0% -> 0% of each run, Pallas kernels for 19% -> 19%
where the time goes in v5:
time: 176 us; the launch traced here: 174 us
  waiting for transfers between devices  77.3 us (44%)
  starting transfers between devices  50.9 us (29%)
  Pallas kernels  41.2 us (23%)
  local copies, waits for them, and re-layouts  3.7 us (2%)
    all_to_all x2, waiting for transfers between devices, per_device(): lax.all_to_all(pack(chunk, asked, relaxed), axes, split_axis=0, concat_ax...  61.5 us
    ppermute x7, starting transfers between devices, after(): halos.append(lax.ppermute(face, name, up(n) if to_above else down(n)))  23.3 us
    all_to_all x2, starting transfers between devices, per_device(): lax.all_to_all(pack(chunk, asked, relaxed), axes, split_axis=0, concat_ax...  16.8 us
    ppermute x7, waiting for transfers between devices, after(): halos.append(lax.ppermute(face, name, up(n) if to_above else down(n)))  15.8 us
    pallas_call x1, Pallas kernels, relax(): pl.pallas_call(relax_kernel, out_shape=[jax.ShapeDtypeStruct(shape_of(c),...  11.7 us
    all_to_all x1, starting transfers between devices, per_device(): lax.all_to_all(jnp.broadcast_to(request, (devices, 128)), axes, split_axi...  10.8 us
    pallas_call x2, Pallas kernels, advance(): pl.pallas_call(lambda *refs: advance_kernel(chunk, *refs), out_shape=jax....  10.7 us
    pallas_call x2, Pallas kernels, pack(): pl.pallas_call(pack_kernel, out_shape=jax.ShapeDtypeStruct(shape_of(chunk...  7.45 us
  transfers between devices with their start and end apart: 10, of which 3 were waited for; matrix products, arithmetic and copies ran while one was open for 0% of the time, Pallas kernels for 19%

profile of v5, /device:TPU:7, one launch (start us, length us, event | category | flops | bytes accessed | tf_op | source)
XLA Modules:
  0.0 174.4 jit_solution(16033150766280043291)
XLA Ops:
  1.6 10.8 %all-to-all-start = ((s32[128,1,128]{2,1,0:T(1,128)}), s32[128,1,128]{2,1,0:T(1,128)S(1)}, u32[]{:S(2)}, u32[]{:S(2)}) async-start(s32[128,1,128]{2,1,0:T(1,128)} %broadcast_in_dim.9), calls=%async_computation | async-start | bytes 131072 | tf_op jit(solution)/shard_map/all_to_all | solution.py:540
  12.4 11.7 %relax.1 = (bf16[96,8,2688]{2,1,0:T(8,128)(2,1)}, bf16[96,8,1408]{2,1,0:T(8,128)(2,1)}) custom-call(bf16[96,8,4096]{2,1,0:T(8,128)(2,1)} %dist.1, bf16[48,4096]{1,0:T(8,128)(2,1)} %constant.13.clone.basis), custom_call_target="tpu_custom_call" | custom-call | flops 9437184000 | bytes 12582912 | tf_op jit(solution)/shard_map/relax/pallas_call | solution.py:172
  24.7 4.2 %pack0.1 = bf16[128,8,2688]{2,1,0:T(8,128)(2,1)} custom-call(s32[128,128]{1,0:T(8,128)} %bitcast.1, bf16[96,8,2688]{2,1,0:T(8,128)(2,1)} %get-tuple-element.20.relaxed), custom_call_target="tpu_custom_call" | custom-call | bytes 8257536 | tf_op jit(solution)/shard_map/pack0/pallas_call | solution.py:219
  28.9 10.2 %all-to-all-start.2 = ((bf16[128,8,2688]{2,1,0:T(8,128)(2,1)}), bf16[128,8,2688]{2,1,0:T(8,128)(2,1)}, u32[]{:S(2)}, u32[]{:S(2)}) async-start(bf16[128,8,2688]{2,1,0:T(8,128)(2,1)} %pack0.1), calls=%async_computation.2 | async-start | bytes 11010048 | tf_op jit(solution)/shard_map/all_to_all | solution.py:544
  39.1 3.3 %pack1.1 = bf16[128,8,1408]{2,1,0:T(8,128)(2,1)} custom-call(s32[128,128]{1,0:T(8,128)} %bitcast.2, bf16[96,8,1408]{2,1,0:T(8,128)(2,1)} %get-tuple-element.19.relaxed), custom_call_target="tpu_custom_call" | custom-call | bytes 4325376 | tf_op jit(solution)/shard_map/pack1/pallas_call | solution.py:219
  42.4 61.5 %all-to-all-done.2.refs_1_ = bf16[128,8,2688]{2,1,0:T(8,128)(2,1)} async-done(((bf16[128,8,2688]{2,1,0:T(8,128)(2,1)}), bf16[128,8,2688]{2,1,0:T(8,128)(2,1)}, u32[]{:S(2)}, u32[]{:S(2)}) %all-to-all-start.2) | async-done | bytes 5505056 | tf_op jit(solution)/shard_map/all_to_all | solution.py:544
  103.8 6.6 %all-to-all-start.1 = ((bf16[128,8,1408]{2,1,0:T(8,128)(2,1)}), bf16[128,8,1408]{2,1,0:T(8,128)(2,1)S(1)}, u32[]{:S(2)}, u32[]{:S(2)}) async-start(bf16[128,8,1408]{2,1,0:T(8,128)(2,1)} %pack1.1), calls=%async_computation.1 | async-start | bytes 5767168 | tf_op jit(solution)/shard_map/all_to_all | solution.py:544
  110.7 4.3 %faces0.1 = (bf16[12,8,1024]{2,1,0:T(8,128)(2,1)S(1)}, bf16[12,8,640]{2,1,0:T(8,128)(2,1)S(1)}, bf16[12,8,1664]{2,1,0:T(8,128)(2,1)S(1)}, bf16[12,8,2048]{2,1,0:T(8,128)(2,1)S(1)}, bf16[128,8,2688]{2,1,0:T(8,128)(2,1)S(1)}) custom-call(s32[96]{0:T(128)S(1)} %copy-done.3, bf16[128,8,2688]{2,1,0:T(8,128)(2,1)} %all-to-all-done.2.refs_1_, ...), custom_call_target="tpu_custom_call" | custom-call | flops 4128768 | bytes 2064384 | tf_op jit(solution)/shard_map/faces0/pallas_call | solution.py:323
  115.1 2.3 %collective-permute-start.3 = (bf16[12,8,2048]{2,1,0:T(8,128)(2,1)S(1)}, bf16[12,8,2048]{2,1,0:T(8,128)(2,1)S(1)}, u32[]{:S(2)}, u32[]{:S(2)}) collective-permute-start(bf16[12,8,2048]{2,1,0:T(8,128)(2,1)S(1)} %get-tuple-element.25), channel_id=1, source_target_pairs={{16,0},{32,16},{48,32},{64,48},{80,64},{96,80},{112,96},{17,1},{33... | collective-permute-start | bytes 1179656 | tf_op jit(solution)/shard_map/ppermute | solution.py:526
  117.3 5.3 %collective-permute-start.2 = (bf16[12,8,1664]{2,1,0:T(8,128)(2,1)S(1)}, bf16[12,8,1664]{2,1,0:T(8,128)(2,1)S(1)}, u32[]{:S(2)}, u32[]{:S(2)}) collective-permute-start(bf16[12,8,1664]{2,1,0:T(8,128)(2,1)S(1)} %get-tuple-element.24), channel_id=1, source_target_pairs={{1,0},{2,1},{3,2},{4,3},{5,4},{6,5},{7,6},{8,7},{9,8},{10,9},{11,1... | collective-permute-start | bytes 958472 | tf_op jit(solution)/shard_map/ppermute | solution.py:526
  122.7 1.9 %collective-permute-start = (bf16[12,8,1024]{2,1,0:T(8,128)(2,1)S(1)}, bf16[12,8,1024]{2,1,0:T(8,128)(2,1)S(1)}, u32[]{:S(2)}, u32[]{:S(2)}) collective-permute-start(bf16[12,8,1024]{2,1,0:T(8,128)(2,1)S(1)} %get-tuple-element.22), channel_id=1, source_target_pairs={{0,1},{1,2},{2,3},{3,4},{4,5},{5,6},{6,7},{7,8},{8,9},{9,10},{10,1... | collective-permute-start | bytes 589832 | tf_op jit(solution)/shard_map/ppermute | solution.py:526
  124.6 3.6 %collective-permute-start.1 = (bf16[12,8,640]{2,1,0:T(8,128)(2,1)S(1)}, bf16[12,8,640]{2,1,0:T(8,128)(2,1)S(1)}, u32[]{:S(2)}, u32[]{:S(2)}) collective-permute-start(bf16[12,8,640]{2,1,0:T(8,128)(2,1)S(1)} %get-tuple-element.23), channel_id=1, source_target_pairs={{0,16},{16,32},{32,48},{48,64},{64,80},{80,96},{96,112},{1,17},{17... | collective-permute-start | bytes 368648 | tf_op jit(solution)/shard_map/ppermute | solution.py:526
  128.4 6.6 %advance0.1.refs_0_ = f32[96,8,2688]{2,1,0:T(8,128)S(1)} custom-call(s32[96]{0:T(128)S(1)} %copy-done.3, bf16[128,8,2688]{2,1,0:T(8,128)(2,1)S(1)} %get-tuple-element.21.refs_1_, f32[96,8,128]{2,1,0:T(8,128)S(1)} %broadcast_in_dim.10.refs_2_, f32[96,8,128]{2,1,0:T(8,128)S(1)} %broadcast_multiply_fusion.refs_3_.refs_1_), custom_call_target="tpu_custom_call" | custom-call | flops 206438400 | bytes 12386304 | tf_op jit(solution)/shard_map/advance0/pallas_call | solution.py:412
  135.0 7.2 %collective-permute-done.1.refs_3_ = bf16[12,8,640]{2,1,0:T(8,128)(2,1)S(1)} collective-permute-done((bf16[12,8,640]{2,1,0:T(8,128)(2,1)S(1)}, bf16[12,8,640]{2,1,0:T(8,128)(2,1)S(1)}, u32[]{:S(2)}, u32[]{:S(2)}) %collective-permute-start.1) | collective-permute-done | bytes 122912 | tf_op jit(solution)/shard_map/ppermute | solution.py:526
  142.2 8.6 %collective-permute-done.refs_2_ = bf16[12,8,1024]{2,1,0:T(8,128)(2,1)S(1)} collective-permute-done((bf16[12,8,1024]{2,1,0:T(8,128)(2,1)S(1)}, bf16[12,8,1024]{2,1,0:T(8,128)(2,1)S(1)}, u32[]{:S(2)}, u32[]{:S(2)}) %collective-permute-start) | collective-permute-done | bytes 196640 | tf_op jit(solution)/shard_map/ppermute | solution.py:526
  150.8 3.2 %edge0.1 = (bf16[96,8,4096]{2,1,0:T(8,128)(2,1)}, f32[96,8,2688]{2,1,0:T(8,128)S(1)}) custom-call(f32[96,8,2688]{2,1,0:T(8,128)S(1)} %advance0.1.refs_0_, f32[96,8,128]{2,1,0:T(8,128)S(1)} %broadcast_multiply_fusion.refs_3_.refs_1_, bf16[12,8,1024]{2,1,0:T(8,128)(2,1)S(1)} %collective-permute-done.refs_2_, ...), custom_call_target="tpu_custom_call", output_to_operand_aliasing={{1}: (0, {})} | custom-call | flops 8257536 | bytes 12386304 | tf_op jit(solution)/shard_map/edge0/pallas_call | solution.py:482
  154.0 1.0 copy-done.1
  155.0 1.4 faces1.1
  156.4 2.9 %collective-permute-start.5 = (bf16[12,8,1408]{2,1,0:T(8,128)(2,1)S(1)}, bf16[12,8,1408]{2,1,0:T(8,128)(2,1)S(1)}, u32[]{:S(2)}, u32[]{:S(2)}) collective-permute-start(bf16[12,8,1408]{2,1,0:T(8,128)(2,1)S(1)} %get-tuple-element.29), channel_id=1, source_target_pairs={{0,16},{16,32},{32,48},{48,64},{64,80},{80,96},{96,112},{1,17},{17... | collective-permute-start | bytes 811016 | tf_op jit(solution)/shard_map/ppermute | solution.py:526
  159.3 3.5 %collective-permute-start.4 = (bf16[12,8,1024]{2,1,0:T(8,128)(2,1)S(1)}, bf16[12,8,1024]{2,1,0:T(8,128)(2,1)S(1)}, u32[]{:S(2)}, u32[]{:S(2)}) collective-permute-start(bf16[12,8,1024]{2,1,0:T(8,128)(2,1)S(1)} %get-tuple-element.28), channel_id=1, source_target_pairs={{0,1},{1,2},{2,3},{3,4},{4,5},{5,6},{6,7},{7,8},{8,9},{9,10},{10,1... | collective-permute-start | bytes 589832 | tf_op jit(solution)/shard_map/ppermute | solution.py:526
  162.8 3.9 %collective-permute-start.6 = (bf16[12,8,384]{2,1,0:T(8,128)(2,1)S(1)}, bf16[12,8,384]{2,1,0:T(8,128)(2,1)S(1)}, u32[]{:S(2)}, u32[]{:S(2)}) collective-permute-start(bf16[12,8,384]{2,1,0:T(8,128)(2,1)S(1)} %get-tuple-element.30), channel_id=1, source_target_pairs={{1,0},{2,1},{3,2},{4,3},{5,4},{6,5},{7,6},{8,7},{9,8},{10,9},{11,1... | collective-permute-start | bytes 221192 | tf_op jit(solution)/shard_map/ppermute | solution.py:526
  166.8 1.0 copy-done.2
  167.7 4.1 %advance1.1.refs_0_ = f32[96,8,1408]{2,1,0:T(8,128)S(1)} custom-call(s32[96]{0:T(128)S(1)} %copy-done.3, bf16[128,8,1408]{2,1,0:T(8,128)(2,1)S(1)} %all-to-all-done.1.refs_1_, f32[96,8,128]{2,1,0:T(8,128)S(1)} %copy-done.2, f32[96,8,128]{2,1,0:T(8,128)S(1)} %broadcast_multiply_fusion.refs_3_.refs_1_), custom_call_target="tpu_custom_call" | custom-call | flops 108134400 | bytes 6488064 | tf_op jit(solution)/shard_map/advance1/pallas_call | solution.py:412
  171.9 2.5 %edge1.1 = (bf16[96,8,4096]{2,1,0:T(8,128)(2,1)}, f32[96,8,1408]{2,1,0:T(8,128)S(1)}) custom-call(f32[96,8,1408]{2,1,0:T(8,128)S(1)} %advance1.1.refs_0_, f32[96,8,128]{2,1,0:T(8,128)S(1)} %broadcast_multiply_fusion.refs_3_.refs_1_, bf16[12,8,1024]{2,1,0:T(8,128)(2,1)S(1)} %collective-permute-done.4.refs_2_, ...), custom_call_target="tpu_custom_call", output_to_operand_aliasing={{1}: (0, {}), {0}: (5, {})} | custom-call | flops 4325376 | bytes 6488064 | tf_op jit(solution)/shard_map/edge1/pallas_call | solution.py:482
  (28 shorter events, 2.8 us)
Async XLA Ops:
  1.6 22.5 %all-to-all-start = ((s32[128,1,128]{2,1,0:T(1,128)}), s32[128,1,128]{2,1,0:T(1,128)S(1)}, u32[]{:S(2)}, u32[]{:S(2)}) async-start(s32[128,1,128]{2,1,0:T(1,128)} %broadcast_in_dim.9), calls=%async_computation | async-start | bytes 131072 | tf_op jit(solution)/shard_map/all_to_all | solution.py:540
  24.1 0.6 copy-start.4
  28.9 75.0 %all-to-all-start.2 = ((bf16[128,8,2688]{2,1,0:T(8,128)(2,1)}), bf16[128,8,2688]{2,1,0:T(8,128)(2,1)}, u32[]{:S(2)}, u32[]{:S(2)}) async-start(bf16[128,8,2688]{2,1,0:T(8,128)(2,1)} %pack0.1), calls=%async_computation.2 | async-start | bytes 11010048 | tf_op jit(solution)/shard_map/all_to_all | solution.py:544
  39.1 71.4 %copy-start.5 = (s32[96,8]{0,1:T(8,128)S(1)}, s32[96,8]{0,1:T(8,128)}, u32[]{:S(2)}) copy-start(s32[96,8]{0,1:T(8,128)} %param.8) | copy-start | bytes 9220
  39.1 71.6 %copy-start.3 = (s32[96]{0:T(128)S(1)}, s32[96]{0:T(128)}, u32[]{:S(2)}) copy-start(s32[96]{0:T(128)} %refs_0_.7) | copy-start | bytes 1156
  42.4 80.3 %copy-start.6 = (s32[96]{0:T(128)S(1)}, s32[96]{0:T(128)}, u32[]{:S(2)}) copy-start(s32[96]{0:T(128)} %param.7) | copy-start | bytes 1156
  103.8 50.2 %all-to-all-start.1 = ((bf16[128,8,1408]{2,1,0:T(8,128)(2,1)}), bf16[128,8,1408]{2,1,0:T(8,128)(2,1)S(1)}, u32[]{:S(2)}, u32[]{:S(2)}) async-start(bf16[128,8,1408]{2,1,0:T(8,128)(2,1)} %pack1.1), calls=%async_computation.1 | async-start | bytes 5767168 | tf_op jit(solution)/shard_map/all_to_all | solution.py:544
  110.7 24.3 %copy-start = (f32[96,8,128]{2,1,0:T(8,128)}, f32[96,8,128]{2,1,0:T(8,128)S(1)}, u32[]{:S(2)}) copy-start(f32[96,8,128]{2,1,0:T(8,128)S(1)} %broadcast_in_dim.10.refs_2_) | copy-start | bytes 1179652
  115.1 35.8 %collective-permute-start.3 = (bf16[12,8,2048]{2,1,0:T(8,128)(2,1)S(1)}, bf16[12,8,2048]{2,1,0:T(8,128)(2,1)S(1)}, u32[]{:S(2)}, u32[]{:S(2)}) collective-permute-start(bf16[12,8,2048]{2,1,0:T(8,128)(2,1)S(1)} %get-tuple-element.25), channel_id=1, source_target_pairs={{16,0},{32,16},{48,32},{64,48},{80,64},{96,80},{112,96},{17,1},{33... | collective-permute-start | bytes 1179656 | tf_op jit(solution)/shard_map/ppermute | solution.py:526
  117.3 33.5 %collective-permute-start.2 = (bf16[12,8,1664]{2,1,0:T(8,128)(2,1)S(1)}, bf16[12,8,1664]{2,1,0:T(8,128)(2,1)S(1)}, u32[]{:S(2)}, u32[]{:S(2)}) collective-permute-start(bf16[12,8,1664]{2,1,0:T(8,128)(2,1)S(1)} %get-tuple-element.24), channel_id=1, source_target_pairs={{1,0},{2,1},{3,2},{4,3},{5,4},{6,5},{7,6},{8,7},{9,8},{10,9},{11,1... | collective-permute-start | bytes 958472 | tf_op jit(solution)/shard_map/ppermute | solution.py:526
  122.7 28.2 %collective-permute-start = (bf16[12,8,1024]{2,1,0:T(8,128)(2,1)S(1)}, bf16[12,8,1024]{2,1,0:T(8,128)(2,1)S(1)}, u32[]{:S(2)}, u32[]{:S(2)}) collective-permute-start(bf16[12,8,1024]{2,1,0:T(8,128)(2,1)S(1)} %get-tuple-element.22), channel_id=1, source_target_pairs={{0,1},{1,2},{2,3},{3,4},{4,5},{5,6},{6,7},{7,8},{8,9},{9,10},{10,1... | collective-permute-start | bytes 589832 | tf_op jit(solution)/shard_map/ppermute | solution.py:526
  124.6 17.7 %collective-permute-start.1 = (bf16[12,8,640]{2,1,0:T(8,128)(2,1)S(1)}, bf16[12,8,640]{2,1,0:T(8,128)(2,1)S(1)}, u32[]{:S(2)}, u32[]{:S(2)}) collective-permute-start(bf16[12,8,640]{2,1,0:T(8,128)(2,1)S(1)} %get-tuple-element.23), channel_id=1, source_target_pairs={{0,16},{16,32},{32,48},{48,64},{64,80},{80,96},{96,112},{1,17},{17... | collective-permute-start | bytes 368648 | tf_op jit(solution)/shard_map/ppermute | solution.py:526
  154.0 1.0 copy-start.1
  156.4 15.5 %collective-permute-start.5 = (bf16[12,8,1408]{2,1,0:T(8,128)(2,1)S(1)}, bf16[12,8,1408]{2,1,0:T(8,128)(2,1)S(1)}, u32[]{:S(2)}, u32[]{:S(2)}) collective-permute-start(bf16[12,8,1408]{2,1,0:T(8,128)(2,1)S(1)} %get-tuple-element.29), channel_id=1, source_target_pairs={{0,16},{16,32},{32,48},{48,64},{64,80},{80,96},{96,112},{1,17},{17... | collective-permute-start | bytes 811016 | tf_op jit(solution)/shard_map/ppermute | solution.py:526
  159.3 12.6 %collective-permute-start.4 = (bf16[12,8,1024]{2,1,0:T(8,128)(2,1)S(1)}, bf16[12,8,1024]{2,1,0:T(8,128)(2,1)S(1)}, u32[]{:S(2)}, u32[]{:S(2)}) collective-permute-start(bf16[12,8,1024]{2,1,0:T(8,128)(2,1)S(1)} %get-tuple-element.28), channel_id=1, source_target_pairs={{0,1},{1,2},{2,3},{3,4},{4,5},{5,6},{6,7},{7,8},{8,9},{9,10},{10,1... | collective-permute-start | bytes 589832 | tf_op jit(solution)/shard_map/ppermute | solution.py:526
  162.8 9.1 %collective-permute-start.6 = (bf16[12,8,384]{2,1,0:T(8,128)(2,1)S(1)}, bf16[12,8,384]{2,1,0:T(8,128)(2,1)S(1)}, u32[]{:S(2)}, u32[]{:S(2)}) collective-permute-start(bf16[12,8,384]{2,1,0:T(8,128)(2,1)S(1)} %get-tuple-element.30), channel_id=1, source_target_pairs={{1,0},{2,1},{3,2},{4,3},{5,4},{6,5},{7,6},{8,7},{9,8},{10,9},{11,1... | collective-permute-start | bytes 221192 | tf_op jit(solution)/shard_map/ppermute | solution.py:526
  166.7 1.0 copy-start.2

commit v6 on v5

--- a/solution.py
+++ b/solution.py
@@ -21,26 +21,16 @@
 LOG2E = 1.0 / math.log(2.0)
 
 TILES = TOTAL // 128
-LATE = (17, 19, 21, 23, 25, 26, 27, 28, 29, 30, 31)
+LATE = tuple(range(TILES // 2 + 5, TILES, 2))
 CHUNKS = (tuple(t for t in range(TILES) if t not in LATE), LATE)
 PIECE = 16
 RELAX_VMEM = 60 << 20
-PACK_VMEM = 54 << 20
-FACES_VMEM = 16 << 20
-ADVANCE_VMEM = 28 << 20
-EDGE_VMEM = 20 << 20
+PACK_VMEM = 52 << 20
+FACES_VMEM = (12 << 20, 4 << 20)
+ADVANCE_VMEM = (20 << 20, 8 << 20)
+EDGE_VMEM = 48 << 20
 GROUP = 8
 STEP = 512
-
-
-def runs_of(chunk):
-    runs = []
-    for place, tile in enumerate(CHUNKS[chunk]):
-        if runs and runs[-1][1] + runs[-1][2] == tile:
-            runs[-1][2] += 1
-        else:
-            runs.append([place, tile, 1])
-    return runs
 
 
 def shape_of(chunk, rows=BLOCKS):
@@ -252,13 +242,12 @@
 PARTS = 4
 
 
-def face_kinds(chunk):
-    kinds = (("y", 1), ("x", 1), ("y", 0), ("x", 0))
-    return [kind for kind in kinds if face_tiles(chunk, *kind)]
-
-
-def face_shape(chunk, kind):
-    return (12, CELLS, 128 * len(face_tiles(chunk, *kind)))
+KINDS = (("y", 0), ("x", 0), ("y", 1), ("x", 1))
+FACE = (12, CELLS, TOTAL // 2)
+
+
+def kinds_of(chunk):
+    return [kind for kind in KINDS if face_tiles(chunk, *kind)]
 
 
 def face_block(axis, up, pair):
@@ -268,16 +257,15 @@
 
 
 def face_tiles(chunk, axis, up):
-    return [
-        (place, tile)
-        for place, tile in enumerate(CHUNKS[chunk])
-        if up == (tile % 2 if axis == "y" else tile // (TILES // 2))
+    whole = [
+        t for t in range(TILES) if up == (t % 2 if axis == "y" else t // (TILES // 2))
     ]
+    return [(n, CHUNKS[chunk].index(t), t) for n, t in enumerate(whole) if t in CHUNKS[chunk]]
 
 
 def write_faces(chunk, owner, received, mask, sent):
     low_x, low_y, _ = row_masks()
-    for (axis, up), face in zip(face_kinds(chunk), sent):
+    for (axis, up), face in zip(kinds_of(chunk), sent):
         low, distance = (low_x, 4) if axis == "x" else (low_y, 2)
 
         @pl.loop(0, 12)
@@ -285,7 +273,7 @@
             block = face_block(axis, up, pair)
             sources = [owner[block + side] for side in range(2)]
             masks = [mask[block + side] for side in range(2)]
-            for n, (place, _) in enumerate(face_tiles(chunk, axis, up)):
+            for n, place, _ in face_tiles(chunk, axis, up):
                 a, b = (
                     received[sources[side], :, lanes(place)].astype(jnp.float32) * masks[side]
                     for side in range(2)
@@ -297,7 +285,12 @@
 
 def faces_kernel(chunk, owner, arrived, mask, *rest):
     if chunk:
-        write_faces(chunk, owner, arrived, mask, rest)
+        kinds = kinds_of(chunk)
+        sent = rest[-len(kinds) :]
+        for kind, before, face in zip(kinds, rest, sent):
+            for n, _, _ in face_tiles(0, *kind):
+                face[:, :, lanes(n)] = before[:, :, lanes(n)]
+        write_faces(chunk, owner, arrived, mask, sent)
         return
     *sent, received, sems = rest
     part = arrived.shape[0] // PARTS
@@ -314,25 +307,28 @@
     write_faces(chunk, owner, received, mask, sent)
 
 
-def faces(chunk, owner, arrived, mask):
-    kinds = face_kinds(chunk)
-    shapes = [jax.ShapeDtypeStruct(face_shape(chunk, kind), jnp.bfloat16) for kind in kinds]
-    moved = sum(math.prod(s.shape) for s in shapes)
+def faces(chunk, owner, arrived, mask, earlier, after_this):
+    extra = after_this
+    n = len(kinds_of(chunk))
+    shapes = [jax.ShapeDtypeStruct(FACE, jnp.bfloat16)] * n
+    moved = n * math.prod(FACE) * len(CHUNKS[chunk]) // TILES
     if chunk == 0:
         shapes.append(jax.ShapeDtypeStruct(arrived.shape, arrived.dtype))
     made = pl.pallas_call(
         lambda *refs: faces_kernel(chunk, *refs),
         out_shape=shapes,
-        in_specs=[pl.BlockSpec(memory_space=pltpu.SMEM), VMEM if chunk else ANY, VMEM],
+        in_specs=[pl.BlockSpec(memory_space=pltpu.SMEM), VMEM if chunk else ANY]
+        + [VMEM] * (1 + len(earlier))
+        + [ANY] * len(extra),
         out_specs=[VMEM] * len(shapes),
         scratch_shapes=[] if chunk else [pltpu.SemaphoreType.DMA((PARTS,))],
-        compiler_params=pltpu.CompilerParams(vmem_limit_bytes=FACES_VMEM),
+        compiler_params=pltpu.CompilerParams(vmem_limit_bytes=FACES_VMEM[chunk]),
         cost_estimate=pl.CostEstimate(
             flops=8 * moved, bytes_accessed=4 * moved, transcendentals=0
         ),
         name=f"faces{chunk}",
-    )(owner, arrived, mask)
-    return made[: len(kinds)], arrived if chunk else made[-1]
+    )(owner, arrived, mask, *earlier, *extra)
+    return made[:n], arrived if chunk else made[-1]
 
 
 def speeds():
@@ -349,7 +345,8 @@
     return SPACING * abs(2 * (tile // 2) + 1 - VS)
 
 
-def advance_kernel(chunk, owner, received, mask, rate, partial, kept):
+def advance_kernel(chunk, owner, received, mask, rate, partial, done, kept):
+    done[...] = jnp.zeros_like(done)
     low_x, low_y, low_z = row_masks()
     speed_y, speed_z, rising_z = speeds()
     from_below = rising_z & ~low_z
@@ -411,21 +408,38 @@
     shape = shape_of(chunk)
     return pl.pallas_call(
         lambda *refs: advance_kernel(chunk, *refs),
-        out_shape=jax.ShapeDtypeStruct(shape, jnp.float32),
+        out_shape=[
+            jax.ShapeDtypeStruct(shape, jnp.float32),
+            jax.ShapeDtypeStruct((8, 128), jnp.float32),
+        ],
         in_specs=[pl.BlockSpec(memory_space=pltpu.SMEM)] + [VMEM] * 3,
-        out_specs=VMEM,
+        out_specs=[VMEM] * 2,
         scratch_shapes=[pltpu.VMEM((BLOCKS + 1, *shape[1:]), jnp.float32)],
-        compiler_params=pltpu.CompilerParams(vmem_limit_bytes=ADVANCE_VMEM),
+        compiler_params=pltpu.CompilerParams(vmem_limit_bytes=ADVANCE_VMEM[chunk]),
         cost_estimate=pl.CostEstimate(
-            flops=100 * math.prod(shape), bytes_accessed=6 * math.prod(shape), transcendentals=0
+            flops=(100, 1)[chunk] * math.prod(shape),
+            bytes_accessed=(6, 1)[chunk] * math.prod(shape),
+            transcendentals=0,
         ),
         name=f"advance{chunk}",
     )(owner, received, mask, rate)
 
 
-def edge_kernel(chunk, _, rate, *rest):
-    kinds = face_kinds(chunk)
-    halos, (out, partial, made, sems) = rest[: len(kinds)], rest[-4:]
+def edge_kernel(rate, *rest):
+    n = len(CHUNKS)
+    sources, halos, out, partials = rest[:n], rest[n : n + 4], rest[n + 4], rest[n + 5 : 2 * n + 5]
+    made, in_sems, sems = rest[2 * n + 5 :]
+
+    def arrivals(bx):
+        rows = pl.ds(bx * SLAB, SLAB)
+        return [
+            pltpu.make_async_copy(source.at[rows], partial.at[rows], in_sems.at[bx, c])
+            for c, (source, partial) in enumerate(zip(sources, partials))
+        ]
+
+    for bx in range(BX):
+        for copy in arrivals(bx):
+            copy.start()
     low_x, low_y, _ = row_masks()
     speed_y, _, _ = speeds()
 
@@ -437,7 +451,10 @@
         @pl.loop(*slots)
         def _(pair):
             block = face_block(axis, 1 - up, pair)
-            for n, (place, tile) in enumerate(face_tiles(chunk, *kind)):
+            for chunk, n, place, tile in [
+                (c, *found) for c in range(len(CHUNKS)) for found in face_tiles(c, *kind)
+            ]:
+                partial = partials[chunk]
                 face = halo[pair, :, lanes(n)].astype(jnp.float32)
                 speed = speed_x(tile) if axis == "x" else speed_y[up]
                 other = swap(face, distance)
@@ -447,19 +464,14 @@
                     partial_at = (block + side, slice(None), lanes(place))
                     partial[partial_at] = partial[partial_at] + gain
 
-    def result_copies(bx):
+    def result_copy(bx):
         rows = pl.ds(bx * SLAB, SLAB)
-        return [
-            pltpu.make_async_copy(
-                made.at[rows, :, pl.ds(place * 128, length * 128)],
-                out.at[rows, :, pl.ds(tile * 128, length * 128)],
-                sems.at[bx, n],
-            )
-            for n, (place, tile, length) in enumerate(runs_of(chunk))
-        ]
+        return pltpu.make_async_copy(made.at[rows], out.at[rows], sems.at[bx])
 
     for bx in range(BX):
-        for kind, halo in zip(kinds, halos):
+        for copy in arrivals(bx):
+            copy.wait()
+        for kind, halo in zip(KINDS, halos):
             if kind[0] == "y":
                 add(kind, halo, (3 * bx, 3 * bx + 3))
             elif bx == (0 if kind[1] else BX - 1):
@@ -467,38 +479,35 @@
 
         @pl.loop(bx * SLAB, bx * SLAB + SLAB)
         def _(block):
-            made[block] = partial[block].astype(jnp.bfloat16)
-
-        for copy in result_copies(bx):
-            copy.start()
+            for chunk, partial in enumerate(partials):
+                for place, tile in enumerate(CHUNKS[chunk]):
+                    made[block, :, lanes(tile)] = partial[block, :, lanes(place)].astype(
+                        jnp.bfloat16
+                    )
+
+        result_copy(bx).start()
     for bx in range(BX):
-        for copy in result_copies(bx):
-            copy.wait()
-
-
-def edge(chunk, partial, rate, halos, earlier):
-    shape = shape_of(chunk)
-    extra = [] if earlier is None else [earlier]
-    out, _ = pl.pallas_call(
-        lambda *refs: edge_kernel(chunk, *refs),
-        out_shape=[
-            jax.ShapeDtypeStruct(WHOLE, jnp.bfloat16),
-            jax.ShapeDtypeStruct(shape, jnp.float32),
+        result_copy(bx).wait()
+
+
+def edge(rate, partials, halos):
+    return pl.pallas_call(
+        edge_kernel,
+        out_shape=jax.ShapeDtypeStruct(WHOLE, jnp.bfloat16),
+        in_specs=[VMEM] + [ANY] * len(partials) + [VMEM] * len(halos),
+        out_specs=ANY,
+        scratch_shapes=[pltpu.VMEM(p.shape, p.dtype) for p in partials]
+        + [
+            pltpu.VMEM(WHOLE, jnp.bfloat16),
+            pltpu.SemaphoreType.DMA((BX, len(partials))),
+            pltpu.SemaphoreType.DMA((BX,)),
         ],
-        in_specs=[VMEM] * (2 + len(halos)) + [ANY] * len(extra),
-        out_specs=[ANY, VMEM],
-        scratch_shapes=[
-            pltpu.VMEM(shape, jnp.bfloat16),
-            pltpu.SemaphoreType.DMA((BX, len(runs_of(chunk)))),
-        ],
-        input_output_aliases={0: 1} | ({} if earlier is None else {2 + len(halos): 0}),
         compiler_params=pltpu.CompilerParams(vmem_limit_bytes=EDGE_VMEM),
         cost_estimate=pl.CostEstimate(
-            flops=4 * math.prod(shape), bytes_accessed=6 * math.prod(shape), transcendentals=0
+            flops=4 * math.prod(WHOLE), bytes_accessed=6 * math.prod(WHOLE), transcendentals=0
         ),
-        name=f"edge{chunk}",
-    )(partial, rate, *halos, *extra)
-    return out
+        name="edge",
+    )(rate, *partials, *halos)
 
 
 def after(received, source_owner, levels, active):
@@ -515,18 +524,24 @@
     def down(n):
         return [(i + 1, i) for i in range(n - 1)]
 
-    out = None
+    def exchange(kind):
+        axis, to_above = kind
+        name, n = ("gx", n_gx) if axis == "x" else ("gy", n_gy)
+        return lax.ppermute(sent[kind], name, up(n) if to_above else down(n))
+
+    partials, sent, halos, done = [], {}, {}, []
     for chunk, arrived in enumerate(received):
-        if out is not None:
-            arrived, out = lax.optimization_barrier((arrived, out))
-        sent, arrived = faces(chunk, source_owner, arrived, mask)
-        halos = []
-        for (axis, to_above), face in zip(face_kinds(chunk), sent):
-            name, n = ("gx", n_gx) if axis == "x" else ("gy", n_gy)
-            halos.append(lax.ppermute(face, name, up(n) if to_above else down(n)))
-        partial = advance(chunk, source_owner, arrived, mask, rate)
-        out = edge(chunk, partial, rate, halos, out)
-    return out
+        kinds = kinds_of(chunk)
+        earlier = [sent[kind] for kind in kinds if kind in sent]
+        made, arrived = faces(chunk, source_owner, arrived, mask, earlier, done)
+        sent.update(zip(kinds, made))
+        for kind in kinds:
+            if not any(kind in kinds_of(later) for later in range(chunk + 1, len(CHUNKS))):
+                halos[kind] = exchange(kind)
+        partial, token = advance(chunk, source_owner, arrived, mask, rate)
+        partials.append(partial)
+        done = [token, *halos.values()]
+    return edge(rate, partials, [halos[kind] for kind in KINDS])
 
 
 def per_device(dist_old, source_owner, levels, active):

time: 176 us -> 180 us (1.023)
  starting transfers between devices: 50.9 us -> 42.5 us
  waiting for transfers between devices: 77.3 us -> 84.1 us
  Pallas kernels: 41.2 us -> 44.3 us
  local copies, waits for them, and re-layouts: 3.7 us -> 6.61 us
    all_to_all x2, waiting for transfers between devices: 61.5 us -> 78.1 us  [per_device(): lax.all_to_all(pack(chunk, asked, relaxed), axes, split_axis=0, concat_ax...]
    ppermute x7 -> x4, waiting for transfers between devices: 15.8 us -> 6.01 us  [exchange(): return lax.ppermute(sent[kind], name, up(n) if to_above else down(n))]
    ppermute x7 -> x4, starting transfers between devices: 23.3 us -> 14.5 us  [exchange(): return lax.ppermute(sent[kind], name, up(n) if to_above else down(n))]
    unnamed x14 -> x18, local copies, waits for them, and re-layouts: 2.62 us -> 5.53 us
    pallas_call x4 -> x3, Pallas kernels: 16.4 us -> 18.4 us  [the longest x2 11.2 us: advance(): pl.pallas_call(lambda *refs: advance_kernel(chunk, *refs), out_shape=[jax...]
  transfers between devices with their start and end apart: 10 -> 7, of which waited for: 3 -> 3; matrix products, arithmetic and copies ran while one was open for 0% -> 0% of each run, Pallas kernels for 19% -> 18%
where the time goes in v6:
time: 180 us; the launch traced here: 179 us
  waiting for transfers between devices  84.1 us (47%)
  Pallas kernels  44.3 us (25%)
  starting transfers between devices  42.5 us (24%)
  local copies, waits for them, and re-layouts  6.61 us (4%)
    all_to_all x2, waiting for transfers between devices, per_device(): lax.all_to_all(pack(chunk, asked, relaxed), axes, split_axis=0, concat_ax...  78.1 us
    all_to_all x2, starting transfers between devices, per_device(): lax.all_to_all(pack(chunk, asked, relaxed), axes, split_axis=0, concat_ax...  17.3 us
    ppermute x4, starting transfers between devices, exchange(): return lax.ppermute(sent[kind], name, up(n) if to_above else down(n))  14.5 us
    pallas_call x1, Pallas kernels, relax(): pl.pallas_call(relax_kernel, out_shape=[jax.ShapeDtypeStruct(shape_of(c),...  11.6 us
    pallas_call x2, Pallas kernels, advance(): pl.pallas_call(lambda *refs: advance_kernel(chunk, *refs), out_shape=[jax...  11.2 us
    all_to_all x1, starting transfers between devices, per_device(): lax.all_to_all(jnp.broadcast_to(request, (devices, 128)), axes, split_axi...  10.8 us
    pallas_call x2, Pallas kernels, pack(): pl.pallas_call(pack_kernel, out_shape=jax.ShapeDtypeStruct(shape_of(chunk...  7.49 us
    pallas_call x1, Pallas kernels, edge(): pl.pallas_call(edge_kernel, out_shape=jax.ShapeDtypeStruct(WHOLE, jnp.bfl...  7.18 us
  transfers between devices with their start and end apart: 7, of which 3 were waited for; matrix products, arithmetic and copies ran while one was open for 0% of the time, Pallas kernels for 18%

profile of v6, /device:TPU:7, one launch (start us, length us, event | category | flops | bytes accessed | tf_op | source)
XLA Modules:
  0.0 178.8 jit_solution(7239716671817234793)
XLA Ops:
  0.0 0.8 select_reduce_fusion
  0.8 0.8 broadcast_in_dim.10
  1.6 10.8 %all-to-all-start = ((s32[128,1,128]{2,1,0:T(1,128)}), s32[128,1,128]{2,1,0:T(1,128)S(1)}, u32[]{:S(2)}, u32[]{:S(2)}) async-start(s32[128,1,128]{2,1,0:T(1,128)} %broadcast_in_dim.10), calls=%async_computation | async-start | bytes 131072 | tf_op jit(solution)/shard_map/all_to_all | solution.py:555
  12.4 11.6 %relax.1 = (bf16[96,8,3328]{2,1,0:T(8,128)(2,1)}, bf16[96,8,768]{2,1,0:T(8,128)(2,1)}) custom-call(bf16[96,8,4096]{2,1,0:T(8,128)(2,1)} %dist.1, bf16[48,4096]{1,0:T(8,128)(2,1)} %constant.13.clone.basis), custom_call_target="tpu_custom_call" | custom-call | flops 9437184000 | bytes 12582912 | tf_op jit(solution)/shard_map/relax/pallas_call | solution.py:162
  24.0 4.3 %pack0.1 = bf16[128,8,3328]{2,1,0:T(8,128)(2,1)} custom-call(s32[128,128]{1,0:T(8,128)S(1)} %bitcast.1, bf16[96,8,3328]{2,1,0:T(8,128)(2,1)} %get-tuple-element.17.relaxed), custom_call_target="tpu_custom_call" | custom-call | bytes 10223616 | tf_op jit(solution)/shard_map/pack0/pallas_call | solution.py:209
  28.4 10.2 %all-to-all-start.1 = ((bf16[128,8,3328]{2,1,0:T(8,128)(2,1)}), bf16[128,8,3328]{2,1,0:T(8,128)(2,1)}, u32[]{:S(2)}, u32[]{:S(2)}) async-start(bf16[128,8,3328]{2,1,0:T(8,128)(2,1)} %pack0.1), calls=%async_computation.1 | async-start | bytes 13631488 | tf_op jit(solution)/shard_map/all_to_all | solution.py:559
  38.6 3.2 %pack1.1 = bf16[128,8,768]{2,1,0:T(8,128)(2,1)} custom-call(s32[128,128]{1,0:T(8,128)S(1)} %bitcast.2, bf16[96,8,768]{2,1,0:T(8,128)(2,1)S(1)} %copy-done.1), custom_call_target="tpu_custom_call" | custom-call | bytes 2359296 | tf_op jit(solution)/shard_map/pack1/pallas_call | solution.py:209
  41.8 78.1 %all-to-all-done.1.refs_1_ = bf16[128,8,3328]{2,1,0:T(8,128)(2,1)} async-done(((bf16[128,8,3328]{2,1,0:T(8,128)(2,1)}), bf16[128,8,3328]{2,1,0:T(8,128)(2,1)}, u32[]{:S(2)}, u32[]{:S(2)}) %all-to-all-start.1) | async-done | bytes 6815776 | tf_op jit(solution)/shard_map/all_to_all | solution.py:559
  119.9 7.1 %all-to-all-start.2 = ((bf16[128,8,768]{2,1,0:T(8,128)(2,1)}), bf16[128,8,768]{2,1,0:T(8,128)(2,1)S(1)}, u32[]{:S(2)}, u32[]{:S(2)}) async-start(bf16[128,8,768]{2,1,0:T(8,128)(2,1)} %pack1.1), calls=%async_computation.2 | async-start | bytes 3145728 | tf_op jit(solution)/shard_map/all_to_all | solution.py:559
  127.1 0.6 copy-done.5
  127.9 5.7 %faces0.1 = (bf16[12,8,2048]{2,1,0:T(8,128)(2,1)}, bf16[12,8,2048]{2,1,0:T(8,128)(2,1)}, bf16[12,8,2048]{2,1,0:T(8,128)(2,1)S(1)}, bf16[12,8,2048]{2,1,0:T(8,128)(2,1)S(1)}, bf16[128,8,3328]{2,1,0:T(8,128)(2,1)S(1)}) custom-call(s32[96]{0:T(128)S(1)} %copy-done.4, bf16[128,8,3328]{2,1,0:T(8,128)(2,1)} %all-to-all-done.1.refs_1_, ...), custom_call_target="tpu_custom_call" | custom-call | flops 5111808 | bytes 2555904 | tf_op jit(solution)/shard_map/faces0/pallas_call | solution.py:317
  133.6 5.3 %collective-permute-start = (bf16[12,8,2048]{2,1,0:T(8,128)(2,1)}, bf16[12,8,2048]{2,1,0:T(8,128)(2,1)S(1)}, u32[]{:S(2)}, u32[]{:S(2)}) collective-permute-start(bf16[12,8,2048]{2,1,0:T(8,128)(2,1)} %get-tuple-element.22), channel_id=1, source_target_pairs={{1,0},{2,1},{3,2},{4,3},{5,4},{6,5},{7,6},{8,7},{9,8},{10,9},{11,1... | collective-permute-start | bytes 1179656 | tf_op jit(solution)/shard_map/ppermute | solution.py:530
  138.9 2.5 %collective-permute-start.1 = (bf16[12,8,2048]{2,1,0:T(8,128)(2,1)}, bf16[12,8,2048]{2,1,0:T(8,128)(2,1)S(1)}, u32[]{:S(2)}, u32[]{:S(2)}) collective-permute-start(bf16[12,8,2048]{2,1,0:T(8,128)(2,1)} %get-tuple-element.23), channel_id=1, source_target_pairs={{16,0},{32,16},{48,32},{64,48},{80,64},{96,80},{112,96},{17,1},{33... | collective-permute-start | bytes 1179656 | tf_op jit(solution)/shard_map/ppermute | solution.py:530
  141.5 0.3 broadcast_multiply_fusion.refs_3_.rate
  141.8 7.7 %advance0.1 = (f32[96,8,3328]{2,1,0:T(8,128)S(1)}, f32[8,128]{1,0:T(8,128)S(1)}) custom-call(s32[96]{0:T(128)S(1)} %copy-done.4, bf16[128,8,3328]{2,1,0:T(8,128)(2,1)S(1)} %get-tuple-element.18.refs_1_, f32[96,8,128]{2,1,0:T(8,128)S(1)} %broadcast_in_dim.8.refs_2_, f32[96,8,128]{2,1,0:T(8,128)S(1)} %broadcast_multiply_fusion.refs_3_.rate), custom_call_target="tpu_custom_call" | custom-call | flops 255590400 | bytes 15335424 | tf_op jit(solution)/shard_map/advance0/pallas_call | solution.py:409
  149.5 3.9 %copy-done = f32[96,8,3328]{2,1,0:T(8,128)} copy-done((f32[96,8,3328]{2,1,0:T(8,128)}, f32[96,8,3328]{2,1,0:T(8,128)S(1)}, u32[]{:S(2)}) %copy-start) | copy-done | bytes 10223640
  153.4 1.8 %collective-permute-done.refs_6_.rest_2_ = bf16[12,8,2048]{2,1,0:T(8,128)(2,1)S(1)} collective-permute-done((bf16[12,8,2048]{2,1,0:T(8,128)(2,1)}, bf16[12,8,2048]{2,1,0:T(8,128)(2,1)S(1)}, u32[]{:S(2)}, u32[]{:S(2)}) %collective-permute-start) | collective-permute-done | bytes 393248 | tf_op jit(solution)/shard_map/ppermute | solution.py:530
  155.3 1.0 copy-done.3
  156.3 1.1 faces1.1
  157.3 3.7 %collective-permute-start.2 = (bf16[12,8,2048]{2,1,0:T(8,128)(2,1)S(1)}, bf16[12,8,2048]{2,1,0:T(8,128)(2,1)S(1)}, u32[]{:S(2)}, u32[]{:S(2)}) collective-permute-start(bf16[12,8,2048]{2,1,0:T(8,128)(2,1)S(1)} %get-tuple-element.27), channel_id=1, source_target_pairs={{0,1},{1,2},{2,3},{3,4},{4,5},{5,6},{6,7},{7,8},{8,9},{9,10},{10,1... | collective-permute-start | bytes 1179656 | tf_op jit(solution)/shard_map/ppermute | solution.py:530
  161.0 2.9 %collective-permute-start.3 = (bf16[12,8,2048]{2,1,0:T(8,128)(2,1)S(1)}, bf16[12,8,2048]{2,1,0:T(8,128)(2,1)S(1)}, u32[]{:S(2)}, u32[]{:S(2)}) collective-permute-start(bf16[12,8,2048]{2,1,0:T(8,128)(2,1)S(1)} %get-tuple-element.28), channel_id=1, source_target_pairs={{0,16},{16,32},{32,48},{48,64},{64,80},{80,96},{96,112},{1,17},{17... | collective-permute-start | bytes 1179656 | tf_op jit(solution)/shard_map/ppermute | solution.py:530
  164.0 3.5 %advance1.1 = (f32[96,8,768]{2,1,0:T(8,128)S(1)}, f32[8,128]{1,0:T(8,128)}) custom-call(s32[96]{0:T(128)S(1)} %copy-done.4, bf16[128,8,768]{2,1,0:T(8,128)(2,1)S(1)} %all-to-all-done.2.refs_1_, f32[96,8,128]{2,1,0:T(8,128)S(1)} %broadcast_in_dim.8.refs_2_, f32[96,8,128]{2,1,0:T(8,128)S(1)} %broadcast_multiply_fusion.refs_3_.rate), custom_call_target="tpu_custom_call" | custom-call | flops 589824 | bytes 589824 | tf_op jit(solution)/shard_map/advance1/pallas_call | solution.py:409
  167.5 4.2 %collective-permute-done.2.rest_4_ = bf16[12,8,2048]{2,1,0:T(8,128)(2,1)S(1)} collective-permute-done((bf16[12,8,2048]{2,1,0:T(8,128)(2,1)S(1)}, bf16[12,8,2048]{2,1,0:T(8,128)(2,1)S(1)}, u32[]{:S(2)}, u32[]{:S(2)}) %collective-permute-start.2) | collective-permute-done | bytes 393248 | tf_op jit(solution)/shard_map/ppermute | solution.py:530
  171.6 7.2 %edge.1 = bf16[96,8,4096]{2,1,0:T(8,128)(2,1)} custom-call(f32[96,8,128]{2,1,0:T(8,128)S(1)} %broadcast_multiply_fusion.refs_3_.rate, f32[96,8,3328]{2,1,0:T(8,128)} %copy-done, f32[96,8,768]{2,1,0:T(8,128)S(1)} %get-tuple-element.21.rest_1_, bf16[12,8,2048]{2,1,0:T(8,128)(2,1)S(1)} %collective-permute-done.refs_6_.rest_2_, ...), custom_call_target="tpu_custom_call" | custom-call | flops 12582912 | bytes 18874368 | tf_op jit(solution)/shard_map/edge/pallas_call | solution.py:494
  (25 shorter events, 0.3 us)
Async XLA Ops:
  1.6 22.4 %all-to-all-start = ((s32[128,1,128]{2,1,0:T(1,128)}), s32[128,1,128]{2,1,0:T(1,128)S(1)}, u32[]{:S(2)}, u32[]{:S(2)}) async-start(s32[128,1,128]{2,1,0:T(1,128)} %broadcast_in_dim.10), calls=%async_computation | async-start | bytes 131072 | tf_op jit(solution)/shard_map/all_to_all | solution.py:555
  28.4 10.2 %copy-start.1 = (bf16[96,8,768]{2,1,0:T(8,128)(2,1)S(1)}, bf16[96,8,768]{2,1,0:T(8,128)(2,1)}, u32[]{:S(2)}) copy-start(bf16[96,8,768]{2,1,0:T(8,128)(2,1)} %get-tuple-element.20.relaxed) | copy-start | bytes 3538948
  28.4 98.6 %copy-start.7 = (s32[96,8]{0,1:T(8,128)S(1)}, s32[96,8]{0,1:T(8,128)}, u32[]{:S(2)}) copy-start(s32[96,8]{0,1:T(8,128)} %param.8) | copy-start | bytes 9220
  28.4 91.5 %all-to-all-start.1 = ((bf16[128,8,3328]{2,1,0:T(8,128)(2,1)}), bf16[128,8,3328]{2,1,0:T(8,128)(2,1)}, u32[]{:S(2)}, u32[]{:S(2)}) async-start(bf16[128,8,3328]{2,1,0:T(8,128)(2,1)} %pack0.1), calls=%async_computation.1 | async-start | bytes 13631488 | tf_op jit(solution)/shard_map/all_to_all | solution.py:559
  38.6 89.3 %copy-start.4 = (s32[96]{0:T(128)S(1)}, s32[96]{0:T(128)}, u32[]{:S(2)}) copy-start(s32[96]{0:T(128)} %refs_0_.7) | copy-start | bytes 1156
  38.6 102.9 %copy-start.8 = (s32[96]{0:T(128)S(1)}, s32[96]{0:T(128)}, u32[]{:S(2)}) copy-start(s32[96]{0:T(128)} %param.7) | copy-start | bytes 1156
  119.9 33.6 %all-to-all-start.2 = ((bf16[128,8,768]{2,1,0:T(8,128)(2,1)}), bf16[128,8,768]{2,1,0:T(8,128)(2,1)S(1)}, u32[]{:S(2)}, u32[]{:S(2)}) async-start(bf16[128,8,768]{2,1,0:T(8,128)(2,1)} %pack1.1), calls=%async_computation.2 | async-start | bytes 3145728 | tf_op jit(solution)/shard_map/all_to_all | solution.py:559
  127.1 0.6 copy-start.5
  127.9 13.6 %copy-start.6 = (f32[96,8]{1,0:T(8,128)S(1)}, f32[96,8]{1,0:T(8,128)}, u32[]{:S(2)}) copy-start(f32[96,8]{1,0:T(8,128)} %copy-done.5) | copy-start | bytes 9220
  133.6 8.2 %copy-start.2 = (bf16[12,8,2048]{2,1,0:T(8,128)(2,1)}, bf16[12,8,2048]{2,1,0:T(8,128)(2,1)S(1)}, u32[]{:S(2)}) copy-start(bf16[12,8,2048]{2,1,0:T(8,128)(2,1)S(1)} %get-tuple-element.25.refs_4_) | copy-start | bytes 1179652
  133.6 21.6 %collective-permute-start = (bf16[12,8,2048]{2,1,0:T(8,128)(2,1)}, bf16[12,8,2048]{2,1,0:T(8,128)(2,1)S(1)}, u32[]{:S(2)}, u32[]{:S(2)}) collective-permute-start(bf16[12,8,2048]{2,1,0:T(8,128)(2,1)} %get-tuple-element.22), channel_id=1, source_target_pairs={{1,0},{2,1},{3,2},{4,3},{5,4},{6,5},{7,6},{8,7},{9,8},{10,9},{11,1... | collective-permute-start | bytes 1179656 | tf_op jit(solution)/shard_map/ppermute | solution.py:530
  138.9 16.4 %collective-permute-start.1 = (bf16[12,8,2048]{2,1,0:T(8,128)(2,1)}, bf16[12,8,2048]{2,1,0:T(8,128)(2,1)S(1)}, u32[]{:S(2)}, u32[]{:S(2)}) collective-permute-start(bf16[12,8,2048]{2,1,0:T(8,128)(2,1)} %get-tuple-element.23), channel_id=1, source_target_pairs={{16,0},{32,16},{48,32},{64,48},{80,64},{96,80},{112,96},{17,1},{33... | collective-permute-start | bytes 1179656 | tf_op jit(solution)/shard_map/ppermute | solution.py:530
  149.5 3.9 %copy-start = (f32[96,8,3328]{2,1,0:T(8,128)}, f32[96,8,3328]{2,1,0:T(8,128)S(1)}, u32[]{:S(2)}) copy-start(f32[96,8,3328]{2,1,0:T(8,128)S(1)} %get-tuple-element.19.rest_0_) | copy-start | bytes 30670852
  155.3 1.0 copy-start.3
  157.3 14.3 %collective-permute-start.2 = (bf16[12,8,2048]{2,1,0:T(8,128)(2,1)S(1)}, bf16[12,8,2048]{2,1,0:T(8,128)(2,1)S(1)}, u32[]{:S(2)}, u32[]{:S(2)}) collective-permute-start(bf16[12,8,2048]{2,1,0:T(8,128)(2,1)S(1)} %get-tuple-element.27), channel_id=1, source_target_pairs={{0,1},{1,2},{2,3},{3,4},{4,5},{5,6},{6,7},{7,8},{8,9},{9,10},{10,1... | collective-permute-start | bytes 1179656 | tf_op jit(solution)/shard_map/ppermute | solution.py:530
  161.0 10.6 %collective-permute-start.3 = (bf16[12,8,2048]{2,1,0:T(8,128)(2,1)S(1)}, bf16[12,8,2048]{2,1,0:T(8,128)(2,1)S(1)}, u32[]{:S(2)}, u32[]{:S(2)}) collective-permute-start(bf16[12,8,2048]{2,1,0:T(8,128)(2,1)S(1)} %get-tuple-element.28), channel_id=1, source_target_pairs={{0,16},{16,32},{32,48},{48,64},{64,80},{80,96},{96,112},{1,17},{17... | collective-permute-start | bytes 1179656 | tf_op jit(solution)/shard_map/ppermute | solution.py:530

commit v7 on v3

--- a/solution.py
+++ b/solution.py
@@ -22,12 +22,12 @@
 
 TILES = TOTAL // 128
 PIECE = 16
-RELAX_VMEM = 60 << 20
-PACK_VMEM = 54 << 20
+RELAX_VMEM = 56 << 20
+PACK_VMEM = 49 << 20
 FACES_VMEM = 16 << 20
 ADVANCE_VMEM = 28 << 20
 EDGE_VMEM = 20 << 20
-GROUP = 8
+GROUP = 16
 STEP = 512
 
 
@@ -81,7 +81,7 @@
     return [LOG2E * r for r in rows], fraction
 
 
-def relax_kernel(dist, basis, out, held, relaxed, sums, factors, in_sems, out_sem):
+def moments_kernel(dist, basis, factors, held, sums, in_sems):
     pieces = BLOCKS // PIECE
 
     def arrival(piece):
@@ -117,9 +117,55 @@
     )
     factors[...] = stacked.T
 
+
+VMEM = pl.BlockSpec(memory_space=pltpu.VMEM)
+ANY = pl.BlockSpec(memory_space=pl.ANY)
+WHOLE = (BLOCKS, CELLS, TOTAL)
+
+
+def moments(dist, basis):
+    return pl.pallas_call(
+        moments_kernel,
+        out_shape=jax.ShapeDtypeStruct((BLOCKS * CELLS, 128), jnp.float32),
+        in_specs=[ANY, VMEM],
+        out_specs=VMEM,
+        scratch_shapes=[
+            pltpu.VMEM(WHOLE, jnp.bfloat16),
+            pltpu.VMEM((16, BLOCKS * CELLS), jnp.float32),
+            pltpu.SemaphoreType.DMA((BLOCKS // PIECE,)),
+        ],
+        compiler_params=pltpu.CompilerParams(vmem_limit_bytes=RELAX_VMEM),
+        cost_estimate=pl.CostEstimate(
+            flops=2 * BLOCKS * CELLS * TOTAL * 1500,
+            bytes_accessed=2 * BLOCKS * CELLS * TOTAL,
+            transcendentals=0,
+        ),
+        name="moments",
+    )(dist, basis)
+
+
+def relax_kernel(
+    asked, dist, basis, factors, send, held, relaxed, row, target, row_sem, in_sems, out_sem
+):
+    def arrival(group):
+        rows = pl.ds(group * GROUP, GROUP)
+        return pltpu.make_async_copy(dist.at[rows], held.at[rows], in_sems.at[group])
+
+    for group in range(BLOCKS // GROUP):
+        arrival(group).start()
+    device = lax.broadcasted_iota(jnp.int32, asked.shape, 0)
+    slot = lax.broadcasted_iota(jnp.int32, asked.shape, 1)
+    row[...] = jnp.broadcast_to(
+        jnp.sum(jnp.where(asked[...] == slot, device, 0), axis=0, keepdims=True), row.shape
+    )
+    to_scalars = pltpu.make_async_copy(row, target, row_sem)
+    to_scalars.start()
+    to_scalars.wait()
+
     @pl.loop(0, BLOCKS // GROUP)
     def _(group):
         first = group * GROUP
+        arrival(group).wait()
         own = factors[pl.ds(pl.multiple_of(first * CELLS, GROUP * CELLS), GROUP * CELLS), :]
         left = own[:, :48].astype(jnp.bfloat16)
         fraction = jnp.broadcast_to(own[:, 48:49], (GROUP * CELLS, 128))
@@ -136,84 +182,38 @@
                 relaxed[pl.ds(first, GROUP), :, place] = mixed.reshape(
                     GROUP, CELLS, 128
                 ).astype(jnp.bfloat16)
-        rows = pl.ds(first, GROUP)
-        pltpu.make_async_copy(relaxed.at[rows], out.at[rows], out_sem).start()
-
-    pltpu.make_async_copy(relaxed, out, out_sem).wait()
-
-
-VMEM = pl.BlockSpec(memory_space=pltpu.VMEM)
-ANY = pl.BlockSpec(memory_space=pl.ANY)
-WHOLE = (BLOCKS, CELLS, TOTAL)
-
-
-def relax(dist):
+        for block in range(GROUP):
+            pltpu.make_async_copy(
+                relaxed.at[first + block], send.at[target[0, first + block]], out_sem
+            ).start()
+
+    pltpu.make_async_copy(relaxed, send.at[pl.ds(0, BLOCKS)], out_sem).wait()
+
+
+def relax(asked, dist, basis, factors):
+    devices = asked.shape[0]
     return pl.pallas_call(
         relax_kernel,
-        out_shape=jax.ShapeDtypeStruct(WHOLE, jnp.bfloat16),
-        in_specs=[ANY, VMEM],
+        out_shape=jax.ShapeDtypeStruct((devices, CELLS, TOTAL), jnp.bfloat16),
+        in_specs=[VMEM, ANY, VMEM, VMEM],
         out_specs=ANY,
         scratch_shapes=[
             pltpu.VMEM(WHOLE, jnp.bfloat16),
             pltpu.VMEM(WHOLE, jnp.bfloat16),
-            pltpu.VMEM((16, BLOCKS * CELLS), jnp.float32),
-            pltpu.VMEM((BLOCKS * CELLS, 128), jnp.float32),
-            pltpu.SemaphoreType.DMA((BLOCKS // PIECE,)),
-            pltpu.SemaphoreType.DMA(()),
-        ],
-        compiler_params=pltpu.CompilerParams(vmem_limit_bytes=RELAX_VMEM),
-        cost_estimate=pl.CostEstimate(
-            flops=2 * BLOCKS * CELLS * TOTAL * 1500,
-            bytes_accessed=4 * BLOCKS * CELLS * TOTAL,
-            transcendentals=BLOCKS * CELLS * TOTAL,
-        ),
-        name="relax",
-    )(dist, basis_rows())
-
-
-def pack_kernel(asked, relaxed, send, held, row, target, row_sem, in_sems, out_sem):
-    def arrival(piece):
-        rows = pl.ds(piece * PIECE, PIECE)
-        return pltpu.make_async_copy(relaxed.at[rows], held.at[rows], in_sems.at[piece])
-
-    for piece in range(BLOCKS // PIECE):
-        arrival(piece).start()
-    device = lax.broadcasted_iota(jnp.int32, asked.shape, 0)
-    slot = lax.broadcasted_iota(jnp.int32, asked.shape, 1)
-    row[...] = jnp.broadcast_to(
-        jnp.sum(jnp.where(asked[...] == slot, device, 0), axis=0, keepdims=True), row.shape
-    )
-    to_scalars = pltpu.make_async_copy(row, target, row_sem)
-    to_scalars.start()
-    to_scalars.wait()
-    for piece in range(BLOCKS // PIECE):
-        arrival(piece).wait()
-        for block in range(piece * PIECE, piece * PIECE + PIECE):
-            pltpu.make_async_copy(held.at[block], send.at[target[0, block]], out_sem).start()
-    pltpu.make_async_copy(held, send.at[pl.ds(0, BLOCKS)], out_sem).wait()
-
-
-def pack(asked, relaxed):
-    devices = asked.shape[0]
-    return pl.pallas_call(
-        pack_kernel,
-        out_shape=jax.ShapeDtypeStruct((devices, CELLS, TOTAL), jnp.bfloat16),
-        in_specs=[VMEM, ANY],
-        out_specs=ANY,
-        scratch_shapes=[
-            pltpu.VMEM(WHOLE, jnp.bfloat16),
             pltpu.VMEM((8, 128), jnp.int32),
             pltpu.SMEM((8, 128), jnp.int32),
             pltpu.SemaphoreType.DMA(()),
-            pltpu.SemaphoreType.DMA((BLOCKS // PIECE,)),
+            pltpu.SemaphoreType.DMA((BLOCKS // GROUP,)),
             pltpu.SemaphoreType.DMA(()),
         ],
         compiler_params=pltpu.CompilerParams(vmem_limit_bytes=PACK_VMEM),
         cost_estimate=pl.CostEstimate(
-            flops=0, bytes_accessed=4 * BLOCKS * CELLS * TOTAL, transcendentals=0
-        ),
-        name="pack",
-    )(asked, relaxed)
+            flops=2 * BLOCKS * CELLS * TOTAL * 64,
+            bytes_accessed=4 * BLOCKS * CELLS * TOTAL,
+            transcendentals=BLOCKS * CELLS * TOTAL,
+        ),
+        name="relax",
+    )(asked, dist, basis, factors)
 
 
 def row_masks():
@@ -309,6 +309,7 @@
 def advance_kernel(owner, received, mask, rate, partial, kept):
     low_x, low_y, low_z = row_masks()
     speed_y, speed_z, rising_z = speeds()
+    speed_yz = [speed + speed_z for speed in speed_y]
     from_below = rising_z & ~low_z
     from_above = ~rising_z & low_z
     nothing = jnp.zeros((CELLS, 128), jnp.float32)
@@ -321,7 +322,8 @@
                 received[source, :, lanes(tile)].astype(jnp.float32) * own_mask
             )
 
-    kept[BLOCKS] = jnp.zeros((CELLS, TOTAL), jnp.float32)
+    for bz in range(BZ):
+        kept[BLOCKS + bz] = jnp.zeros((CELLS, TOTAL), jnp.float32)
 
     @pl.loop(0, BX * BY)
     def _(column):
@@ -329,39 +331,35 @@
         line = column * BZ
         outside = BLOCKS
         near_x = (
-            [jnp.where(bx == BX - 1, outside, line + SLAB), jnp.where(bx == BX - 1, 0, 1)],
-            [jnp.where(bx == 0, outside, line - SLAB), jnp.where(bx == 0, 0, 1)],
+            jnp.where(bx == BX - 1, outside, line + SLAB),
+            jnp.where(bx == 0, outside, line - SLAB),
         )
         near_y = (
-            [jnp.where(by == BY - 1, outside, line + BZ), jnp.where(by == BY - 1, 0, 1)],
-            [jnp.where(by == 0, outside, line - BZ), jnp.where(by == 0, 0, 1)],
+            jnp.where(by == BY - 1, outside, line + BZ),
+            jnp.where(by == 0, outside, line - BZ),
         )
+        rates = [rate[line + bz] for bz in range(BZ)]
         for tile in range(TILES):
             x, y = tile // (TILES // 2), tile % 2
             own_line = [kept[line + bz, :, lanes(tile)] for bz in range(BZ)]
+            total = speed_x(tile) + speed_yz[y]
             for bz in range(BZ):
                 own = own_line[bz]
                 below = own_line[bz - 1] if bz else nothing
                 above = own_line[bz + 1] if bz < BZ - 1 else nothing
-                start, stride = near_x[x]
-                other = kept[start + stride * bz, :, lanes(tile)]
+                other = kept[near_x[x] + bz, :, lanes(tile)]
                 from_x = swap(
                     jnp.where(low_x, own, other) if x else jnp.where(low_x, other, own), 4
                 )
-                start, stride = near_y[y]
-                other = kept[start + stride * bz, :, lanes(tile)]
+                other = kept[near_y[y] + bz, :, lanes(tile)]
                 from_y = swap(
                     jnp.where(low_y, own, other) if y else jnp.where(low_y, other, own), 2
                 )
                 from_z = swap(
                     jnp.where(from_below, below, jnp.where(from_above, above, own)), 1
                 )
-                flux = (
-                    speed_x(tile) * (own - from_x)
-                    + speed_y[y] * (own - from_y)
-                    + speed_z * (own - from_z)
-                )
-                partial[line + bz, :, lanes(tile)] = own - rate[line + bz] * flux
+                gain = speed_x(tile) * from_x + speed_y[y] * from_y + speed_z * from_z
+                partial[line + bz, :, lanes(tile)] = own + rates[bz] * (gain - total * own)
 
 
 def advance(owner, received, mask, rate):
@@ -370,7 +368,7 @@
         out_shape=jax.ShapeDtypeStruct(WHOLE, jnp.float32),
         in_specs=[pl.BlockSpec(memory_space=pltpu.SMEM)] + [VMEM] * 3,
         out_specs=VMEM,
-        scratch_shapes=[pltpu.VMEM((BLOCKS + 1, CELLS, TOTAL), jnp.float32)],
+        scratch_shapes=[pltpu.VMEM((BLOCKS + BZ, CELLS, TOTAL), jnp.float32)],
         compiler_params=pltpu.CompilerParams(vmem_limit_bytes=ADVANCE_VMEM),
         cost_estimate=pl.CostEstimate(
             flops=100 * math.prod(WHOLE), bytes_accessed=6 * math.prod(WHOLE), transcendentals=0
@@ -469,7 +467,8 @@
     asked = lax.all_to_all(
         jnp.broadcast_to(request, (devices, 128)), axes, split_axis=0, concat_axis=0, tiled=True
     )
-    send = pack(asked, relax(dist_old))
+    basis = jnp.asarray(basis_rows())
+    send = relax(asked, dist_old, basis, moments(dist_old, basis))
     received = lax.all_to_all(send, axes, split_axis=0, concat_axis=0, tiled=True)
     return after(received, source_owner, levels, active)
 

time: 173 us -> 169 us (0.977)
  Pallas kernels: 36.1 us -> 31.1 us
    pallas_call x2, Pallas kernels: 17.7 us -> 13.1 us  [the longest x1 7.21 us: moments(): pl.pallas_call(moments_kernel, out_shape=jax.ShapeDtypeStruct((BLOCKS * C...]
  transfers between devices with their start and end apart: 6 -> 6, of which waited for: 1 -> 2; matrix products, arithmetic and copies ran while one was open for 0% -> 0% of each run, Pallas kernels for 12% -> 10%
where the time goes in v7:
time: 169 us
  waiting for transfers between devices  102 us (60%)
  starting transfers between devices  31.8 us (19%)
  Pallas kernels  31.1 us (18%)
  local copies, waits for them, and re-layouts  2.09 us (1%)
    all_to_all x1, waiting for transfers between devices, per_device(): lax.all_to_all(send, axes, split_axis=0, concat_axis=0, tiled=True)  102 us
    ppermute x4, starting transfers between devices, after(): halos.append(lax.ppermute(face, name, up(n) if to_above else down(n)))  11.5 us
    all_to_all x1, starting transfers between devices, per_device(): lax.all_to_all(jnp.broadcast_to(request, (devices, 128)), axes, split_axi...  10.8 us
    all_to_all x1, starting transfers between devices, per_device(): lax.all_to_all(send, axes, split_axis=0, concat_axis=0, tiled=True)  9.53 us
    pallas_call x1, Pallas kernels, advance(): pl.pallas_call(advance_kernel, out_shape=jax.ShapeDtypeStruct(WHOLE, jnp....  8.83 us
    pallas_call x1, Pallas kernels, moments(): pl.pallas_call(moments_kernel, out_shape=jax.ShapeDtypeStruct((BLOCKS * C...  7.21 us
    pallas_call x1, Pallas kernels, relax(): pl.pallas_call(relax_kernel, out_shape=jax.ShapeDtypeStruct((devices, CEL...  5.87 us
    pallas_call x1, Pallas kernels, faces(): pl.pallas_call(faces_kernel, out_shape=[jax.ShapeDtypeStruct(FACE, jnp.bf...  5.4 us
  transfers between devices with their start and end apart: 6, of which 2 were waited for; matrix products, arithmetic and copies ran while one was open for 0% of the time, Pallas kernels for 10%

profile of v7, /device:TPU:7, one launch (start us, length us, event | category | flops | bytes accessed | tf_op | source)
XLA Modules:
  0.0 168.5 jit_solution(11980864089270065049)
XLA Ops:
  0.0 0.8 select_reduce_fusion
  0.8 0.8 broadcast_in_dim.9
  1.6 10.8 %all-to-all-start = ((s32[128,1,128]{2,1,0:T(1,128)}), s32[128,1,128]{2,1,0:T(1,128)S(1)}, u32[]{:S(2)}, u32[]{:S(2)}) async-start(s32[128,1,128]{2,1,0:T(1,128)} %broadcast_in_dim.9), calls=%async_computation | async-start | bytes 131072 | tf_op jit(solution)/shard_map/all_to_all | solution.py:467
  12.4 0.0 copy-start
  12.4 7.2 %moments.1.factors = f32[768,128]{1,0:T(8,128)} custom-call(bf16[96,8,4096]{2,1,0:T(8,128)(2,1)} %dist.3, bf16[48,4096]{1,0:T(8,128)(2,1)} %constant.13.clone.basis), custom_call_target="tpu_custom_call" | custom-call | flops 9437184000 | bytes 6291456 | tf_op jit(solution)/shard_map/moments/pallas_call | solution.py:127
  19.6 0.7 all-to-all-done
  20.3 1.0 copy-done.1
  21.3 5.9 %relax.1 = bf16[128,8,4096]{2,1,0:T(8,128)(2,1)} custom-call(s32[128,128]{1,0:T(8,128)S(1)} %bitcast.1, bf16[96,8,4096]{2,1,0:T(8,128)(2,1)} %dist.3, bf16[48,4096]{1,0:T(8,128)(2,1)S(1)} %copy-done, f32[768,128]{1,0:T(8,128)S(1)} %copy-done.1), custom_call_target="tpu_custom_call" | custom-call | flops 402653184 | bytes 12582912 | tf_op jit(solution)/shard_map/relax/pallas_call | solution.py:195
  27.2 0.0 copy-start.3
  27.2 0.0 copy-start.2
  27.2 9.5 %all-to-all-start.1 = ((bf16[128,8,4096]{2,1,0:T(8,128)(2,1)}), bf16[128,8,4096]{2,1,0:T(8,128)(2,1)}, u32[]{:S(2)}, u32[]{:S(2)}) async-start(bf16[128,8,4096]{2,1,0:T(8,128)(2,1)} %relax.1), calls=%async_computation.1 | async-start | bytes 16777216 | tf_op jit(solution)/shard_map/all_to_all | solution.py:472
  36.8 0.0 copy-start.4
  36.8 0.1 copy.8
  36.9 101.6 %all-to-all-done.1.arrived = bf16[128,8,4096]{2,1,0:T(8,128)(2,1)} async-done(((bf16[128,8,4096]{2,1,0:T(8,128)(2,1)}), bf16[128,8,4096]{2,1,0:T(8,128)(2,1)}, u32[]{:S(2)}, u32[]{:S(2)}) %all-to-all-start.1) | async-done | bytes 8388640 | tf_op jit(solution)/shard_map/all_to_all | solution.py:472
  138.4 0.2 broadcast_in_dim.10.mask
  138.6 5.4 %faces.1 = (bf16[12,8,2048]{2,1,0:T(8,128)(2,1)S(1)}, bf16[12,8,2048]{2,1,0:T(8,128)(2,1)S(1)}, bf16[12,8,2048]{2,1,0:T(8,128)(2,1)S(1)}, bf16[12,8,2048]{2,1,0:T(8,128)(2,1)S(1)}, bf16[128,8,4096]{2,1,0:T(8,128)(2,1)S(1)}) custom-call(s32[96]{0:T(128)S(1)} %copy-done.2, bf16[128,8,4096]{2,1,0:T(8,128)(2,1)} %all-to-all-done.1.arrived, ...), custom_call_target="tpu_custom_call" | custom-call | flops 6291456 | bytes 3145728 | tf_op jit(solution)/shard_map/faces/pallas_call | solution.py:280
  144.0 1.9 %collective-permute-start = (bf16[12,8,2048]{2,1,0:T(8,128)(2,1)S(1)}, bf16[12,8,2048]{2,1,0:T(8,128)(2,1)S(1)}, u32[]{:S(2)}, u32[]{:S(2)}) collective-permute-start(bf16[12,8,2048]{2,1,0:T(8,128)(2,1)S(1)} %get-tuple-element.11), channel_id=1, source_target_pairs={{1,0},{2,1},{3,2},{4,3},{5,4},{6,5},{7,6},{8,7},{9,8},{10,9},{11,1... | collective-permute-start | bytes 1179656 | tf_op jit(solution)/shard_map/ppermute | solution.py:455
  145.9 3.5 %collective-permute-start.1 = (bf16[12,8,2048]{2,1,0:T(8,128)(2,1)S(1)}, bf16[12,8,2048]{2,1,0:T(8,128)(2,1)S(1)}, u32[]{:S(2)}, u32[]{:S(2)}) collective-permute-start(bf16[12,8,2048]{2,1,0:T(8,128)(2,1)S(1)} %get-tuple-element.12), channel_id=1, source_target_pairs={{0,1},{1,2},{2,3},{3,4},{4,5},{5,6},{6,7},{7,8},{8,9},{9,10},{10,1... | collective-permute-start | bytes 1179656 | tf_op jit(solution)/shard_map/ppermute | solution.py:455
  149.5 3.3 %collective-permute-start.2 = (bf16[12,8,2048]{2,1,0:T(8,128)(2,1)S(1)}, bf16[12,8,2048]{2,1,0:T(8,128)(2,1)S(1)}, u32[]{:S(2)}, u32[]{:S(2)}) collective-permute-start(bf16[12,8,2048]{2,1,0:T(8,128)(2,1)S(1)} %get-tuple-element.13), channel_id=1, source_target_pairs={{16,0},{32,16},{48,32},{64,48},{80,64},{96,80},{112,96},{17,1},{33... | collective-permute-start | bytes 1179656 | tf_op jit(solution)/shard_map/ppermute | solution.py:455
  152.8 2.7 %collective-permute-start.3 = (bf16[12,8,2048]{2,1,0:T(8,128)(2,1)S(1)}, bf16[12,8,2048]{2,1,0:T(8,128)(2,1)S(1)}, u32[]{:S(2)}, u32[]{:S(2)}) collective-permute-start(bf16[12,8,2048]{2,1,0:T(8,128)(2,1)S(1)} %get-tuple-element.14), channel_id=1, source_target_pairs={{0,16},{16,32},{32,48},{48,64},{64,80},{80,96},{96,112},{1,17},{17... | collective-permute-start | bytes 1179656 | tf_op jit(solution)/shard_map/ppermute | solution.py:455
  155.5 0.3 broadcast_multiply_fusion.rate
  155.8 8.8 %advance.1.partial = f32[96,8,4096]{2,1,0:T(8,128)S(1)} custom-call(s32[96]{0:T(128)S(1)} %copy-done.2, bf16[128,8,4096]{2,1,0:T(8,128)(2,1)S(1)} %get-tuple-element.10.received, f32[96,8,128]{2,1,0:T(8,128)S(1)} %broadcast_in_dim.10.mask, f32[96,8,128]{2,1,0:T(8,128)S(1)} %broadcast_multiply_fusion.rate), custom_call_target="tpu_custom_call" | custom-call | flops 314572800 | bytes 18874368 | tf_op jit(solution)/shard_map/advance/pallas_call | solution.py:366
  164.7 0.0 collective-permute-done.1.up_y
  164.7 3.8 %edge.1 = bf16[96,8,4096]{2,1,0:T(8,128)(2,1)} custom-call(f32[96,8,4096]{2,1,0:T(8,128)S(1)} %advance.1.partial, f32[96,8,128]{2,1,0:T(8,128)S(1)} %broadcast_multiply_fusion.rate, bf16[12,8,2048]{2,1,0:T(8,128)(2,1)S(1)} %collective-permute-done.down_y, bf16[12,8,2048]{2,1,0:T(8,128)(2,1)S(1)} %collective-permute-done.1.up_y, ...), custom_call_target="tpu_custom_call" | custom-call | flops 12582912 | bytes 18874368 | tf_op jit(solution)/shard_map/edge/pallas_call | solution.py:423
  (12 shorter events, 0.0 us)
Async XLA Ops:
  1.6 18.7 %all-to-all-start = ((s32[128,1,128]{2,1,0:T(1,128)}), s32[128,1,128]{2,1,0:T(1,128)S(1)}, u32[]{:S(2)}, u32[]{:S(2)}) async-start(s32[128,1,128]{2,1,0:T(1,128)} %broadcast_in_dim.9), calls=%async_computation | async-start | bytes 131072 | tf_op jit(solution)/shard_map/all_to_all | solution.py:467
  12.4 7.9 %copy-start = (bf16[48,4096]{1,0:T(8,128)(2,1)S(1)}, bf16[48,4096]{1,0:T(8,128)(2,1)}, u32[]{:S(2)}) copy-start(bf16[48,4096]{1,0:T(8,128)(2,1)} %constant.13.clone.basis) | copy-start | bytes 1179652
  20.3 1.0 copy-start.1
  27.2 9.6 %copy-start.3 = (s32[96,8]{0,1:T(8,128)S(1)}, s32[96,8]{0,1:T(8,128)}, u32[]{:S(2)}) copy-start(s32[96,8]{0,1:T(8,128)} %param.8) | copy-start | bytes 9220
  27.2 111.4 %copy-start.2 = (s32[96]{0:T(128)S(1)}, s32[96]{0:T(128)}, u32[]{:S(2)}) copy-start(s32[96]{0:T(128)} %owner.3) | copy-start | bytes 1156
  27.2 111.2 %all-to-all-start.1 = ((bf16[128,8,4096]{2,1,0:T(8,128)(2,1)}), bf16[128,8,4096]{2,1,0:T(8,128)(2,1)}, u32[]{:S(2)}, u32[]{:S(2)}) async-start(bf16[128,8,4096]{2,1,0:T(8,128)(2,1)} %relax.1), calls=%async_computation.1 | async-start | bytes 16777216 | tf_op jit(solution)/shard_map/all_to_all | solution.py:472
  36.8 118.8 %copy-start.4 = (s32[96]{0:T(128)S(1)}, s32[96]{0:T(128)}, u32[]{:S(2)}) copy-start(s32[96]{0:T(128)} %param.7) | copy-start | bytes 1156
  144.0 20.6 %collective-permute-start = (bf16[12,8,2048]{2,1,0:T(8,128)(2,1)S(1)}, bf16[12,8,2048]{2,1,0:T(8,128)(2,1)S(1)}, u32[]{:S(2)}, u32[]{:S(2)}) collective-permute-start(bf16[12,8,2048]{2,1,0:T(8,128)(2,1)S(1)} %get-tuple-element.11), channel_id=1, source_target_pairs={{1,0},{2,1},{3,2},{4,3},{5,4},{6,5},{7,6},{8,7},{9,8},{10,9},{11,1... | collective-permute-start | bytes 1179656 | tf_op jit(solution)/shard_map/ppermute | solution.py:455
  145.9 18.7 %collective-permute-start.1 = (bf16[12,8,2048]{2,1,0:T(8,128)(2,1)S(1)}, bf16[12,8,2048]{2,1,0:T(8,128)(2,1)S(1)}, u32[]{:S(2)}, u32[]{:S(2)}) collective-permute-start(bf16[12,8,2048]{2,1,0:T(8,128)(2,1)S(1)} %get-tuple-element.12), channel_id=1, source_target_pairs={{0,1},{1,2},{2,3},{3,4},{4,5},{5,6},{6,7},{7,8},{8,9},{9,10},{10,1... | collective-permute-start | bytes 1179656 | tf_op jit(solution)/shard_map/ppermute | solution.py:455
  149.5 15.2 %collective-permute-start.2 = (bf16[12,8,2048]{2,1,0:T(8,128)(2,1)S(1)}, bf16[12,8,2048]{2,1,0:T(8,128)(2,1)S(1)}, u32[]{:S(2)}, u32[]{:S(2)}) collective-permute-start(bf16[12,8,2048]{2,1,0:T(8,128)(2,1)S(1)} %get-tuple-element.13), channel_id=1, source_target_pairs={{16,0},{32,16},{48,32},{64,48},{80,64},{96,80},{112,96},{17,1},{33... | collective-permute-start | bytes 1179656 | tf_op jit(solution)/shard_map/ppermute | solution.py:455
  152.8 11.9 %collective-permute-start.3 = (bf16[12,8,2048]{2,1,0:T(8,128)(2,1)S(1)}, bf16[12,8,2048]{2,1,0:T(8,128)(2,1)S(1)}, u32[]{:S(2)}, u32[]{:S(2)}) collective-permute-start(bf16[12,8,2048]{2,1,0:T(8,128)(2,1)S(1)} %get-tuple-element.14), channel_id=1, source_target_pairs={{0,16},{16,32},{32,48},{48,64},{64,80},{80,96},{96,112},{1,17},{17... | collective-permute-start | bytes 1179656 | tf_op jit(solution)/shard_map/ppermute | solution.py:455

commit v8 on v7

--- a/solution.py
+++ b/solution.py
@@ -22,7 +22,7 @@
 
 TILES = TOTAL // 128
 PIECE = 16
-RELAX_VMEM = 56 << 20
+RELAX_VMEM = 50 << 20
 PACK_VMEM = 49 << 20
 FACES_VMEM = 16 << 20
 ADVANCE_VMEM = 28 << 20
@@ -228,7 +228,6 @@
     return jnp.take_along_axis(x, row ^ distance, axis=0)
 
 
-PARTS = 4
 FACES = (("y", 0), ("y", 1), ("x", 0), ("x", 1))
 FACE = (12, CELLS, TOTAL // 2)
 
@@ -243,36 +242,76 @@
     return [t for t in range(TILES) if up == (t % 2 if axis == "y" else t // (TILES // 2))]
 
 
+GROUPS = (
+    [(bx, 0) for bx in range(BX)],
+    [(bx, BY - 1) for bx in range(BX)],
+    [(0, by) for by in range(1, BY - 1)],
+    [(BX - 1, by) for by in range(1, BY - 1)],
+    [(bx, by) for bx in range(1, BX - 1) for by in range(1, BY - 1)],
+)
+PLACES = {column: BZ * n for n, column in enumerate(c for group in GROUPS for c in group)}
+
+
 def faces_kernel(owner, arrived, mask, *rest):
     sent, (received, sems) = rest[: len(FACES)], rest[len(FACES) :]
-    part = arrived.shape[0] // PARTS
-    copies = [
+    low_x, low_y, _ = row_masks()
+
+    def fetch(group):
+        for bx, by in GROUPS[group]:
+            for bz in range(BZ):
+                pltpu.make_async_copy(
+                    arrived.at[owner[(bx * BY + by) * BZ + bz]],
+                    received.at[PLACES[bx, by] + bz],
+                    sems.at[group],
+                ).start()
+
+    def arrive(group):
+        count = BZ * len(GROUPS[group])
         pltpu.make_async_copy(
-            arrived.at[pl.ds(i * part, part)], received.at[pl.ds(i * part, part)], sems.at[i]
-        )
-        for i in range(PARTS)
-    ]
-    for copy in copies:
-        copy.start()
-    for copy in copies:
-        copy.wait()
-    low_x, low_y, _ = row_masks()
-    for (axis, up), face in zip(FACES, sent):
+            arrived.at[pl.ds(0, count)],
+            received.at[pl.ds(PLACES[GROUPS[group][0]], count)],
+            sems.at[group],
+        ).wait()
+
+    def write(axis, up):
+        face = sent[FACES.index((axis, up))]
         low, distance = (low_x, 4) if axis == "x" else (low_y, 2)
 
         @pl.loop(0, 12)
         def _(pair):
             block = face_block(axis, up, pair)
-            sources = [owner[block + side] for side in range(2)]
+            edge = (BX - 1) * up
+            places = [PLACES[(edge, n) if axis == "x" else (n, edge)] for n in range(4)]
+            line = pair // 3
+            place = pair % 3 * 2 + jnp.where(
+                line < 2,
+                jnp.where(line == 0, places[0], places[1]),
+                jnp.where(line == 2, places[2], places[3]),
+            )
             masks = [mask[block + side] for side in range(2)]
-            for place, tile in enumerate(face_tiles(axis, up)):
+            for n, tile in enumerate(face_tiles(axis, up)):
                 a, b = (
-                    received[sources[side], :, lanes(tile)].astype(jnp.float32) * masks[side]
+                    received[place + side, :, lanes(tile)].astype(jnp.float32) * masks[side]
                     for side in range(2)
                 )
                 b = swap(b, distance)
                 joined = jnp.where(low, b, a) if up else jnp.where(low, a, b)
-                face[pair, :, lanes(place)] = joined.astype(jnp.bfloat16)
+                face[pair, :, lanes(n)] = joined.astype(jnp.bfloat16)
+
+    fetch(0)
+    fetch(1)
+    fetch(2)
+    arrive(0)
+    write("y", 0)
+    fetch(3)
+    fetch(4)
+    arrive(1)
+    write("y", 1)
+    arrive(2)
+    write("x", 0)
+    arrive(3)
+    write("x", 1)
+    arrive(4)
 
 
 def faces(owner, received, mask):
@@ -280,10 +319,10 @@
     return pl.pallas_call(
         faces_kernel,
         out_shape=[jax.ShapeDtypeStruct(FACE, jnp.bfloat16) for _ in FACES]
-        + [jax.ShapeDtypeStruct(received.shape, received.dtype)],
+        + [jax.ShapeDtypeStruct(WHOLE, received.dtype)],
         in_specs=[pl.BlockSpec(memory_space=pltpu.SMEM), ANY, VMEM],
         out_specs=[VMEM] * (len(FACES) + 1),
-        scratch_shapes=[pltpu.SemaphoreType.DMA((PARTS,))],
+        scratch_shapes=[pltpu.SemaphoreType.DMA((len(GROUPS),))],
         compiler_params=pltpu.CompilerParams(vmem_limit_bytes=FACES_VMEM),
         cost_estimate=pl.CostEstimate(
             flops=8 * moved, bytes_accessed=4 * moved, transcendentals=0
@@ -306,7 +345,7 @@
     return SPACING * abs(2 * (tile // 2) + 1 - VS)
 
 
-def advance_kernel(owner, received, mask, rate, partial, kept):
+def advance_kernel(received, mask, rate, partial, kept):
     low_x, low_y, low_z = row_masks()
     speed_y, speed_z, rising_z = speeds()
     speed_yz = [speed + speed_z for speed in speed_y]
@@ -314,13 +353,16 @@
     from_above = ~rising_z & low_z
     nothing = jnp.zeros((CELLS, 128), jnp.float32)
 
-    @pl.loop(0, BLOCKS)
-    def _(block):
-        source, own_mask = owner[block], mask[block]
-        for tile in range(TILES):
-            kept[block, :, lanes(tile)] = (
-                received[source, :, lanes(tile)].astype(jnp.float32) * own_mask
-            )
+    for (bx, by), place in PLACES.items():
+
+        @pl.loop(0, BZ)
+        def _(bz):
+            block = (bx * BY + by) * BZ + bz
+            own_mask = mask[block]
+            for tile in range(TILES):
+                kept[block, :, lanes(tile)] = (
+                    received[place + bz, :, lanes(tile)].astype(jnp.float32) * own_mask
+                )
 
     for bz in range(BZ):
         kept[BLOCKS + bz] = jnp.zeros((CELLS, TOTAL), jnp.float32)
@@ -362,11 +404,11 @@
                 partial[line + bz, :, lanes(tile)] = own + rates[bz] * (gain - total * own)
 
 
-def advance(owner, received, mask, rate):
+def advance(received, mask, rate):
     return pl.pallas_call(
         advance_kernel,
         out_shape=jax.ShapeDtypeStruct(WHOLE, jnp.float32),
-        in_specs=[pl.BlockSpec(memory_space=pltpu.SMEM)] + [VMEM] * 3,
+        in_specs=[VMEM] * 3,
         out_specs=VMEM,
         scratch_shapes=[pltpu.VMEM((BLOCKS + BZ, CELLS, TOTAL), jnp.float32)],
         compiler_params=pltpu.CompilerParams(vmem_limit_bytes=ADVANCE_VMEM),
@@ -374,7 +416,7 @@
             flops=100 * math.prod(WHOLE), bytes_accessed=6 * math.prod(WHOLE), transcendentals=0
         ),
         name="advance",
-    )(owner, received, mask, rate)
+    )(received, mask, rate)
 
 
 def edge_kernel(partial, rate, down_y, up_y, down_x, up_x, out, made, sems):
@@ -453,7 +495,7 @@
     for (axis, to_above), face in zip(FACES, sent):
         name, n = ("gx", n_gx) if axis == "x" else ("gy", n_gy)
         halos.append(lax.ppermute(face, name, up(n) if to_above else down(n)))
-    return edge(advance(source_owner, received, mask, rate), rate, halos)
+    return edge(advance(received, mask, rate), rate, halos)
 
 
 def per_device(dist_old, source_owner, levels, active):

time: 169 us -> 165 us (0.976)
  Pallas kernels: 31.1 us -> 27.1 us
    pallas_call x1, Pallas kernels: 7.21 us -> 5.45 us  [moments(): pl.pallas_call(moments_kernel, out_shape=jax.ShapeDtypeStruct((BLOCKS * C...]
  transfers between devices with their start and end apart: 6 -> 6, of which waited for: 2 -> 2; matrix products, arithmetic and copies ran while one was open for 0% -> 0% of each run, Pallas kernels for 10% -> 8%
where the time goes in v8:
time: 165 us
  waiting for transfers between devices  103 us (62%)
  starting transfers between devices  31.2 us (19%)
  Pallas kernels  27.1 us (16%)
  local copies, waits for them, and re-layouts  2.1 us (1%)
    all_to_all x1, waiting for transfers between devices, per_device(): lax.all_to_all(send, axes, split_axis=0, concat_axis=0, tiled=True)  102 us
    ppermute x4, starting transfers between devices, after(): halos.append(lax.ppermute(face, name, up(n) if to_above else down(n)))  11.5 us
    all_to_all x1, starting transfers between devices, per_device(): lax.all_to_all(jnp.broadcast_to(request, (devices, 128)), axes, split_axi...  10.8 us
    all_to_all x1, starting transfers between devices, per_device(): lax.all_to_all(send, axes, split_axis=0, concat_axis=0, tiled=True)  8.93 us
    pallas_call x1, Pallas kernels, advance(): pl.pallas_call(advance_kernel, out_shape=jax.ShapeDtypeStruct(WHOLE, jnp....  8.04 us
    pallas_call x1, Pallas kernels, relax(): pl.pallas_call(relax_kernel, out_shape=jax.ShapeDtypeStruct((devices, CEL...  5.81 us
    pallas_call x1, Pallas kernels, moments(): pl.pallas_call(moments_kernel, out_shape=jax.ShapeDtypeStruct((BLOCKS * C...  5.45 us
    pallas_call x1, Pallas kernels, faces(): pl.pallas_call(faces_kernel, out_shape=[jax.ShapeDtypeStruct(FACE, jnp.bf...  3.94 us
  transfers between devices with their start and end apart: 6, of which 2 were waited for; matrix products, arithmetic and copies ran while one was open for 0% of the time, Pallas kernels for 8%

profile of v8, /device:TPU:7, one launch (start us, length us, event | category | flops | bytes accessed | tf_op | source)
XLA Modules:
  0.0 164.5 jit_solution(5816544674840505372)
XLA Ops:
  0.0 0.8 select_reduce_fusion
  0.8 0.8 broadcast_in_dim.9
  1.6 10.8 %all-to-all-start = ((s32[128,1,128]{2,1,0:T(1,128)}), s32[128,1,128]{2,1,0:T(1,128)S(1)}, u32[]{:S(2)}, u32[]{:S(2)}) async-start(s32[128,1,128]{2,1,0:T(1,128)} %broadcast_in_dim.9), calls=%async_computation | async-start | bytes 131072 | tf_op jit(solution)/shard_map/all_to_all | solution.py:509
  12.4 0.0 copy-start
  12.4 1.0 copy-done
  13.4 5.5 %moments.1.factors = f32[768,128]{1,0:T(8,128)S(1)} custom-call(bf16[96,8,4096]{2,1,0:T(8,128)(2,1)} %dist.3, bf16[48,4096]{1,0:T(8,128)(2,1)S(1)} %copy-done), custom_call_target="tpu_custom_call" | custom-call | flops 9437184000 | bytes 6291456 | tf_op jit(solution)/shard_map/moments/pallas_call | solution.py:127
  18.9 1.4 all-to-all-done
  20.2 5.8 %relax.1 = bf16[128,8,4096]{2,1,0:T(8,128)(2,1)} custom-call(s32[128,128]{1,0:T(8,128)S(1)} %bitcast.1, bf16[96,8,4096]{2,1,0:T(8,128)(2,1)} %dist.3, bf16[48,4096]{1,0:T(8,128)(2,1)S(1)} %copy-done.1, f32[768,128]{1,0:T(8,128)S(1)} %moments.1.factors), custom_call_target="tpu_custom_call" | custom-call | flops 402653184 | bytes 12582912 | tf_op jit(solution)/shard_map/relax/pallas_call | solution.py:195
  26.1 0.0 copy-start.3
  26.1 0.0 copy-start.2
  26.1 8.9 %all-to-all-start.1 = ((bf16[128,8,4096]{2,1,0:T(8,128)(2,1)}), bf16[128,8,4096]{2,1,0:T(8,128)(2,1)}, u32[]{:S(2)}, u32[]{:S(2)}) async-start(bf16[128,8,4096]{2,1,0:T(8,128)(2,1)} %relax.1), calls=%async_computation.1 | async-start | bytes 16777216 | tf_op jit(solution)/shard_map/all_to_all | solution.py:514
  35.0 0.0 copy-start.4
  35.1 0.1 copy.8
  35.1 101.6 %all-to-all-done.1.arrived = bf16[128,8,4096]{2,1,0:T(8,128)(2,1)} async-done(((bf16[128,8,4096]{2,1,0:T(8,128)(2,1)}), bf16[128,8,4096]{2,1,0:T(8,128)(2,1)}, u32[]{:S(2)}, u32[]{:S(2)}) %all-to-all-start.1) | async-done | bytes 8388640 | tf_op jit(solution)/shard_map/all_to_all | solution.py:514
  136.7 0.2 broadcast_in_dim.10.mask
  136.9 3.9 %faces.1 = (bf16[12,8,2048]{2,1,0:T(8,128)(2,1)S(1)}, bf16[12,8,2048]{2,1,0:T(8,128)(2,1)S(1)}, bf16[12,8,2048]{2,1,0:T(8,128)(2,1)S(1)}, bf16[12,8,2048]{2,1,0:T(8,128)(2,1)S(1)}, bf16[96,8,4096]{2,1,0:T(8,128)(2,1)S(1)}) custom-call(s32[96]{0:T(128)S(1)} %copy-done.2, bf16[128,8,4096]{2,1,0:T(8,128)(2,1)} %all-to-all-done.1.arrived, ...), custom_call_target="tpu_custom_call" | custom-call | flops 6291456 | bytes 3145728 | tf_op jit(solution)/shard_map/faces/pallas_call | solution.py:319
  140.8 1.9 %collective-permute-start = (bf16[12,8,2048]{2,1,0:T(8,128)(2,1)S(1)}, bf16[12,8,2048]{2,1,0:T(8,128)(2,1)S(1)}, u32[]{:S(2)}, u32[]{:S(2)}) collective-permute-start(bf16[12,8,2048]{2,1,0:T(8,128)(2,1)S(1)} %get-tuple-element.11), channel_id=1, source_target_pairs={{1,0},{2,1},{3,2},{4,3},{5,4},{6,5},{7,6},{8,7},{9,8},{10,9},{11,1... | collective-permute-start | bytes 1179656 | tf_op jit(solution)/shard_map/ppermute | solution.py:497
  142.8 3.5 %collective-permute-start.1 = (bf16[12,8,2048]{2,1,0:T(8,128)(2,1)S(1)}, bf16[12,8,2048]{2,1,0:T(8,128)(2,1)S(1)}, u32[]{:S(2)}, u32[]{:S(2)}) collective-permute-start(bf16[12,8,2048]{2,1,0:T(8,128)(2,1)S(1)} %get-tuple-element.12), channel_id=1, source_target_pairs={{0,1},{1,2},{2,3},{3,4},{4,5},{5,6},{6,7},{7,8},{8,9},{9,10},{10,1... | collective-permute-start | bytes 1179656 | tf_op jit(solution)/shard_map/ppermute | solution.py:497
  146.3 3.3 %collective-permute-start.2 = (bf16[12,8,2048]{2,1,0:T(8,128)(2,1)S(1)}, bf16[12,8,2048]{2,1,0:T(8,128)(2,1)S(1)}, u32[]{:S(2)}, u32[]{:S(2)}) collective-permute-start(bf16[12,8,2048]{2,1,0:T(8,128)(2,1)S(1)} %get-tuple-element.13), channel_id=1, source_target_pairs={{16,0},{32,16},{48,32},{64,48},{80,64},{96,80},{112,96},{17,1},{33... | collective-permute-start | bytes 1179656 | tf_op jit(solution)/shard_map/ppermute | solution.py:497
  149.6 2.7 %collective-permute-start.3 = (bf16[12,8,2048]{2,1,0:T(8,128)(2,1)S(1)}, bf16[12,8,2048]{2,1,0:T(8,128)(2,1)S(1)}, u32[]{:S(2)}, u32[]{:S(2)}) collective-permute-start(bf16[12,8,2048]{2,1,0:T(8,128)(2,1)S(1)} %get-tuple-element.14), channel_id=1, source_target_pairs={{0,16},{16,32},{32,48},{48,64},{64,80},{80,96},{96,112},{1,17},{17... | collective-permute-start | bytes 1179656 | tf_op jit(solution)/shard_map/ppermute | solution.py:497
  152.4 0.3 broadcast_multiply_fusion.rate
  152.6 8.0 %advance.1.partial = f32[96,8,4096]{2,1,0:T(8,128)S(1)} custom-call(bf16[96,8,4096]{2,1,0:T(8,128)(2,1)S(1)} %get-tuple-element.10.received, f32[96,8,128]{2,1,0:T(8,128)S(1)} %broadcast_in_dim.10.mask, f32[96,8,128]{2,1,0:T(8,128)S(1)} %broadcast_multiply_fusion.rate), custom_call_target="tpu_custom_call" | custom-call | flops 314572800 | bytes 18874368 | tf_op jit(solution)/shard_map/advance/pallas_call | solution.py:408
  160.7 0.0 collective-permute-done.1.up_y
  160.7 3.8 %edge.1 = bf16[96,8,4096]{2,1,0:T(8,128)(2,1)} custom-call(f32[96,8,4096]{2,1,0:T(8,128)S(1)} %advance.1.partial, f32[96,8,128]{2,1,0:T(8,128)S(1)} %broadcast_multiply_fusion.rate, bf16[12,8,2048]{2,1,0:T(8,128)(2,1)S(1)} %collective-permute-done.down_y, bf16[12,8,2048]{2,1,0:T(8,128)(2,1)S(1)} %collective-permute-done.1.up_y, ...), custom_call_target="tpu_custom_call" | custom-call | flops 12582912 | bytes 18874368 | tf_op jit(solution)/shard_map/edge/pallas_call | solution.py:465
  (12 shorter events, 0.0 us)
Async XLA Ops:
  1.6 18.6 %all-to-all-start = ((s32[128,1,128]{2,1,0:T(1,128)}), s32[128,1,128]{2,1,0:T(1,128)S(1)}, u32[]{:S(2)}, u32[]{:S(2)}) async-start(s32[128,1,128]{2,1,0:T(1,128)} %broadcast_in_dim.9), calls=%async_computation | async-start | bytes 131072 | tf_op jit(solution)/shard_map/all_to_all | solution.py:509
  12.4 1.0 copy-start
  13.4 6.8 %copy-start.1 = (bf16[48,4096]{1,0:T(8,128)(2,1)S(1)}, bf16[48,4096]{1,0:T(8,128)(2,1)}, u32[]{:S(2)}) copy-start(bf16[48,4096]{1,0:T(8,128)(2,1)} %constant.13.clone.basis) | copy-start | bytes 1179652
  26.1 9.0 %copy-start.3 = (s32[96,8]{0,1:T(8,128)S(1)}, s32[96,8]{0,1:T(8,128)}, u32[]{:S(2)}) copy-start(s32[96,8]{0,1:T(8,128)} %param.8) | copy-start | bytes 9220
  26.1 110.8 %copy-start.2 = (s32[96]{0:T(128)S(1)}, s32[96]{0:T(128)}, u32[]{:S(2)}) copy-start(s32[96]{0:T(128)} %owner.1) | copy-start | bytes 1156
  26.1 110.6 %all-to-all-start.1 = ((bf16[128,8,4096]{2,1,0:T(8,128)(2,1)}), bf16[128,8,4096]{2,1,0:T(8,128)(2,1)}, u32[]{:S(2)}, u32[]{:S(2)}) async-start(bf16[128,8,4096]{2,1,0:T(8,128)(2,1)} %relax.1), calls=%async_computation.1 | async-start | bytes 16777216 | tf_op jit(solution)/shard_map/all_to_all | solution.py:514
  35.0 117.3 %copy-start.4 = (s32[96]{0:T(128)S(1)}, s32[96]{0:T(128)}, u32[]{:S(2)}) copy-start(s32[96]{0:T(128)} %param.7) | copy-start | bytes 1156
  140.8 19.8 %collective-permute-start = (bf16[12,8,2048]{2,1,0:T(8,128)(2,1)S(1)}, bf16[12,8,2048]{2,1,0:T(8,128)(2,1)S(1)}, u32[]{:S(2)}, u32[]{:S(2)}) collective-permute-start(bf16[12,8,2048]{2,1,0:T(8,128)(2,1)S(1)} %get-tuple-element.11), channel_id=1, source_target_pairs={{1,0},{2,1},{3,2},{4,3},{5,4},{6,5},{7,6},{8,7},{9,8},{10,9},{11,1... | collective-permute-start | bytes 1179656 | tf_op jit(solution)/shard_map/ppermute | solution.py:497
  142.8 17.9 %collective-permute-start.1 = (bf16[12,8,2048]{2,1,0:T(8,128)(2,1)S(1)}, bf16[12,8,2048]{2,1,0:T(8,128)(2,1)S(1)}, u32[]{:S(2)}, u32[]{:S(2)}) collective-permute-start(bf16[12,8,2048]{2,1,0:T(8,128)(2,1)S(1)} %get-tuple-element.12), channel_id=1, source_target_pairs={{0,1},{1,2},{2,3},{3,4},{4,5},{5,6},{6,7},{7,8},{8,9},{9,10},{10,1... | collective-permute-start | bytes 1179656 | tf_op jit(solution)/shard_map/ppermute | solution.py:497
  146.3 14.4 %collective-permute-start.2 = (bf16[12,8,2048]{2,1,0:T(8,128)(2,1)S(1)}, bf16[12,8,2048]{2,1,0:T(8,128)(2,1)S(1)}, u32[]{:S(2)}, u32[]{:S(2)}) collective-permute-start(bf16[12,8,2048]{2,1,0:T(8,128)(2,1)S(1)} %get-tuple-element.13), channel_id=1, source_target_pairs={{16,0},{32,16},{48,32},{64,48},{80,64},{96,80},{112,96},{17,1},{33... | collective-permute-start | bytes 1179656 | tf_op jit(solution)/shard_map/ppermute | solution.py:497
  149.6 11.1 %collective-permute-start.3 = (bf16[12,8,2048]{2,1,0:T(8,128)(2,1)S(1)}, bf16[12,8,2048]{2,1,0:T(8,128)(2,1)S(1)}, u32[]{:S(2)}, u32[]{:S(2)}) collective-permute-start(bf16[12,8,2048]{2,1,0:T(8,128)(2,1)S(1)} %get-tuple-element.14), channel_id=1, source_target_pairs={{0,16},{16,32},{32,48},{48,64},{64,80},{80,96},{96,112},{1,17},{17... | collective-permute-start | bytes 1179656 | tf_op jit(solution)/shard_map/ppermute | solution.py:497

commit v9 on v8

--- a/solution.py
+++ b/solution.py
@@ -22,10 +22,10 @@
 
 TILES = TOTAL // 128
 PIECE = 16
-RELAX_VMEM = 50 << 20
+RELAX_VMEM = 53 << 20
 PACK_VMEM = 49 << 20
 FACES_VMEM = 16 << 20
-ADVANCE_VMEM = 28 << 20
+ADVANCE_VMEM = 8 << 20
 EDGE_VMEM = 20 << 20
 GROUP = 16
 STEP = 512
@@ -81,7 +81,9 @@
     return [LOG2E * r for r in rows], fraction
 
 
-def moments_kernel(dist, basis, factors, held, sums, in_sems):
+def moments_kernel(dist, basis_rows, factors, held, basis, sums, in_sems, basis_sem):
+    wanted = pltpu.make_async_copy(basis_rows.at[pl.ds(0, 16)], basis, basis_sem)
+    wanted.start()
     pieces = BLOCKS // PIECE
 
     def arrival(piece):
@@ -90,12 +92,13 @@
 
     for piece in range(pieces):
         arrival(piece).start()
+    wanted.wait()
     for piece in range(pieces):
         arrival(piece).wait()
         cells = held[pl.ds(piece * PIECE, PIECE)].astype(jnp.float32)
         cells = cells.reshape(PIECE * CELLS, TOTAL).astype(jnp.bfloat16)
         sums[:, pl.ds(piece * PIECE * CELLS, PIECE * CELLS)] = lax.dot_general(
-            basis[0:16, :], cells, (((1,), (1,)), ((), ())), preferred_element_type=jnp.float32
+            basis[...], cells, (((1,), (1,)), ((), ())), preferred_element_type=jnp.float32
         )
 
     rows, fraction = coefficients_of(sums[...])
@@ -127,12 +130,14 @@
     return pl.pallas_call(
         moments_kernel,
         out_shape=jax.ShapeDtypeStruct((BLOCKS * CELLS, 128), jnp.float32),
-        in_specs=[ANY, VMEM],
+        in_specs=[ANY, ANY],
         out_specs=VMEM,
         scratch_shapes=[
             pltpu.VMEM(WHOLE, jnp.bfloat16),
+            pltpu.VMEM((16, TOTAL), jnp.bfloat16),
             pltpu.VMEM((16, BLOCKS * CELLS), jnp.float32),
             pltpu.SemaphoreType.DMA((BLOCKS // PIECE,)),
+            pltpu.SemaphoreType.DMA(()),
         ],
         compiler_params=pltpu.CompilerParams(vmem_limit_bytes=RELAX_VMEM),
         cost_estimate=pl.CostEstimate(
@@ -228,6 +233,8 @@
     return jnp.take_along_axis(x, row ^ distance, axis=0)
 
 
+PARTS = 4
+PART = TILES // PARTS
 FACES = (("y", 0), ("y", 1), ("x", 0), ("x", 1))
 FACE = (12, CELLS, TOTAL // 2)
 
@@ -345,7 +352,8 @@
     return SPACING * abs(2 * (tile // 2) + 1 - VS)
 
 
-def advance_kernel(received, mask, rate, partial, kept):
+def advance_kernel(part, received, mask, rate, _, partial, done, kept):
+    done[...] = jnp.zeros_like(done)
     low_x, low_y, low_z = row_masks()
     speed_y, speed_z, rising_z = speeds()
     speed_yz = [speed + speed_z for speed in speed_y]
@@ -359,13 +367,13 @@
         def _(bz):
             block = (bx * BY + by) * BZ + bz
             own_mask = mask[block]
-            for tile in range(TILES):
+            for tile in range(PART):
                 kept[block, :, lanes(tile)] = (
-                    received[place + bz, :, lanes(tile)].astype(jnp.float32) * own_mask
+                    received[place + bz, :, lanes(part * PART + tile)].astype(jnp.float32) * own_mask
                 )
 
     for bz in range(BZ):
-        kept[BLOCKS + bz] = jnp.zeros((CELLS, TOTAL), jnp.float32)
+        kept[BLOCKS + bz] = jnp.zeros((CELLS, PART * 128), jnp.float32)
 
     @pl.loop(0, BX * BY)
     def _(column):
@@ -381,19 +389,19 @@
             jnp.where(by == 0, outside, line - BZ),
         )
         rates = [rate[line + bz] for bz in range(BZ)]
-        for tile in range(TILES):
+        for held_at, tile in enumerate(range(part * PART, part * PART + PART)):
             x, y = tile // (TILES // 2), tile % 2
-            own_line = [kept[line + bz, :, lanes(tile)] for bz in range(BZ)]
+            own_line = [kept[line + bz, :, lanes(held_at)] for bz in range(BZ)]
             total = speed_x(tile) + speed_yz[y]
             for bz in range(BZ):
                 own = own_line[bz]
                 below = own_line[bz - 1] if bz else nothing
                 above = own_line[bz + 1] if bz < BZ - 1 else nothing
-                other = kept[near_x[x] + bz, :, lanes(tile)]
+                other = kept[near_x[x] + bz, :, lanes(held_at)]
                 from_x = swap(
                     jnp.where(low_x, own, other) if x else jnp.where(low_x, other, own), 4
                 )
-                other = kept[near_y[y] + bz, :, lanes(tile)]
+                other = kept[near_y[y] + bz, :, lanes(held_at)]
                 from_y = swap(
                     jnp.where(low_y, own, other) if y else jnp.where(low_y, other, own), 2
                 )
@@ -401,25 +409,30 @@
                     jnp.where(from_below, below, jnp.where(from_above, above, own)), 1
                 )
                 gain = speed_x(tile) * from_x + speed_y[y] * from_y + speed_z * from_z
-                partial[line + bz, :, lanes(tile)] = own + rates[bz] * (gain - total * own)
-
-
-def advance(received, mask, rate):
+                partial[line + bz, :, lanes(held_at)] = own + rates[bz] * (gain - total * own)
+
+
+def advance(part, received, mask, rate, token):
+    shape = (BLOCKS, CELLS, PART * 128)
     return pl.pallas_call(
-        advance_kernel,
-        out_shape=jax.ShapeDtypeStruct(WHOLE, jnp.float32),
-        in_specs=[VMEM] * 3,
-        out_specs=VMEM,
-        scratch_shapes=[pltpu.VMEM((BLOCKS + BZ, CELLS, TOTAL), jnp.float32)],
+        lambda *refs: advance_kernel(part, *refs),
+        out_shape=[
+            jax.ShapeDtypeStruct(shape, jnp.float32),
+            jax.ShapeDtypeStruct((8, 128), jnp.float32),
+        ],
+        in_specs=[VMEM] * 4,
+        out_specs=[VMEM] * 2,
+        scratch_shapes=[pltpu.VMEM((BLOCKS + BZ, *shape[1:]), jnp.float32)],
         compiler_params=pltpu.CompilerParams(vmem_limit_bytes=ADVANCE_VMEM),
         cost_estimate=pl.CostEstimate(
-            flops=100 * math.prod(WHOLE), bytes_accessed=6 * math.prod(WHOLE), transcendentals=0
+            flops=100 * math.prod(shape), bytes_accessed=6 * math.prod(shape), transcendentals=0
         ),
-        name="advance",
-    )(received, mask, rate)
-
-
-def edge_kernel(partial, rate, down_y, up_y, down_x, up_x, out, made, sems):
+        name=f"advance{part}",
+    )(received, mask, rate, token)
+
+
+def edge_kernel(rate, down_y, up_y, down_x, up_x, *rest):
+    partials, (out, made, sems) = rest[:PARTS], rest[PARTS:]
     low_x, low_y, _ = row_masks()
     speed_y, _, _ = speeds()
 
@@ -437,7 +450,8 @@
                 near = (jnp.where(edge, face, 0.0), jnp.where(edge, other, 0.0))
                 for side in range(2):
                     gain = rate[block + side] * (speed * swap(near[side], distance))
-                    partial_at = (block + side, slice(None), lanes(tile))
+                    partial = partials[tile // PART]
+                    partial_at = (block + side, slice(None), lanes(tile % PART))
                     partial[partial_at] = partial[partial_at] + gain
 
     def result_copy(bx):
@@ -454,18 +468,20 @@
 
         @pl.loop(bx * SLAB, bx * SLAB + SLAB)
         def _(block):
-            made[block] = partial[block].astype(jnp.bfloat16)
+            for part, partial in enumerate(partials):
+                lanes_at = pl.ds(part * PART * 128, PART * 128)
+                made[block, :, lanes_at] = partial[block].astype(jnp.bfloat16)
 
         result_copy(bx).start()
     for bx in range(BX):
         result_copy(bx).wait()
 
 
-def edge(partial, rate, halos):
+def edge(partials, rate, halos):
     return pl.pallas_call(
         edge_kernel,
         out_shape=jax.ShapeDtypeStruct(WHOLE, jnp.bfloat16),
-        in_specs=[VMEM] * 6,
+        in_specs=[VMEM] * (5 + PARTS),
         out_specs=ANY,
         scratch_shapes=[pltpu.VMEM(WHOLE, jnp.bfloat16), pltpu.SemaphoreType.DMA((BX,))],
         compiler_params=pltpu.CompilerParams(vmem_limit_bytes=EDGE_VMEM),
@@ -473,7 +489,7 @@
             flops=4 * math.prod(WHOLE), bytes_accessed=6 * math.prod(WHOLE), transcendentals=0
         ),
         name="edge",
-    )(partial, rate, *halos)
+    )(rate, *halos, *partials)
 
 
 def after(received, source_owner, levels, active):
@@ -491,11 +507,15 @@
         return [(i + 1, i) for i in range(n - 1)]
 
     *sent, received = faces(source_owner, received, mask)
-    halos = []
-    for (axis, to_above), face in zip(FACES, sent):
+    halos, partials, token = [], [], jnp.zeros((8, 128), jnp.float32)
+    for part, ((axis, to_above), face) in enumerate(zip(FACES, sent)):
         name, n = ("gx", n_gx) if axis == "x" else ("gy", n_gy)
+        if part:
+            face, token = lax.optimization_barrier((face, token))
         halos.append(lax.ppermute(face, name, up(n) if to_above else down(n)))
-    return edge(advance(received, mask, rate), rate, halos)
+        partial, token = advance(part, received, mask, rate, token)
+        partials.append(partial)
+    return edge(partials, rate, halos)
 
 
 def per_device(dist_old, source_owner, levels, active):

time: 165 us -> 170 us (1.030)
  Pallas kernels: 27.1 us -> 29.5 us
    pallas_call x1 -> x4, Pallas kernels: 8.04 us -> 10.6 us  [advance(): pl.pallas_call(lambda *refs: advance_kernel(part, *refs), out_shape=[jax....]
  transfers between devices with their start and end apart: 6 -> 6, of which waited for: 2 -> 3; matrix products, arithmetic and copies ran while one was open for 0% -> 0% of each run, Pallas kernels for 8% -> 10%
where the time goes in v9:
time: 170 us; the launch traced here: 168 us
  waiting for transfers between devices  104 us (61%)
  starting transfers between devices  31.3 us (18%)
  Pallas kernels  29.5 us (17%)
  local copies, waits for them, and re-layouts  2.1 us (1%)
    all_to_all x1, waiting for transfers between devices, per_device(): lax.all_to_all(send, axes, split_axis=0, concat_axis=0, tiled=True)  101 us
    ppermute x4, starting transfers between devices, after(): halos.append(lax.ppermute(face, name, up(n) if to_above else down(n)))  11.5 us
    all_to_all x1, starting transfers between devices, per_device(): lax.all_to_all(jnp.broadcast_to(request, (devices, 128)), axes, split_axi...  10.8 us
    pallas_call x4, Pallas kernels, advance(): pl.pallas_call(lambda *refs: advance_kernel(part, *refs), out_shape=[jax....  10.6 us
    all_to_all x1, starting transfers between devices, per_device(): lax.all_to_all(send, axes, split_axis=0, concat_axis=0, tiled=True)  9 us
    pallas_call x1, Pallas kernels, relax(): pl.pallas_call(relax_kernel, out_shape=jax.ShapeDtypeStruct((devices, CEL...  5.81 us
    pallas_call x1, Pallas kernels, moments(): pl.pallas_call(moments_kernel, out_shape=jax.ShapeDtypeStruct((BLOCKS * C...  5.56 us
    pallas_call x1, Pallas kernels, faces(): pl.pallas_call(faces_kernel, out_shape=[jax.ShapeDtypeStruct(FACE, jnp.bf...  3.94 us
  transfers between devices with their start and end apart: 6, of which 3 were waited for; matrix products, arithmetic and copies ran while one was open for 0% of the time, Pallas kernels for 10%

profile of v9, /device:TPU:7, one launch (start us, length us, event | category | flops | bytes accessed | tf_op | source)
XLA Modules:
  0.0 168.3 jit_solution(5552814669666733038)
XLA Ops:
  0.0 0.8 select_reduce_fusion
  0.8 0.8 broadcast_in_dim.12
  1.6 10.8 %all-to-all-start = ((s32[128,1,128]{2,1,0:T(1,128)}), s32[128,1,128]{2,1,0:T(1,128)S(1)}, u32[]{:S(2)}, u32[]{:S(2)}) async-start(s32[128,1,128]{2,1,0:T(1,128)} %broadcast_in_dim.12), calls=%async_computation | async-start | bytes 131072 | tf_op jit(solution)/shard_map/all_to_all | solution.py:529
  12.4 0.0 copy-start
  12.4 1.0 copy-done
  13.4 5.6 %moments.1.factors = f32[768,128]{1,0:T(8,128)S(1)} custom-call(bf16[96,8,4096]{2,1,0:T(8,128)(2,1)} %dist.3, bf16[48,4096]{1,0:T(8,128)(2,1)S(1)} %copy-done), custom_call_target="tpu_custom_call" | custom-call | flops 9437184000 | bytes 6291456 | tf_op jit(solution)/shard_map/moments/pallas_call | solution.py:130
  19.0 1.3 all-to-all-done
  20.2 5.8 %relax.1 = bf16[128,8,4096]{2,1,0:T(8,128)(2,1)} custom-call(s32[128,128]{1,0:T(8,128)S(1)} %bitcast.1, bf16[96,8,4096]{2,1,0:T(8,128)(2,1)} %dist.3, bf16[48,4096]{1,0:T(8,128)(2,1)S(1)} %copy-done.1, f32[768,128]{1,0:T(8,128)S(1)} %moments.1.factors), custom_call_target="tpu_custom_call" | custom-call | flops 402653184 | bytes 12582912 | tf_op jit(solution)/shard_map/relax/pallas_call | solution.py:200
  26.1 9.0 %all-to-all-start.1 = ((bf16[128,8,4096]{2,1,0:T(8,128)(2,1)}), bf16[128,8,4096]{2,1,0:T(8,128)(2,1)}, u32[]{:S(2)}, u32[]{:S(2)}) async-start(bf16[128,8,4096]{2,1,0:T(8,128)(2,1)} %relax.1), calls=%async_computation.1 | async-start | bytes 16777216 | tf_op jit(solution)/shard_map/all_to_all | solution.py:534
  35.1 0.1 copy.8
  35.2 0.3 broadcast_multiply_fusion.refs_2_.rate
  35.5 101.3 %all-to-all-done.1.arrived = bf16[128,8,4096]{2,1,0:T(8,128)(2,1)} async-done(((bf16[128,8,4096]{2,1,0:T(8,128)(2,1)}), bf16[128,8,4096]{2,1,0:T(8,128)(2,1)}, u32[]{:S(2)}, u32[]{:S(2)}) %all-to-all-start.1) | async-done | bytes 8388640 | tf_op jit(solution)/shard_map/all_to_all | solution.py:534
  136.8 0.2 broadcast_in_dim.10.mask.refs_1_
  137.0 3.9 %faces.1 = (bf16[12,8,2048]{2,1,0:T(8,128)(2,1)S(1)}, bf16[12,8,2048]{2,1,0:T(8,128)(2,1)S(1)}, bf16[12,8,2048]{2,1,0:T(8,128)(2,1)S(1)}, bf16[12,8,2048]{2,1,0:T(8,128)(2,1)S(1)}, bf16[96,8,4096]{2,1,0:T(8,128)(2,1)S(1)}) custom-call(s32[96]{0:T(128)S(1)} %copy-done.2, bf16[128,8,4096]{2,1,0:T(8,128)(2,1)} %all-to-all-done.1.arrived, ...), custom_call_target="tpu_custom_call" | custom-call | flops 6291456 | bytes 3145728 | tf_op jit(solution)/shard_map/faces/pallas_call | solution.py:326
  140.9 1.9 %collective-permute-start = (bf16[12,8,2048]{2,1,0:T(8,128)(2,1)S(1)}, bf16[12,8,2048]{2,1,0:T(8,128)(2,1)S(1)}, u32[]{:S(2)}, u32[]{:S(2)}) collective-permute-start(bf16[12,8,2048]{2,1,0:T(8,128)(2,1)S(1)} %get-tuple-element.23), channel_id=1, source_target_pairs={{1,0},{2,1},{3,2},{4,3},{5,4},{6,5},{7,6},{8,7},{9,8},{10,9},{11,1... | collective-permute-start | bytes 1179656 | tf_op jit(solution)/shard_map/ppermute | solution.py:515
  142.9 2.5 %advance0.1 = (f32[96,8,1024]{2,1,0:T(8,128)S(1)}, f32[8,128]{1,0:T(8,128)S(1)}) custom-call(bf16[96,8,4096]{2,1,0:T(8,128)(2,1)S(1)} %get-tuple-element.25.refs_0_, f32[96,8,128]{2,1,0:T(8,128)S(1)} %broadcast_in_dim.10.mask.refs_1_, f32[96,8,128]{2,1,0:T(8,128)S(1)} %broadcast_multiply_fusion.refs_2_.rate, f32[8,128]{1,0:T(8,128)S(1)} %broadcast_in_dim.24.refs_3_), custom_call_target="tpu_custom_call" | custom-call | flops 78643200 | bytes 4718592 | tf_op jit(solution)/shard_map/advance0/pallas_call | solution.py:417
  145.4 3.5 %collective-permute-start.1 = (bf16[12,8,2048]{2,1,0:T(8,128)(2,1)S(1)}, bf16[12,8,2048]{2,1,0:T(8,128)(2,1)S(1)}, u32[]{:S(2)}, u32[]{:S(2)}) collective-permute-start(bf16[12,8,2048]{2,1,0:T(8,128)(2,1)S(1)} %get-tuple-element.27), channel_id=1, source_target_pairs={{0,1},{1,2},{2,3},{3,4},{4,5},{5,6},{6,7},{7,8},{8,9},{9,10},{10,1... | collective-permute-start | bytes 1179656 | tf_op jit(solution)/shard_map/ppermute | solution.py:515
  148.9 2.5 %advance1.1 = (f32[96,8,1024]{2,1,0:T(8,128)S(1)}, f32[8,128]{1,0:T(8,128)S(1)}) custom-call(bf16[96,8,4096]{2,1,0:T(8,128)(2,1)S(1)} %get-tuple-element.25.refs_0_, f32[96,8,128]{2,1,0:T(8,128)S(1)} %broadcast_in_dim.10.mask.refs_1_, f32[96,8,128]{2,1,0:T(8,128)S(1)} %broadcast_multiply_fusion.refs_2_.rate, f32[8,128]{1,0:T(8,128)S(1)} %get-tuple-element.29.refs_3_), custom_call_target="tpu_custom_call" | custom-call | flops 78643200 | bytes 4718592 | tf_op jit(solution)/shard_map/advance1/pallas_call | solution.py:417
  151.4 3.3 %collective-permute-start.2 = (bf16[12,8,2048]{2,1,0:T(8,128)(2,1)S(1)}, bf16[12,8,2048]{2,1,0:T(8,128)(2,1)S(1)}, u32[]{:S(2)}, u32[]{:S(2)}) collective-permute-start(bf16[12,8,2048]{2,1,0:T(8,128)(2,1)S(1)} %get-tuple-element.31), channel_id=1, source_target_pairs={{16,0},{32,16},{48,32},{64,48},{80,64},{96,80},{112,96},{17,1},{33... | collective-permute-start | bytes 1179656 | tf_op jit(solution)/shard_map/ppermute | solution.py:515
  154.8 2.5 %advance2.1 = (f32[96,8,1024]{2,1,0:T(8,128)S(1)}, f32[8,128]{1,0:T(8,128)S(1)}) custom-call(bf16[96,8,4096]{2,1,0:T(8,128)(2,1)S(1)} %get-tuple-element.25.refs_0_, f32[96,8,128]{2,1,0:T(8,128)S(1)} %broadcast_in_dim.10.mask.refs_1_, f32[96,8,128]{2,1,0:T(8,128)S(1)} %broadcast_multiply_fusion.refs_2_.rate, f32[8,128]{1,0:T(8,128)S(1)} %get-tuple-element.33.refs_3_), custom_call_target="tpu_custom_call" | custom-call | flops 78643200 | bytes 4718592 | tf_op jit(solution)/shard_map/advance2/pallas_call | solution.py:417
  157.3 2.7 %collective-permute-start.3 = (bf16[12,8,2048]{2,1,0:T(8,128)(2,1)S(1)}, bf16[12,8,2048]{2,1,0:T(8,128)(2,1)S(1)}, u32[]{:S(2)}, u32[]{:S(2)}) collective-permute-start(bf16[12,8,2048]{2,1,0:T(8,128)(2,1)S(1)} %get-tuple-element.35), channel_id=1, source_target_pairs={{0,16},{16,32},{32,48},{48,64},{64,80},{80,96},{96,112},{1,17},{17... | collective-permute-start | bytes 1179656 | tf_op jit(solution)/shard_map/ppermute | solution.py:515
  160.0 3.0 %advance3.1 = (f32[96,8,1024]{2,1,0:T(8,128)S(1)}, f32[8,128]{1,0:T(8,128)}) custom-call(bf16[96,8,4096]{2,1,0:T(8,128)(2,1)S(1)} %get-tuple-element.25.refs_0_, f32[96,8,128]{2,1,0:T(8,128)S(1)} %broadcast_in_dim.10.mask.refs_1_, f32[96,8,128]{2,1,0:T(8,128)S(1)} %broadcast_multiply_fusion.refs_2_.rate, f32[8,128]{1,0:T(8,128)S(1)} %get-tuple-element.39.refs_3_), custom_call_target="tpu_custom_call" | custom-call | flops 78643200 | bytes 4718592 | tf_op jit(solution)/shard_map/advance3/pallas_call | solution.py:417
  163.1 1.7 collective-permute-done.3.up_x
  164.7 3.6 %edge.1 = bf16[96,8,4096]{2,1,0:T(8,128)(2,1)} custom-call(f32[96,8,128]{2,1,0:T(8,128)S(1)} %broadcast_multiply_fusion.refs_2_.rate, bf16[12,8,2048]{2,1,0:T(8,128)(2,1)S(1)} %collective-permute-done.down_y, bf16[12,8,2048]{2,1,0:T(8,128)(2,1)S(1)} %collective-permute-done.1.up_y, bf16[12,8,2048]{2,1,0:T(8,128)(2,1)S(1)} %collective-permute-done.2.down_x, ...), custom_call_target="tpu_custom_call" | custom-call | flops 12582912 | bytes 18874368 | tf_op jit(solution)/shard_map/edge/pallas_call | solution.py:481
  (16 shorter events, 0.1 us)
Async XLA Ops:
  1.6 18.6 %all-to-all-start = ((s32[128,1,128]{2,1,0:T(1,128)}), s32[128,1,128]{2,1,0:T(1,128)S(1)}, u32[]{:S(2)}, u32[]{:S(2)}) async-start(s32[128,1,128]{2,1,0:T(1,128)} %broadcast_in_dim.12), calls=%async_computation | async-start | bytes 131072 | tf_op jit(solution)/shard_map/all_to_all | solution.py:529
  12.4 1.0 copy-start
  13.4 6.8 %copy-start.1 = (bf16[48,4096]{1,0:T(8,128)(2,1)S(1)}, bf16[48,4096]{1,0:T(8,128)(2,1)}, u32[]{:S(2)}) copy-start(bf16[48,4096]{1,0:T(8,128)(2,1)} %constant.15.clone.basis_rows.basis) | copy-start | bytes 1179652
  26.1 9.0 %copy-start.3 = (s32[96,8]{0,1:T(8,128)S(1)}, s32[96,8]{0,1:T(8,128)}, u32[]{:S(2)}) copy-start(s32[96,8]{0,1:T(8,128)} %param.8) | copy-start | bytes 9220
  26.1 9.2 %copy-start.4 = (s32[96]{0:T(128)S(1)}, s32[96]{0:T(128)}, u32[]{:S(2)}) copy-start(s32[96]{0:T(128)} %param.7) | copy-start | bytes 1156
  26.1 110.9 %copy-start.2 = (s32[96]{0:T(128)S(1)}, s32[96]{0:T(128)}, u32[]{:S(2)}) copy-start(s32[96]{0:T(128)} %owner.1) | copy-start | bytes 1156
  26.1 110.7 %all-to-all-start.1 = ((bf16[128,8,4096]{2,1,0:T(8,128)(2,1)}), bf16[128,8,4096]{2,1,0:T(8,128)(2,1)}, u32[]{:S(2)}, u32[]{:S(2)}) async-start(bf16[128,8,4096]{2,1,0:T(8,128)(2,1)} %relax.1), calls=%async_computation.1 | async-start | bytes 16777216 | tf_op jit(solution)/shard_map/all_to_all | solution.py:534
  140.9 22.1 %collective-permute-start = (bf16[12,8,2048]{2,1,0:T(8,128)(2,1)S(1)}, bf16[12,8,2048]{2,1,0:T(8,128)(2,1)S(1)}, u32[]{:S(2)}, u32[]{:S(2)}) collective-permute-start(bf16[12,8,2048]{2,1,0:T(8,128)(2,1)S(1)} %get-tuple-element.23), channel_id=1, source_target_pairs={{1,0},{2,1},{3,2},{4,3},{5,4},{6,5},{7,6},{8,7},{9,8},{10,9},{11,1... | collective-permute-start | bytes 1179656 | tf_op jit(solution)/shard_map/ppermute | solution.py:515
  145.4 17.7 %collective-permute-start.1 = (bf16[12,8,2048]{2,1,0:T(8,128)(2,1)S(1)}, bf16[12,8,2048]{2,1,0:T(8,128)(2,1)S(1)}, u32[]{:S(2)}, u32[]{:S(2)}) collective-permute-start(bf16[12,8,2048]{2,1,0:T(8,128)(2,1)S(1)} %get-tuple-element.27), channel_id=1, source_target_pairs={{0,1},{1,2},{2,3},{3,4},{4,5},{5,6},{6,7},{7,8},{8,9},{9,10},{10,1... | collective-permute-start | bytes 1179656 | tf_op jit(solution)/shard_map/ppermute | solution.py:515
  151.4 11.6 %collective-permute-start.2 = (bf16[12,8,2048]{2,1,0:T(8,128)(2,1)S(1)}, bf16[12,8,2048]{2,1,0:T(8,128)(2,1)S(1)}, u32[]{:S(2)}, u32[]{:S(2)}) collective-permute-start(bf16[12,8,2048]{2,1,0:T(8,128)(2,1)S(1)} %get-tuple-element.31), channel_id=1, source_target_pairs={{16,0},{32,16},{48,32},{64,48},{80,64},{96,80},{112,96},{17,1},{33... | collective-permute-start | bytes 1179656 | tf_op jit(solution)/shard_map/ppermute | solution.py:515
  157.3 7.4 %collective-permute-start.3 = (bf16[12,8,2048]{2,1,0:T(8,128)(2,1)S(1)}, bf16[12,8,2048]{2,1,0:T(8,128)(2,1)S(1)}, u32[]{:S(2)}, u32[]{:S(2)}) collective-permute-start(bf16[12,8,2048]{2,1,0:T(8,128)(2,1)S(1)} %get-tuple-element.35), channel_id=1, source_target_pairs={{0,16},{16,32},{32,48},{48,64},{64,80},{80,96},{96,112},{1,17},{17... | collective-permute-start | bytes 1179656 | tf_op jit(solution)/shard_map/ppermute | solution.py:515

commit v10 on v8

--- a/solution.py
+++ b/solution.py
@@ -81,7 +81,7 @@
     return [LOG2E * r for r in rows], fraction
 
 
-def moments_kernel(dist, basis, factors, held, sums, in_sems):
+def moments_kernel(dist, factors, held, basis, sums, in_sems):
     pieces = BLOCKS // PIECE
 
     def arrival(piece):
@@ -90,12 +90,21 @@
 
     for piece in range(pieces):
         arrival(piece).start()
+    point = lax.broadcasted_iota(jnp.int32, (1, TOTAL), 1)
+    x, y, z = (
+        (2 * i + 1 - VS).astype(jnp.float32)
+        for i in (point >> 8, (point >> 4) & (VS - 1), point & (VS - 1))
+    )
+    table = [jnp.ones_like(x), x, y, z, x * x, y * y, z * z, x * y, x * z, y * z]
+    basis[...] = jnp.concatenate(
+        table + [jnp.zeros((6, TOTAL), jnp.float32)], axis=0
+    ).astype(jnp.bfloat16)
     for piece in range(pieces):
         arrival(piece).wait()
         cells = held[pl.ds(piece * PIECE, PIECE)].astype(jnp.float32)
         cells = cells.reshape(PIECE * CELLS, TOTAL).astype(jnp.bfloat16)
         sums[:, pl.ds(piece * PIECE * CELLS, PIECE * CELLS)] = lax.dot_general(
-            basis[0:16, :], cells, (((1,), (1,)), ((), ())), preferred_element_type=jnp.float32
+            basis[...], cells, (((1,), (1,)), ((), ())), preferred_element_type=jnp.float32
         )
 
     rows, fraction = coefficients_of(sums[...])
@@ -123,14 +132,15 @@
 WHOLE = (BLOCKS, CELLS, TOTAL)
 
 
-def moments(dist, basis):
+def moments(dist):
     return pl.pallas_call(
         moments_kernel,
         out_shape=jax.ShapeDtypeStruct((BLOCKS * CELLS, 128), jnp.float32),
-        in_specs=[ANY, VMEM],
+        in_specs=[ANY],
         out_specs=VMEM,
         scratch_shapes=[
             pltpu.VMEM(WHOLE, jnp.bfloat16),
+            pltpu.VMEM((16, TOTAL), jnp.bfloat16),
             pltpu.VMEM((16, BLOCKS * CELLS), jnp.float32),
             pltpu.SemaphoreType.DMA((BLOCKS // PIECE,)),
         ],
@@ -141,7 +151,7 @@
             transcendentals=0,
         ),
         name="moments",
-    )(dist, basis)
+    )(dist)
 
 
 def relax_kernel(
@@ -502,15 +512,13 @@
     axes = ("gx", "gy")
     devices = lax.axis_size("gx") * lax.axis_size("gy")
     owners = lax.broadcasted_iota(jnp.int32, (devices, BLOCKS), 0)
-    slots = lax.broadcasted_iota(jnp.int32, (devices, BLOCKS), 1)
-    request = BLOCKS + jnp.sum(
-        jnp.where(source_owner[None, :] == owners, slots - BLOCKS, 0), axis=1, keepdims=True
-    )
-    asked = lax.all_to_all(
-        jnp.broadcast_to(request, (devices, 128)), axes, split_axis=0, concat_axis=0, tiled=True
-    )
-    basis = jnp.asarray(basis_rows())
-    send = relax(asked, dist_old, basis, moments(dist_old, basis))
+    wanted = (source_owner[None, :] == owners).astype(jnp.bfloat16)
+    slots = lax.broadcasted_iota(jnp.int32, (BLOCKS, 128), 0) - BLOCKS
+    request = BLOCKS + jnp.dot(
+        wanted, slots.astype(jnp.bfloat16), preferred_element_type=jnp.float32
+    ).astype(jnp.int32)
+    asked = lax.all_to_all(request, axes, split_axis=0, concat_axis=0, tiled=True)
+    send = relax(asked, dist_old, jnp.asarray(basis_rows()), moments(dist_old))
     received = lax.all_to_all(send, axes, split_axis=0, concat_axis=0, tiled=True)
     return after(received, source_owner, levels, active)
 

time: 165 us -> 164 us (level)
  local copies, waits for them, and re-layouts: 2.1 us -> 0.27 us
where the time goes in v10:
time: 164 us; the launch traced here: 163 us
  waiting for transfers between devices  104 us (63%)
  starting transfers between devices  30.2 us (18%)
  Pallas kernels  27.1 us (17%)
    all_to_all x1, waiting for transfers between devices, per_device(): lax.all_to_all(send, axes, split_axis=0, concat_axis=0, tiled=True)  102 us
    ppermute x4, starting transfers between devices, after(): halos.append(lax.ppermute(face, name, up(n) if to_above else down(n)))  11.5 us
    all_to_all x1, starting transfers between devices, per_device(): lax.all_to_all(request, axes, split_axis=0, concat_axis=0, tiled=True)  10.8 us
    pallas_call x1, Pallas kernels, advance(): pl.pallas_call(advance_kernel, out_shape=jax.ShapeDtypeStruct(WHOLE, jnp....  8.04 us
    all_to_all x1, starting transfers between devices, per_device(): lax.all_to_all(send, axes, split_axis=0, concat_axis=0, tiled=True)  7.92 us
    pallas_call x1, Pallas kernels, relax(): pl.pallas_call(relax_kernel, out_shape=jax.ShapeDtypeStruct((devices, CEL...  5.84 us
    pallas_call x1, Pallas kernels, moments(): pl.pallas_call(moments_kernel, out_shape=jax.ShapeDtypeStruct((BLOCKS * C...  5.46 us
    pallas_call x1, Pallas kernels, faces(): pl.pallas_call(faces_kernel, out_shape=[jax.ShapeDtypeStruct(FACE, jnp.bf...  3.94 us
  transfers between devices with their start and end apart: 6, of which 2 were waited for; matrix products, arithmetic and copies ran while one was open for 0% of the time, Pallas kernels for 8%

profile of v10, /device:TPU:7, one launch (start us, length us, event | category | flops | bytes accessed | tf_op | source)
XLA Modules:
  0.0 163.4 jit_solution(12677045533984630356)
XLA Ops:
  0.0 1.5 fusion
  1.5 10.8 %all-to-all-start = ((s32[128,1,128]{2,1,0:T(1,128)}), s32[128,1,128]{2,1,0:T(1,128)S(1)}, u32[]{:S(2)}, u32[]{:S(2)}) async-start(s32[128,1,128]{2,1,0:T(1,128)} %bitcast.1), calls=%async_computation | async-start | bytes 131072 | tf_op jit(solution)/shard_map/all_to_all | solution.py:520
  12.3 0.0 copy-start
  12.3 5.5 %moments.1.factors = f32[768,128]{1,0:T(8,128)S(1)} custom-call(bf16[96,8,4096]{2,1,0:T(8,128)(2,1)} %dist.3), custom_call_target="tpu_custom_call" | custom-call | flops 9437184000 | bytes 6291456 | tf_op jit(solution)/shard_map/moments/pallas_call | solution.py:136
  17.8 2.4 %all-to-all-done = s32[128,1,128]{2,1,0:T(1,128)S(1)} async-done(((s32[128,1,128]{2,1,0:T(1,128)}), s32[128,1,128]{2,1,0:T(1,128)S(1)}, u32[]{:S(2)}, u32[]{:S(2)}) %all-to-all-start) | async-done | bytes 65568 | tf_op jit(solution)/shard_map/all_to_all | solution.py:520
  20.1 5.8 %relax.1 = bf16[128,8,4096]{2,1,0:T(8,128)(2,1)} custom-call(s32[128,128]{1,0:T(8,128)S(1)} %bitcast.4, bf16[96,8,4096]{2,1,0:T(8,128)(2,1)} %dist.3, bf16[48,4096]{1,0:T(8,128)(2,1)S(1)} %copy-done, f32[768,128]{1,0:T(8,128)S(1)} %moments.1.factors), custom_call_target="tpu_custom_call" | custom-call | flops 402653184 | bytes 12582912 | tf_op jit(solution)/shard_map/relax/pallas_call | solution.py:205
  26.0 0.0 copy-start.2
  26.0 0.0 copy-start.1
  26.0 7.9 %all-to-all-start.1 = ((bf16[128,8,4096]{2,1,0:T(8,128)(2,1)}), bf16[128,8,4096]{2,1,0:T(8,128)(2,1)}, u32[]{:S(2)}, u32[]{:S(2)}) async-start(bf16[128,8,4096]{2,1,0:T(8,128)(2,1)} %relax.1), calls=%async_computation.1 | async-start | bytes 16777216 | tf_op jit(solution)/shard_map/all_to_all | solution.py:522
  33.9 0.0 copy-start.3
  34.0 0.1 copy.8
  34.1 101.6 %all-to-all-done.1.arrived = bf16[128,8,4096]{2,1,0:T(8,128)(2,1)} async-done(((bf16[128,8,4096]{2,1,0:T(8,128)(2,1)}), bf16[128,8,4096]{2,1,0:T(8,128)(2,1)}, u32[]{:S(2)}, u32[]{:S(2)}) %all-to-all-start.1) | async-done | bytes 8388640 | tf_op jit(solution)/shard_map/all_to_all | solution.py:522
  135.6 0.2 broadcast_in_dim.2.mask
  135.8 3.9 %faces.1 = (bf16[12,8,2048]{2,1,0:T(8,128)(2,1)S(1)}, bf16[12,8,2048]{2,1,0:T(8,128)(2,1)S(1)}, bf16[12,8,2048]{2,1,0:T(8,128)(2,1)S(1)}, bf16[12,8,2048]{2,1,0:T(8,128)(2,1)S(1)}, bf16[96,8,4096]{2,1,0:T(8,128)(2,1)S(1)}) custom-call(s32[96]{0:T(128)S(1)} %copy-done.1, bf16[128,8,4096]{2,1,0:T(8,128)(2,1)} %all-to-all-done.1.arrived, ...), custom_call_target="tpu_custom_call" | custom-call | flops 6291456 | bytes 3145728 | tf_op jit(solution)/shard_map/faces/pallas_call | solution.py:329
  139.8 1.9 %collective-permute-start = (bf16[12,8,2048]{2,1,0:T(8,128)(2,1)S(1)}, bf16[12,8,2048]{2,1,0:T(8,128)(2,1)S(1)}, u32[]{:S(2)}, u32[]{:S(2)}) collective-permute-start(bf16[12,8,2048]{2,1,0:T(8,128)(2,1)S(1)} %get-tuple-element.11), channel_id=1, source_target_pairs={{1,0},{2,1},{3,2},{4,3},{5,4},{6,5},{7,6},{8,7},{9,8},{10,9},{11,1... | collective-permute-start | bytes 1179656 | tf_op jit(solution)/shard_map/ppermute | solution.py:507
  141.7 3.5 %collective-permute-start.1 = (bf16[12,8,2048]{2,1,0:T(8,128)(2,1)S(1)}, bf16[12,8,2048]{2,1,0:T(8,128)(2,1)S(1)}, u32[]{:S(2)}, u32[]{:S(2)}) collective-permute-start(bf16[12,8,2048]{2,1,0:T(8,128)(2,1)S(1)} %get-tuple-element.12), channel_id=1, source_target_pairs={{0,1},{1,2},{2,3},{3,4},{4,5},{5,6},{6,7},{7,8},{8,9},{9,10},{10,1... | collective-permute-start | bytes 1179656 | tf_op jit(solution)/shard_map/ppermute | solution.py:507
  145.2 3.3 %collective-permute-start.2 = (bf16[12,8,2048]{2,1,0:T(8,128)(2,1)S(1)}, bf16[12,8,2048]{2,1,0:T(8,128)(2,1)S(1)}, u32[]{:S(2)}, u32[]{:S(2)}) collective-permute-start(bf16[12,8,2048]{2,1,0:T(8,128)(2,1)S(1)} %get-tuple-element.13), channel_id=1, source_target_pairs={{16,0},{32,16},{48,32},{64,48},{80,64},{96,80},{112,96},{17,1},{33... | collective-permute-start | bytes 1179656 | tf_op jit(solution)/shard_map/ppermute | solution.py:507
  148.5 2.7 %collective-permute-start.3 = (bf16[12,8,2048]{2,1,0:T(8,128)(2,1)S(1)}, bf16[12,8,2048]{2,1,0:T(8,128)(2,1)S(1)}, u32[]{:S(2)}, u32[]{:S(2)}) collective-permute-start(bf16[12,8,2048]{2,1,0:T(8,128)(2,1)S(1)} %get-tuple-element.14), channel_id=1, source_target_pairs={{0,16},{16,32},{32,48},{48,64},{64,80},{80,96},{96,112},{1,17},{17... | collective-permute-start | bytes 1179656 | tf_op jit(solution)/shard_map/ppermute | solution.py:507
  151.3 0.3 broadcast_multiply_fusion.rate
  151.6 8.0 %advance.1.partial = f32[96,8,4096]{2,1,0:T(8,128)S(1)} custom-call(bf16[96,8,4096]{2,1,0:T(8,128)(2,1)S(1)} %get-tuple-element.10.received, f32[96,8,128]{2,1,0:T(8,128)S(1)} %broadcast_in_dim.2.mask, f32[96,8,128]{2,1,0:T(8,128)S(1)} %broadcast_multiply_fusion.rate), custom_call_target="tpu_custom_call" | custom-call | flops 314572800 | bytes 18874368 | tf_op jit(solution)/shard_map/advance/pallas_call | solution.py:418
  159.6 0.0 collective-permute-done.down_y
  159.6 0.0 collective-permute-done.1.up_y
  159.6 0.0 collective-permute-done.3.up_x
  159.6 3.8 %edge.1 = bf16[96,8,4096]{2,1,0:T(8,128)(2,1)} custom-call(f32[96,8,4096]{2,1,0:T(8,128)S(1)} %advance.1.partial, f32[96,8,128]{2,1,0:T(8,128)S(1)} %broadcast_multiply_fusion.rate, bf16[12,8,2048]{2,1,0:T(8,128)(2,1)S(1)} %collective-permute-done.down_y, bf16[12,8,2048]{2,1,0:T(8,128)(2,1)S(1)} %collective-permute-done.1.up_y, ...), custom_call_target="tpu_custom_call" | custom-call | flops 12582912 | bytes 18874368 | tf_op jit(solution)/shard_map/edge/pallas_call | solution.py:475
  (8 shorter events, 0.0 us)
Async XLA Ops:
  1.5 18.6 %all-to-all-start = ((s32[128,1,128]{2,1,0:T(1,128)}), s32[128,1,128]{2,1,0:T(1,128)S(1)}, u32[]{:S(2)}, u32[]{:S(2)}) async-start(s32[128,1,128]{2,1,0:T(1,128)} %bitcast.1), calls=%async_computation | async-start | bytes 131072 | tf_op jit(solution)/shard_map/all_to_all | solution.py:520
  12.3 7.8 %copy-start = (bf16[48,4096]{1,0:T(8,128)(2,1)S(1)}, bf16[48,4096]{1,0:T(8,128)(2,1)}, u32[]{:S(2)}) copy-start(bf16[48,4096]{1,0:T(8,128)(2,1)} %constant.11.clone.basis) | copy-start | bytes 1179652
  26.0 8.0 %copy-start.2 = (s32[96,8]{0,1:T(8,128)S(1)}, s32[96,8]{0,1:T(8,128)}, u32[]{:S(2)}) copy-start(s32[96,8]{0,1:T(8,128)} %param.8) | copy-start | bytes 9220
  26.0 109.8 %copy-start.1 = (s32[96]{0:T(128)S(1)}, s32[96]{0:T(128)}, u32[]{:S(2)}) copy-start(s32[96]{0:T(128)} %owner.1) | copy-start | bytes 1156
  26.0 109.6 %all-to-all-start.1 = ((bf16[128,8,4096]{2,1,0:T(8,128)(2,1)}), bf16[128,8,4096]{2,1,0:T(8,128)(2,1)}, u32[]{:S(2)}, u32[]{:S(2)}) async-start(bf16[128,8,4096]{2,1,0:T(8,128)(2,1)} %relax.1), calls=%async_computation.1 | async-start | bytes 16777216 | tf_op jit(solution)/shard_map/all_to_all | solution.py:522
  33.9 117.3 %copy-start.3 = (s32[96]{0:T(128)S(1)}, s32[96]{0:T(128)}, u32[]{:S(2)}) copy-start(s32[96]{0:T(128)} %param.7) | copy-start | bytes 1156
  139.8 19.8 %collective-permute-start = (bf16[12,8,2048]{2,1,0:T(8,128)(2,1)S(1)}, bf16[12,8,2048]{2,1,0:T(8,128)(2,1)S(1)}, u32[]{:S(2)}, u32[]{:S(2)}) collective-permute-start(bf16[12,8,2048]{2,1,0:T(8,128)(2,1)S(1)} %get-tuple-element.11), channel_id=1, source_target_pairs={{1,0},{2,1},{3,2},{4,3},{5,4},{6,5},{7,6},{8,7},{9,8},{10,9},{11,1... | collective-permute-start | bytes 1179656 | tf_op jit(solution)/shard_map/ppermute | solution.py:507
  141.7 17.9 %collective-permute-start.1 = (bf16[12,8,2048]{2,1,0:T(8,128)(2,1)S(1)}, bf16[12,8,2048]{2,1,0:T(8,128)(2,1)S(1)}, u32[]{:S(2)}, u32[]{:S(2)}) collective-permute-start(bf16[12,8,2048]{2,1,0:T(8,128)(2,1)S(1)} %get-tuple-element.12), channel_id=1, source_target_pairs={{0,1},{1,2},{2,3},{3,4},{4,5},{5,6},{6,7},{7,8},{8,9},{9,10},{10,1... | collective-permute-start | bytes 1179656 | tf_op jit(solution)/shard_map/ppermute | solution.py:507
  145.2 14.4 %collective-permute-start.2 = (bf16[12,8,2048]{2,1,0:T(8,128)(2,1)S(1)}, bf16[12,8,2048]{2,1,0:T(8,128)(2,1)S(1)}, u32[]{:S(2)}, u32[]{:S(2)}) collective-permute-start(bf16[12,8,2048]{2,1,0:T(8,128)(2,1)S(1)} %get-tuple-element.13), channel_id=1, source_target_pairs={{16,0},{32,16},{48,32},{64,48},{80,64},{96,80},{112,96},{17,1},{33... | collective-permute-start | bytes 1179656 | tf_op jit(solution)/shard_map/ppermute | solution.py:507
  148.5 11.1 %collective-permute-start.3 = (bf16[12,8,2048]{2,1,0:T(8,128)(2,1)S(1)}, bf16[12,8,2048]{2,1,0:T(8,128)(2,1)S(1)}, u32[]{:S(2)}, u32[]{:S(2)}) collective-permute-start(bf16[12,8,2048]{2,1,0:T(8,128)(2,1)S(1)} %get-tuple-element.14), channel_id=1, source_target_pairs={{0,16},{16,32},{32,48},{48,64},{64,80},{80,96},{96,112},{1,17},{17... | collective-permute-start | bytes 1179656 | tf_op jit(solution)/shard_map/ppermute | solution.py:507

commit v11 on v10

--- a/solution.py
+++ b/solution.py
@@ -262,7 +262,7 @@
 PLACES = {column: BZ * n for n, column in enumerate(c for group in GROUPS for c in group)}
 
 
-def faces_kernel(owner, arrived, mask, *rest):
+def faces_kernel(owner, arrived, mask, _, *rest):
     sent, (received, sems) = rest[: len(FACES)], rest[len(FACES) :]
     low_x, low_y, _ = row_masks()
 
@@ -324,13 +324,13 @@
     arrive(4)
 
 
-def faces(owner, received, mask):
+def faces(owner, received, mask, rate):
     moved = 4 * math.prod(FACE)
     return pl.pallas_call(
         faces_kernel,
         out_shape=[jax.ShapeDtypeStruct(FACE, jnp.bfloat16) for _ in FACES]
         + [jax.ShapeDtypeStruct(WHOLE, received.dtype)],
-        in_specs=[pl.BlockSpec(memory_space=pltpu.SMEM), ANY, VMEM],
+        in_specs=[pl.BlockSpec(memory_space=pltpu.SMEM), ANY, VMEM, ANY],
         out_specs=[VMEM] * (len(FACES) + 1),
         scratch_shapes=[pltpu.SemaphoreType.DMA((len(GROUPS),))],
         compiler_params=pltpu.CompilerParams(vmem_limit_bytes=FACES_VMEM),
@@ -338,7 +338,7 @@
             flops=8 * moved, bytes_accessed=4 * moved, transcendentals=0
         ),
         name="faces",
-    )(owner, received, mask)
+    )(owner, received, mask, rate)
 
 
 def speeds():
@@ -454,7 +454,7 @@
         rows = pl.ds(bx * SLAB, SLAB)
         return pltpu.make_async_copy(made.at[rows], out.at[rows], sems.at[bx])
 
-    for bx in range(BX):
+    for bx in (1, 2, 0, 3):
         if bx == 0:
             add(up_x, "x", 1, (0, 12))
         if bx == BX - 1:
@@ -500,7 +500,7 @@
     def down(n):
         return [(i + 1, i) for i in range(n - 1)]
 
-    *sent, received = faces(source_owner, received, mask)
+    *sent, received = faces(source_owner, received, mask, rate)
     halos = []
     for (axis, to_above), face in zip(FACES, sent):
         name, n = ("gx", n_gx) if axis == "x" else ("gy", n_gy)

time: 164 us -> 164 us (level)
  no operation moved by 1% of the time
where the time goes in v11:
time: 164 us; the launch traced here: 163 us
  waiting for transfers between devices  104 us (63%)
  starting transfers between devices  30.2 us (18%)
  Pallas kernels  27.1 us (17%)
    all_to_all x1, waiting for transfers between devices, per_device(): lax.all_to_all(send, axes, split_axis=0, concat_axis=0, tiled=True)  101 us
    ppermute x4, starting transfers between devices, after(): halos.append(lax.ppermute(face, name, up(n) if to_above else down(n)))  11.5 us
    all_to_all x1, starting transfers between devices, per_device(): lax.all_to_all(request, axes, split_axis=0, concat_axis=0, tiled=True)  10.8 us
    pallas_call x1, Pallas kernels, advance(): pl.pallas_call(advance_kernel, out_shape=jax.ShapeDtypeStruct(WHOLE, jnp....  8.04 us
    all_to_all x1, starting transfers between devices, per_device(): lax.all_to_all(send, axes, split_axis=0, concat_axis=0, tiled=True)  7.92 us
    pallas_call x1, Pallas kernels, relax(): pl.pallas_call(relax_kernel, out_shape=jax.ShapeDtypeStruct((devices, CEL...  5.85 us
    pallas_call x1, Pallas kernels, moments(): pl.pallas_call(moments_kernel, out_shape=jax.ShapeDtypeStruct((BLOCKS * C...  5.46 us
    pallas_call x1, Pallas kernels, faces(): pl.pallas_call(faces_kernel, out_shape=[jax.ShapeDtypeStruct(FACE, jnp.bf...  3.95 us
  transfers between devices with their start and end apart: 6, of which 2 were waited for; matrix products, arithmetic and copies ran while one was open for 0% of the time, Pallas kernels for 8%

profile of v11, /device:TPU:7, one launch (start us, length us, event | category | flops | bytes accessed | tf_op | source)
XLA Modules:
  0.0 163.2 jit_solution(16306823547564897)
XLA Ops:
  0.0 1.5 fusion
  1.5 10.8 %all-to-all-start = ((s32[128,1,128]{2,1,0:T(1,128)}), s32[128,1,128]{2,1,0:T(1,128)S(1)}, u32[]{:S(2)}, u32[]{:S(2)}) async-start(s32[128,1,128]{2,1,0:T(1,128)} %bitcast.1), calls=%async_computation | async-start | bytes 131072 | tf_op jit(solution)/shard_map/all_to_all | solution.py:520
  12.3 0.0 copy-start
  12.3 5.5 %moments.1.factors = f32[768,128]{1,0:T(8,128)S(1)} custom-call(bf16[96,8,4096]{2,1,0:T(8,128)(2,1)} %dist.3), custom_call_target="tpu_custom_call" | custom-call | flops 9437184000 | bytes 6291456 | tf_op jit(solution)/shard_map/moments/pallas_call | solution.py:136
  17.8 2.4 %all-to-all-done = s32[128,1,128]{2,1,0:T(1,128)S(1)} async-done(((s32[128,1,128]{2,1,0:T(1,128)}), s32[128,1,128]{2,1,0:T(1,128)S(1)}, u32[]{:S(2)}, u32[]{:S(2)}) %all-to-all-start) | async-done | bytes 65568 | tf_op jit(solution)/shard_map/all_to_all | solution.py:520
  20.1 5.9 %relax.1 = bf16[128,8,4096]{2,1,0:T(8,128)(2,1)} custom-call(s32[128,128]{1,0:T(8,128)S(1)} %bitcast.4, bf16[96,8,4096]{2,1,0:T(8,128)(2,1)} %dist.3, bf16[48,4096]{1,0:T(8,128)(2,1)S(1)} %copy-done, f32[768,128]{1,0:T(8,128)S(1)} %moments.1.factors), custom_call_target="tpu_custom_call" | custom-call | flops 402653184 | bytes 12582912 | tf_op jit(solution)/shard_map/relax/pallas_call | solution.py:205
  26.0 0.0 copy-start.2
  26.0 0.0 copy-start.3
  26.0 0.0 copy-start.1
  26.0 7.9 %all-to-all-start.1 = ((bf16[128,8,4096]{2,1,0:T(8,128)(2,1)}), bf16[128,8,4096]{2,1,0:T(8,128)(2,1)}, u32[]{:S(2)}, u32[]{:S(2)}) async-start(bf16[128,8,4096]{2,1,0:T(8,128)(2,1)} %relax.1), calls=%async_computation.1 | async-start | bytes 16777216 | tf_op jit(solution)/shard_map/all_to_all | solution.py:522
  34.0 0.1 copy.8
  34.1 0.3 broadcast_multiply_fusion._.rate
  34.4 101.3 %all-to-all-done.1.arrived = bf16[128,8,4096]{2,1,0:T(8,128)(2,1)} async-done(((bf16[128,8,4096]{2,1,0:T(8,128)(2,1)}), bf16[128,8,4096]{2,1,0:T(8,128)(2,1)}, u32[]{:S(2)}, u32[]{:S(2)}) %all-to-all-start.1) | async-done | bytes 8388640 | tf_op jit(solution)/shard_map/all_to_all | solution.py:522
  135.6 0.2 broadcast_in_dim.2.mask
  135.8 3.9 %faces.1 = (bf16[12,8,2048]{2,1,0:T(8,128)(2,1)S(1)}, bf16[12,8,2048]{2,1,0:T(8,128)(2,1)S(1)}, bf16[12,8,2048]{2,1,0:T(8,128)(2,1)S(1)}, bf16[12,8,2048]{2,1,0:T(8,128)(2,1)S(1)}, bf16[96,8,4096]{2,1,0:T(8,128)(2,1)S(1)}) custom-call(s32[96]{0:T(128)S(1)} %copy-done.1, bf16[128,8,4096]{2,1,0:T(8,128)(2,1)} %all-to-all-done.1.arrived, ...), custom_call_target="tpu_custom_call" | custom-call | flops 6291456 | bytes 3145728 | tf_op jit(solution)/shard_map/faces/pallas_call | solution.py:329
  139.8 1.9 %collective-permute-start = (bf16[12,8,2048]{2,1,0:T(8,128)(2,1)S(1)}, bf16[12,8,2048]{2,1,0:T(8,128)(2,1)S(1)}, u32[]{:S(2)}, u32[]{:S(2)}) collective-permute-start(bf16[12,8,2048]{2,1,0:T(8,128)(2,1)S(1)} %get-tuple-element.11), channel_id=1, source_target_pairs={{1,0},{2,1},{3,2},{4,3},{5,4},{6,5},{7,6},{8,7},{9,8},{10,9},{11,1... | collective-permute-start | bytes 1179656 | tf_op jit(solution)/shard_map/ppermute | solution.py:507
  141.7 3.5 %collective-permute-start.1 = (bf16[12,8,2048]{2,1,0:T(8,128)(2,1)S(1)}, bf16[12,8,2048]{2,1,0:T(8,128)(2,1)S(1)}, u32[]{:S(2)}, u32[]{:S(2)}) collective-permute-start(bf16[12,8,2048]{2,1,0:T(8,128)(2,1)S(1)} %get-tuple-element.12), channel_id=1, source_target_pairs={{0,1},{1,2},{2,3},{3,4},{4,5},{5,6},{6,7},{7,8},{8,9},{9,10},{10,1... | collective-permute-start | bytes 1179656 | tf_op jit(solution)/shard_map/ppermute | solution.py:507
  145.2 3.3 %collective-permute-start.2 = (bf16[12,8,2048]{2,1,0:T(8,128)(2,1)S(1)}, bf16[12,8,2048]{2,1,0:T(8,128)(2,1)S(1)}, u32[]{:S(2)}, u32[]{:S(2)}) collective-permute-start(bf16[12,8,2048]{2,1,0:T(8,128)(2,1)S(1)} %get-tuple-element.13), channel_id=1, source_target_pairs={{16,0},{32,16},{48,32},{64,48},{80,64},{96,80},{112,96},{17,1},{33... | collective-permute-start | bytes 1179656 | tf_op jit(solution)/shard_map/ppermute | solution.py:507
  148.5 2.7 %collective-permute-start.3 = (bf16[12,8,2048]{2,1,0:T(8,128)(2,1)S(1)}, bf16[12,8,2048]{2,1,0:T(8,128)(2,1)S(1)}, u32[]{:S(2)}, u32[]{:S(2)}) collective-permute-start(bf16[12,8,2048]{2,1,0:T(8,128)(2,1)S(1)} %get-tuple-element.14), channel_id=1, source_target_pairs={{0,16},{16,32},{32,48},{48,64},{64,80},{80,96},{96,112},{1,17},{17... | collective-permute-start | bytes 1179656 | tf_op jit(solution)/shard_map/ppermute | solution.py:507
  151.3 8.0 %advance.1.partial = f32[96,8,4096]{2,1,0:T(8,128)S(1)} custom-call(bf16[96,8,4096]{2,1,0:T(8,128)(2,1)S(1)} %get-tuple-element.10.received, f32[96,8,128]{2,1,0:T(8,128)S(1)} %broadcast_in_dim.2.mask, f32[96,8,128]{2,1,0:T(8,128)S(1)} %broadcast_multiply_fusion._.rate), custom_call_target="tpu_custom_call" | custom-call | flops 314572800 | bytes 18874368 | tf_op jit(solution)/shard_map/advance/pallas_call | solution.py:418
  159.3 0.0 collective-permute-done.down_y
  159.3 0.0 collective-permute-done.2.down_x
  159.3 0.0 collective-permute-done.3.up_x
  159.4 3.8 %edge.1 = bf16[96,8,4096]{2,1,0:T(8,128)(2,1)} custom-call(f32[96,8,4096]{2,1,0:T(8,128)S(1)} %advance.1.partial, f32[96,8,128]{2,1,0:T(8,128)S(1)} %broadcast_multiply_fusion._.rate, bf16[12,8,2048]{2,1,0:T(8,128)(2,1)S(1)} %collective-permute-done.down_y, bf16[12,8,2048]{2,1,0:T(8,128)(2,1)S(1)} %collective-permute-done.1.up_y, ...), custom_call_target="tpu_custom_call" | custom-call | flops 12582912 | bytes 18874368 | tf_op jit(solution)/shard_map/edge/pallas_call | solution.py:475
  (8 shorter events, 0.0 us)
Async XLA Ops:
  1.5 18.6 %all-to-all-start = ((s32[128,1,128]{2,1,0:T(1,128)}), s32[128,1,128]{2,1,0:T(1,128)S(1)}, u32[]{:S(2)}, u32[]{:S(2)}) async-start(s32[128,1,128]{2,1,0:T(1,128)} %bitcast.1), calls=%async_computation | async-start | bytes 131072 | tf_op jit(solution)/shard_map/all_to_all | solution.py:520
  12.3 7.8 %copy-start = (bf16[48,4096]{1,0:T(8,128)(2,1)S(1)}, bf16[48,4096]{1,0:T(8,128)(2,1)}, u32[]{:S(2)}) copy-start(bf16[48,4096]{1,0:T(8,128)(2,1)} %constant.11.clone.basis) | copy-start | bytes 1179652
  26.0 8.0 %copy-start.2 = (s32[96,8]{0,1:T(8,128)S(1)}, s32[96,8]{0,1:T(8,128)}, u32[]{:S(2)}) copy-start(s32[96,8]{0,1:T(8,128)} %param.8) | copy-start | bytes 9220
  26.0 8.1 %copy-start.3 = (s32[96]{0:T(128)S(1)}, s32[96]{0:T(128)}, u32[]{:S(2)}) copy-start(s32[96]{0:T(128)} %param.7) | copy-start | bytes 1156
  26.0 109.8 %copy-start.1 = (s32[96]{0:T(128)S(1)}, s32[96]{0:T(128)}, u32[]{:S(2)}) copy-start(s32[96]{0:T(128)} %owner.1) | copy-start | bytes 1156
  26.0 109.6 %all-to-all-start.1 = ((bf16[128,8,4096]{2,1,0:T(8,128)(2,1)}), bf16[128,8,4096]{2,1,0:T(8,128)(2,1)}, u32[]{:S(2)}, u32[]{:S(2)}) async-start(bf16[128,8,4096]{2,1,0:T(8,128)(2,1)} %relax.1), calls=%async_computation.1 | async-start | bytes 16777216 | tf_op jit(solution)/shard_map/all_to_all | solution.py:522
  139.8 19.5 %collective-permute-start = (bf16[12,8,2048]{2,1,0:T(8,128)(2,1)S(1)}, bf16[12,8,2048]{2,1,0:T(8,128)(2,1)S(1)}, u32[]{:S(2)}, u32[]{:S(2)}) collective-permute-start(bf16[12,8,2048]{2,1,0:T(8,128)(2,1)S(1)} %get-tuple-element.11), channel_id=1, source_target_pairs={{1,0},{2,1},{3,2},{4,3},{5,4},{6,5},{7,6},{8,7},{9,8},{10,9},{11,1... | collective-permute-start | bytes 1179656 | tf_op jit(solution)/shard_map/ppermute | solution.py:507
  141.7 17.6 %collective-permute-start.1 = (bf16[12,8,2048]{2,1,0:T(8,128)(2,1)S(1)}, bf16[12,8,2048]{2,1,0:T(8,128)(2,1)S(1)}, u32[]{:S(2)}, u32[]{:S(2)}) collective-permute-start(bf16[12,8,2048]{2,1,0:T(8,128)(2,1)S(1)} %get-tuple-element.12), channel_id=1, source_target_pairs={{0,1},{1,2},{2,3},{3,4},{4,5},{5,6},{6,7},{7,8},{8,9},{9,10},{10,1... | collective-permute-start | bytes 1179656 | tf_op jit(solution)/shard_map/ppermute | solution.py:507
  145.2 14.1 %collective-permute-start.2 = (bf16[12,8,2048]{2,1,0:T(8,128)(2,1)S(1)}, bf16[12,8,2048]{2,1,0:T(8,128)(2,1)S(1)}, u32[]{:S(2)}, u32[]{:S(2)}) collective-permute-start(bf16[12,8,2048]{2,1,0:T(8,128)(2,1)S(1)} %get-tuple-element.13), channel_id=1, source_target_pairs={{16,0},{32,16},{48,32},{64,48},{80,64},{96,80},{112,96},{17,1},{33... | collective-permute-start | bytes 1179656 | tf_op jit(solution)/shard_map/ppermute | solution.py:507
  148.5 10.8 %collective-permute-start.3 = (bf16[12,8,2048]{2,1,0:T(8,128)(2,1)S(1)}, bf16[12,8,2048]{2,1,0:T(8,128)(2,1)S(1)}, u32[]{:S(2)}, u32[]{:S(2)}) collective-permute-start(bf16[12,8,2048]{2,1,0:T(8,128)(2,1)S(1)} %get-tuple-element.14), channel_id=1, source_target_pairs={{0,16},{16,32},{32,48},{48,64},{64,80},{80,96},{96,112},{1,17},{17... | collective-permute-start | bytes 1179656 | tf_op jit(solution)/shard_map/ppermute | solution.py:507
